TPU v7x, 128 devices: a whole 4x4x4 slice. The times are simulated.
128 devices in a mesh: group: 8 (over y, core), local: 16 (over z, x).
Axes of the slice: x: 4, y: 4, z: 4, core: 2. Of those that a mesh axis runs over, the one named last changes fastest.
Arguments:
- lookup_grads: bfloat16 [1048576, 256], P(('group', 'local')), may hold values from -0.29882812 to 0.29882812
- slot_index: int32 [2, 1048576], P(None, ('group', 'local')), may hold values from 0 to 2047, as said below
- unique_rows: int32 [2, 16384], P(None, ('group', 'local')), may hold values from -1 to 131071, as said below
- tables: float32 [2, 131072, 256], P(None, ('group', 'local')), may hold values from -6 to 6
- accums: float32 [2, 131072], P(None, ('group', 'local')), may hold values from 0.01 to 1
Outputs:
- new_tables: float32 [2, 131072, 256], P(None, ('group', 'local'))
- new_accums: float32 [2, 131072], P(None, ('group', 'local'))
Inputs may be any that keep to these rules, and one draw needn't show every extreme that they name: slot_index[t, i] names a slot of lookup i's group list whose entry in unique_rows[t] is not -1. `unique_rows`: table row p is owned by device p // 1024, which is device (group p // 16384, local p // 1024 % 16). Group g's list is entries g * 2048 to (g + 1) * 2048 - 1; its block l of 128 entries consists of 8 buckets of 16 entries, bucket h holding only rows owned by device (group h, local l), the used entries first and -1 after them. Rows within a group's list are distinct. In every draw and table some device (group h, local l) gets a full bucket from every group.
All inputs are finite; a program needn't handle non-finite values.
Results may differ from a plain program's by a relative error of at most 0.0003.
Values sent between devices are 32-bit elements; how exact they have to be, the bound alone decides.
No kernel may reach another device: no remote copies, remote signals or barrier semaphores. Data moves between devices by JAX's collectives and lax.ppermute only.
A program may use at most 64 MiB of HBM per device.

v0:
```python
import jax
import jax.numpy as jnp
from jax import lax
from jax.sharding import PartitionSpec as P

learning_rate = 0.1
epsilon = 1e-08


def slot_sums(lookup_grads, slot_index, row_count):
    block_len = min(2048, lookup_grads.shape[0])
    block_count = lookup_grads.shape[0] // block_len
    width = lookup_grads.shape[1]
    grad_blocks = lookup_grads.reshape(block_count, block_len, width)
    index_blocks = jnp.transpose(slot_index.reshape(2, block_count, block_len), (1, 0, 2))
    targets = lax.iota(jnp.int32, row_count)

    def accumulate(running, inputs):
        gradients, indices = inputs
        pieces = []
        for table_index in range(2):
            onehot = (indices[table_index][:, None] == targets[None, :]).astype(jnp.bfloat16)
            pieces.append(
                lax.dot_general(
                    onehot, gradients, (((0,), (0,)), ((), ())), preferred_element_type=jnp.float32
                )
            )
        return (running + jnp.concatenate(pieces, axis=1), None)

    start_sums = jnp.zeros((row_count, 2 * width), jnp.float32)
    summed, _ = lax.scan(accumulate, start_sums, (grad_blocks, index_blocks))
    return summed


def apply_update(summed, row_pairs, tables, accums):
    rows_dev = tables.shape[1]
    width = tables.shape[2]
    new_tables = []
    new_accums = []
    for table_index in range(2):
        row_numbers = row_pairs[:, table_index]
        local_rows = jnp.where(row_numbers < 0, rows_dev, row_numbers % rows_dev)
        values = summed[:, table_index * width : (table_index + 1) * width]
        row_grads = (
            jnp.zeros((rows_dev, width), jnp.float32).at[local_rows].add(values, mode="drop")
        )
        accum_new = accums[table_index] + jnp.mean(row_grads * row_grads, axis=1)
        table_new = tables[table_index] - learning_rate * row_grads / (
            jnp.sqrt(accum_new)[:, None] + epsilon
        )
        new_tables.append(table_new)
        new_accums.append(accum_new)
    return (jnp.stack(new_tables), jnp.stack(new_accums))


def local(lookup_grads, slot_index, unique_rows, tables, accums):
    n_group = lax.axis_size("group")
    n_local = lax.axis_size("local")
    slots = unique_rows.shape[1]
    capacity = slots // n_group
    width = lookup_grads.shape[1]
    row_pairs = jnp.transpose(unique_rows)
    own_sums = slot_sums(lookup_grads, slot_index, slots * n_local)
    ordered = own_sums.reshape(n_local, n_group, capacity, 2 * width)
    ordered = jnp.transpose(ordered, (1, 0, 2, 3)).reshape(n_local * slots, 2 * width)
    received = lax.all_to_all(ordered, ("group", "local"), split_axis=0, concat_axis=0, tiled=True)
    arrived = jnp.sum(received.reshape(n_group, n_local, capacity, 2 * width), axis=1).reshape(
        slots, 2 * width
    )
    arrived_rows = lax.all_to_all(row_pairs, "group", split_axis=0, concat_axis=0, tiled=True)
    return apply_update(arrived, arrived_rows, tables, accums)


def solution(mesh):
    return jax.shard_map(
        local,
        mesh=mesh,
        in_specs=(
            P(("group", "local"), None),
            P(None, ("group", "local")),
            P(None, ("group", "local")),
            P(None, ("group", "local"), None),
            P(None, ("group", "local")),
        ),
        out_specs=(P(None, ("group", "local"), None), P(None, ("group", "local"))),
        check_vma=False,
    )
```

profile of v0, /device:TPU:1, one launch (start us, length us, event | category | flops | bytes accessed | tf_op | source)
XLA Modules:
  0.0 159.0 jit_solution(276250633649171804)
XLA Ops:
  0.6 0.8 all_to_all.14
  1.4 0.6 copy.11
  2.0 6.0 %all-to-all-start = ((s32[8,16,2]{1,2,0:T(2,128)}), s32[8,16,2]{1,2,0:T(2,128)S(1)}, u32[]{:S(2)}, u32[]{:S(2)}) async-start(s32[8,16,2]{1,2,0:T(2,128)} %copy.11), calls=%async_computation | async-start | bytes 16384 | tf_op jit(solution)/shard_map/all_to_all | solution.py:70
  8.0 68.6 %while.12 = (s32[]{:T(128)}, f32[2048,512]{0,1:T(8,128)}, s32[4,2,2048]{2,1,0:T(2,128)}, bf16[4,2048,256]{2,1,0:T(8,128)(2,1)}, s32[]{:T(128)}, /*index=5*/s32[]{:T(128)}, s32[]{}) while((s32[]{:T(128)}, f32[2048,512]{0,1:T(8,128)}, s32[4,2,2048]{2,1,0:T(2,128)}, bf16[4,2048,256]{2,1,0:T(8,128)(2,1)}, s32[]{:T(128)}, ...), condition=%wide.region_1.2_spmd.clone.clone, body=%wide.region_0.1_spmd.clone.clone.sunk | while | flops 4306501632 | bytes 18924652 | solution.py:31
  8.0 0.8 constant_dynamic-slice_fusion.3
  8.8 4.8 %fusion.30 = f32[2048,256]{0,1:T(8,128)S(1)} fusion(s32[2048]{0:T(1024)S(1)} %bitcast.56, bf16[4,2048,256]{2,1,0:T(8,128)(2,1)} %get-tuple-element.130, s32[]{:T(128)} %get-tuple-element.120), kind=kOutput, calls=%fused_computation.6.clone.1 | convolution fusion | flops 2151677952 | bytes 3154432 | tf_op jit(solution)/shard_map/while/body/eval_jaxpr/dot_general | solution.py:24
  13.6 6.1 %fusion.31 = f32[2048,256]{0,1:T(8,128)} fusion(s32[2048]{0:T(1024)S(1)} %bitcast.55, bf16[4,2048,256]{2,1,0:T(8,128)(2,1)} %get-tuple-element.130, s32[]{:T(128)} %get-tuple-element.120), kind=kOutput, calls=%fused_computation.5.clone.1 | convolution fusion | flops 2151677952 | bytes 3154432 | tf_op jit(solution)/shard_map/while/body/eval_jaxpr/dot_general | solution.py:24
  19.7 4.5 %maximum_add_fusion.2 = f32[2048,512]{0,1:T(8,128)} fusion(f32[2048,256]{0,1:T(8,128)S(1)} %fusion.30, f32[2048,256]{0,1:T(8,128)} %fusion.31, f32[2048,512]{0,1:T(8,128)} %get-tuple-element.121, pred[]{:T(512)S(6)} %compare.5), kind=kLoop, calls=%fused_computation.9.clone.1 | loop fusion | flops 3145728 | bytes 12582913 | tf_op jit(solution)/shard_map/while/body/eval_jaxpr/add | solution.py:28
  24.2 0.8 constant_dynamic-slice_fusion.3
  25.0 4.8 %fusion.30 = f32[2048,256]{0,1:T(8,128)S(1)} fusion(s32[2048]{0:T(1024)S(1)} %bitcast.56, bf16[4,2048,256]{2,1,0:T(8,128)(2,1)} %get-tuple-element.130, s32[]{:T(128)} %get-tuple-element.120), kind=kOutput, calls=%fused_computation.6.clone.1 | convolution fusion | flops 2151677952 | bytes 3154432 | tf_op jit(solution)/shard_map/while/body/eval_jaxpr/dot_general | solution.py:24
  29.8 6.1 %fusion.31 = f32[2048,256]{0,1:T(8,128)} fusion(s32[2048]{0:T(1024)S(1)} %bitcast.55, bf16[4,2048,256]{2,1,0:T(8,128)(2,1)} %get-tuple-element.130, s32[]{:T(128)} %get-tuple-element.120), kind=kOutput, calls=%fused_computation.5.clone.1 | convolution fusion | flops 2151677952 | bytes 3154432 | tf_op jit(solution)/shard_map/while/body/eval_jaxpr/dot_general | solution.py:24
  35.9 5.8 %maximum_add_fusion.2 = f32[2048,512]{0,1:T(8,128)} fusion(f32[2048,256]{0,1:T(8,128)S(1)} %fusion.30, f32[2048,256]{0,1:T(8,128)} %fusion.31, f32[2048,512]{0,1:T(8,128)} %get-tuple-element.121, pred[]{:T(512)S(6)} %compare.5), kind=kLoop, calls=%fused_computation.9.clone.1 | loop fusion | flops 3145728 | bytes 12582913 | tf_op jit(solution)/shard_map/while/body/eval_jaxpr/add | solution.py:28
  41.6 0.8 constant_dynamic-slice_fusion.3
  42.5 4.8 %fusion.30 = f32[2048,256]{0,1:T(8,128)S(1)} fusion(s32[2048]{0:T(1024)S(1)} %bitcast.56, bf16[4,2048,256]{2,1,0:T(8,128)(2,1)} %get-tuple-element.130, s32[]{:T(128)} %get-tuple-element.120), kind=kOutput, calls=%fused_computation.6.clone.1 | convolution fusion | flops 2151677952 | bytes 3154432 | tf_op jit(solution)/shard_map/while/body/eval_jaxpr/dot_general | solution.py:24
  47.2 6.1 %fusion.31 = f32[2048,256]{0,1:T(8,128)} fusion(s32[2048]{0:T(1024)S(1)} %bitcast.55, bf16[4,2048,256]{2,1,0:T(8,128)(2,1)} %get-tuple-element.130, s32[]{:T(128)} %get-tuple-element.120), kind=kOutput, calls=%fused_computation.5.clone.1 | convolution fusion | flops 2151677952 | bytes 3154432 | tf_op jit(solution)/shard_map/while/body/eval_jaxpr/dot_general | solution.py:24
  53.3 5.8 %maximum_add_fusion.2 = f32[2048,512]{0,1:T(8,128)} fusion(f32[2048,256]{0,1:T(8,128)S(1)} %fusion.30, f32[2048,256]{0,1:T(8,128)} %fusion.31, f32[2048,512]{0,1:T(8,128)} %get-tuple-element.121, pred[]{:T(512)S(6)} %compare.5), kind=kLoop, calls=%fused_computation.9.clone.1 | loop fusion | flops 3145728 | bytes 12582913 | tf_op jit(solution)/shard_map/while/body/eval_jaxpr/add | solution.py:28
  59.1 0.8 constant_dynamic-slice_fusion.3
  59.9 4.8 %fusion.30 = f32[2048,256]{0,1:T(8,128)S(1)} fusion(s32[2048]{0:T(1024)S(1)} %bitcast.56, bf16[4,2048,256]{2,1,0:T(8,128)(2,1)} %get-tuple-element.130, s32[]{:T(128)} %get-tuple-element.120), kind=kOutput, calls=%fused_computation.6.clone.1 | convolution fusion | flops 2151677952 | bytes 3154432 | tf_op jit(solution)/shard_map/while/body/eval_jaxpr/dot_general | solution.py:24
  64.7 6.1 %fusion.31 = f32[2048,256]{0,1:T(8,128)} fusion(s32[2048]{0:T(1024)S(1)} %bitcast.55, bf16[4,2048,256]{2,1,0:T(8,128)(2,1)} %get-tuple-element.130, s32[]{:T(128)} %get-tuple-element.120), kind=kOutput, calls=%fused_computation.5.clone.1 | convolution fusion | flops 2151677952 | bytes 3154432 | tf_op jit(solution)/shard_map/while/body/eval_jaxpr/dot_general | solution.py:24
  70.8 5.8 %maximum_add_fusion.2 = f32[2048,512]{0,1:T(8,128)} fusion(f32[2048,256]{0,1:T(8,128)S(1)} %fusion.30, f32[2048,256]{0,1:T(8,128)} %fusion.31, f32[2048,512]{0,1:T(8,128)} %get-tuple-element.121, pred[]{:T(512)S(6)} %compare.5), kind=kLoop, calls=%fused_computation.9.clone.1 | loop fusion | flops 3145728 | bytes 12582913 | tf_op jit(solution)/shard_map/while/body/eval_jaxpr/add | solution.py:28
  76.6 5.3 %copy.13 = f32[2048,512]{1,0:T(8,128)} copy(f32[2048,512]{0,1:T(8,128)} %get-tuple-element.32) | data formatting | bytes 8388608 | tf_op jit(solution)/shard_map/while | solution.py:31
  81.9 5.0 %copy.14 = f32[8,16,16,512]{3,2,1,0:T(8,128)} copy(f32[8,16,16,512]{3,2,0,1:T(8,128)} %bitcast.52) | data formatting | bytes 8388608 | tf_op jit(solution)/shard_map/transpose | solution.py:65
  86.9 10.8 %all-to-all-start.1 = ((f32[128,16,512]{2,1,0:T(8,128)}), f32[128,16,512]{2,1,0:T(8,128)}, u32[]{:S(2)}, u32[]{:S(2)}) async-start(f32[128,16,512]{2,1,0:T(8,128)} %bitcast.51), calls=%async_computation.1 | async-start | bytes 8388608 | tf_op jit(solution)/shard_map/all_to_all | solution.py:66
  97.8 51.1 %all-to-all-done.1 = f32[128,16,512]{2,1,0:T(8,128)} async-done(((f32[128,16,512]{2,1,0:T(8,128)}), f32[128,16,512]{2,1,0:T(8,128)}, u32[]{:S(2)}, u32[]{:S(2)}) %all-to-all-start.1) | async-done | bytes 4194336 | tf_op jit(solution)/shard_map/all_to_all | solution.py:66
  148.8 2.6 %bitcast_reduce_fusion = f32[8,16,512]{2,1,0:T(8,128)S(1)} fusion(f32[128,16,512]{2,1,0:T(8,128)} %all-to-all-done.1), kind=kLoop, calls=%fused_computation.18 | loop fusion | flops 983040 | bytes 4456448 | tf_op jit(solution)/shard_map/reduce_sum | solution.py:67
  151.5 1.5 scatter_custom_fusion
  153.0 0.2 multiply_reduce_fusion.1
  153.2 1.5 scatter_custom_fusion.1
  154.8 0.2 multiply_reduce_fusion
  155.0 1.9 %fusion.13 = (f32[1,1024,256]{2,1,0:T(8,128)S(1)}, f32[1,1024,256]{2,1,0:T(8,128)S(1)}) fusion(f32[1024,256]{1,0:T(8,128)S(1)} %scatter_custom_fusion, f32[2,1024,256]{2,1,0:T(8,128)} %param.10, f32[1024]{0:T(1024)S(1)} %get-tuple-element.83, f32[1024]{0:T(1024)S(1)} %get-tuple-element.82, f32[1024,256]{1,0:T(8,128)S(1)} %scatter_custom_fusion.1), kind=kLoop, calls=%fused_computation.23 | loop fusion | flops 1572864 | bytes 6299648 | tf_op jit(solution)/shard_map/stack | solution.py:53
  156.9 1.5 pad_maximum_fusion
  158.4 0.6 pad_maximum_fusion.1
  (11 shorter events, 0.1 us)
Async XLA Ops:
  2.0 84.9 %all-to-all-start = ((s32[8,16,2]{1,2,0:T(2,128)}), s32[8,16,2]{1,2,0:T(2,128)S(1)}, u32[]{:S(2)}, u32[]{:S(2)}) async-start(s32[8,16,2]{1,2,0:T(2,128)} %copy.11), calls=%async_computation | async-start | bytes 16384 | tf_op jit(solution)/shard_map/all_to_all | solution.py:70
  86.9 62.0 %all-to-all-start.1 = ((f32[128,16,512]{2,1,0:T(8,128)}), f32[128,16,512]{2,1,0:T(8,128)}, u32[]{:S(2)}, u32[]{:S(2)}) async-start(f32[128,16,512]{2,1,0:T(8,128)} %bitcast.51), calls=%async_computation.1 | async-start | bytes 8388608 | tf_op jit(solution)/shard_map/all_to_all | solution.py:66
  97.8 57.2 %copy-start = (f32[2,1024]{1,0:T(2,128)S(1)}, f32[2,1024]{1,0:T(2,128)}, u32[]{:S(2)}) copy-start(f32[2,1024]{1,0:T(2,128)} %param.11) | copy-start | bytes 24580
where the time goes:
time: 160 us; the launch traced here: 159 us
  waiting for transfers between devices  51.1 us (32%)
  matrix products  43.5 us (27%)
  other arithmetic  31.9 us (20%)
  starting transfers between devices  16.8 us (10%)
  local copies, waits for them, and re-layouts  15 us (9%)
    all_to_all x1, waiting for transfers between devices, local(): lax.all_to_all(ordered, ('group', 'local'), split_axis=0, concat_axis=0,...  51.1 us
    dot_general x8, matrix products, accumulate(): lax.dot_general(onehot, gradients, (((0,), (0,)), ((), ())), preferred_el...  43.5 us
    add x4, other arithmetic, accumulate(): return (running + jnp.concatenate(pieces, axis=1), None)  21.8 us
    all_to_all x1, starting transfers between devices, local(): lax.all_to_all(ordered, ('group', 'local'), split_axis=0, concat_axis=0,...  10.8 us
    all_to_all x1, starting transfers between devices, local(): lax.all_to_all(row_pairs, 'group', split_axis=0, concat_axis=0, tiled=True)  5.97 us
    while x1, local copies, waits for them, and re-layouts, slot_sums(): summed, _ = lax.scan(accumulate, start_sums, (grad_blocks, index_blocks))  5.34 us
    transpose x1, local copies, waits for them, and re-layouts, local(): jnp.transpose(ordered, (1, 0, 2, 3)).reshape(n_local * slots, 2 * width)  4.95 us
    another operation x3, other arithmetic, apply_update(): return (jnp.stack(new_tables), jnp.stack(new_accums))  3.95 us
  transfers between devices with their start and end apart: 2, of which 1 were waited for; matrix products, arithmetic and copies ran while one was open for 50% of the time, Pallas kernels for 0%

commit v1 on v0

v1 whole, which is shorter than its diff:
```python
import jax
import jax.numpy as jnp
from jax import lax
from jax.experimental import pallas as pl
from jax.experimental.pallas import tpu as pltpu
from jax.sharding import PartitionSpec as P

learning_rate = 0.1
epsilon = 1e-08

AXES = ("group", "local")
SIDE = 4
CORES = 2
VMEM_BYTES = 40 << 20


def ring_pairs(n_group, n_local, stage, step):
    pairs = []
    for group in range(n_group):
        for place in range(n_local):
            z, x = divmod(place, SIDE)
            if (group % CORES + stage) % 2 == 0:
                x = (x + step) % SIDE
            else:
                z = (z + step) % SIDE
            pairs.append((group * n_local + place, group * n_local + z * SIDE + x))
    return pairs


def slot_sums(place, slot_index, lookup_grads, offsets):
    count, width = lookup_grads.shape
    slots = 128
    rows = SIDE * slots
    block = 1024

    def body(place_ref, index_ref, grads_ref, *out_refs):
        for start in range(0, count, block):
            grads = grads_ref[pl.ds(start, block), :]
            for table in range(2):
                index = index_ref[table : table + 1, pl.ds(start, block)]
                first = lax.shift_right_logical(index, place_ref[2]) & (SIDE - 1)
                second = lax.shift_right_logical(index, place_ref[3]) & (SIDE - 1)
                row = ((second - place_ref[1]) & (SIDE - 1)) * slots + (index & (slots - 1))
                mine = ((first - place_ref[0]) & (SIDE - 1)) == offsets[table]
                row = jnp.where(mine, row, -1)
                hit = lax.broadcasted_iota(jnp.int32, (rows, block), 0) == row
                onehot = jnp.where(hit, jnp.float32(1), jnp.float32(0)).astype(jnp.bfloat16)
                piece = jnp.dot(onehot, grads, preferred_element_type=jnp.float32)
                if start == 0:
                    out_refs[table][...] = piece
                else:
                    out_refs[table][...] += piece

    return pl.pallas_call(
        body,
        out_shape=[jax.ShapeDtypeStruct((rows, width), jnp.float32)] * 2,
        in_specs=[pl.BlockSpec(memory_space=pltpu.SMEM)]
        + [pl.BlockSpec(memory_space=pltpu.VMEM)] * 2,
        out_specs=[pl.BlockSpec(memory_space=pltpu.VMEM)] * 2,
        compiler_params=pltpu.CompilerParams(vmem_limit_bytes=VMEM_BYTES),
        cost_estimate=pl.CostEstimate(
            flops=4 * rows * count * width,
            bytes_accessed=count * width * 2 + rows * width * 8,
            transcendentals=0,
        ),
        name="slot_sums",
    )(place, slot_index, lookup_grads)


def apply_update(arrived, tables, accums):
    slots = arrived.shape[0]
    rows_dev, width = tables.shape[1:]
    parts = 2
    rows = rows_dev // parts
    lanes = 128

    def body(arrived_ref, tables_ref, accums_ref, new_tables_ref, new_accums_ref):
        half = pl.program_id(1)
        eye = lax.broadcasted_iota(jnp.int32, (lanes, lanes), 0) == lax.broadcasted_iota(
            jnp.int32, (lanes, lanes), 1
        )

        def update(table):
            values = arrived_ref[:, table * width : (table + 1) * width]
            high = values.astype(jnp.bfloat16)
            rest = values - high.astype(jnp.float32)
            middle = rest.astype(jnp.bfloat16)
            low = (rest - middle.astype(jnp.float32)).astype(jnp.bfloat16)
            pieces = jnp.concatenate([high, middle, low], axis=0)
            numbers = arrived_ref[:, 2 * width + table : 2 * width + table + 1]
            numbers = jnp.sum(
                jnp.where(eye, jnp.broadcast_to(numbers, (slots, lanes)), 0.0),
                axis=0,
                keepdims=True,
            ).astype(jnp.int32)
            hit = lax.broadcasted_iota(jnp.int32, (rows, slots), 0) + half * rows == numbers
            onehot = jnp.where(hit, jnp.float32(1), jnp.float32(0)).astype(jnp.bfloat16)
            onehot = jnp.concatenate([onehot] * 3, axis=1)
            row_grads = jnp.dot(onehot, pieces, preferred_element_type=jnp.float32)
            squares = jnp.sum(row_grads * row_grads, axis=1, keepdims=True)
            for start in range(0, rows, lanes):
                square = squares[start : start + lanes]
                square = jnp.sum(
                    jnp.where(eye, jnp.broadcast_to(square, (lanes, lanes)), 0.0),
                    axis=0,
                    keepdims=True,
                )
                accum = accums_ref[table : table + 1, pl.ds(half * rows + start, lanes)]
                accum = accum + square * (1.0 / width)
                new_accums_ref[table : table + 1, pl.ds(half * rows + start, lanes)] = accum
                scale = learning_rate / (jnp.sqrt(accum) + epsilon)
                scale = jnp.sum(
                    jnp.where(eye, jnp.broadcast_to(scale, (lanes, lanes)), 0.0),
                    axis=1,
                    keepdims=True,
                )
                new_tables_ref[0, start : start + lanes, :] = (
                    tables_ref[0, start : start + lanes, :]
                    - row_grads[start : start + lanes] * scale
                )

        for table in range(2):

            @pl.when(pl.program_id(0) == table)
            def _(table=table):
                update(table)

    return pl.pallas_call(
        body,
        grid=(2, parts),
        out_shape=[
            jax.ShapeDtypeStruct(tables.shape, jnp.float32),
            jax.ShapeDtypeStruct(accums.shape, jnp.float32),
        ],
        in_specs=[
            pl.BlockSpec(arrived.shape, lambda t, i: (0, 0)),
            pl.BlockSpec((1, rows, width), lambda t, i: (t, i, 0)),
            pl.BlockSpec(accums.shape, lambda t, i: (0, 0)),
        ],
        out_specs=[
            pl.BlockSpec((1, rows, width), lambda t, i: (t, i, 0)),
            pl.BlockSpec(accums.shape, lambda t, i: (0, 0)),
        ],
        compiler_params=pltpu.CompilerParams(vmem_limit_bytes=VMEM_BYTES),
        name="apply_update",
    )(arrived, tables, accums)


def local(lookup_grads, slot_index, unique_rows, tables, accums):
    n_group = lax.axis_size("group")
    n_local = lax.axis_size("local")
    rows_dev, width = tables.shape[1:]
    slots = unique_rows.shape[1]
    even = lax.axis_index("group") % CORES == 0
    z = lax.axis_index("local") // SIDE
    x = lax.axis_index("local") % SIDE
    place = jnp.stack(
        [
            jnp.where(even, x, z),
            jnp.where(even, z, x),
            jnp.where(even, 7, 9),
            jnp.where(even, 9, 7),
        ]
    ).astype(jnp.int32)

    def send(value, stage, step):
        return lax.ppermute(value, AXES, ring_pairs(n_group, n_local, stage, step))

    far0, far1 = slot_sums(place, slot_index, lookup_grads, (2, 2))
    far0 = send(far0, 0, 1)
    far1 = send(far1, 0, -1)
    back0, next1 = slot_sums(place, slot_index, lookup_grads, (3, 1))
    next1 = send(next1, 0, 1)
    back0 = send(back0, 0, -1)
    next0, back1 = slot_sums(place, slot_index, lookup_grads, (1, 3))
    next0 = send(next0 + far0, 0, 1)
    back1 = send(back1 + far1, 0, -1)
    own0, own1 = slot_sums(place, slot_index, lookup_grads, (0, 0))
    own0 = own0 + back0 + next0
    own1 = own1 + next1 + back1

    def part(value, offset):
        return value[offset * slots : (offset + 1) * slots]

    far0 = send(part(own0, 2), 1, 1)
    far1 = send(part(own1, 2), 1, -1)
    ahead = send(jnp.concatenate([part(own0, 1) + far0, part(own1, 1)]), 1, 1)
    behind = send(jnp.concatenate([part(own0, 3), part(own1, 3) + far1]), 1, -1)
    sum0 = part(own0, 0) + part(ahead, 0) + part(behind, 0)
    sum1 = part(own1, 0) + part(ahead, 1) + part(behind, 1)

    local_rows = jnp.where(unique_rows < 0, -1, unique_rows % rows_dev).astype(jnp.float32)
    local_rows = jnp.pad(jnp.transpose(local_rows), ((0, 0), (0, 126)))
    payload = jnp.concatenate([sum0, sum1, local_rows], axis=1)
    arrived = lax.all_to_all(payload, "group", split_axis=0, concat_axis=0, tiled=True)
    new_tables, new_accums = apply_update(arrived, tables, accums)
    return (new_tables, new_accums)


def solution(mesh):
    return jax.shard_map(
        local,
        mesh=mesh,
        in_specs=(
            P(("group", "local"), None),
            P(None, ("group", "local")),
            P(None, ("group", "local")),
            P(None, ("group", "local"), None),
            P(None, ("group", "local")),
        ),
        out_specs=(P(None, ("group", "local"), None), P(None, ("group", "local"))),
        check_vma=False,
    )
```

time: 160 us -> 76.9 us (0.48)
  waiting for transfers between devices: 51.1 us -> 6.74 us
  matrix products: 43.5 us -> 0 us
  other arithmetic: 31.9 us -> 5.73 us
  Pallas kernels: 0 us -> 23.4 us
  blocking collectives: 0 us -> 15.8 us
  local copies, waits for them, and re-layouts: 15 us -> 8.47 us
    all_to_all x2 -> x0, waiting for transfers between devices: 51.1 us -> none  [the longest x1 51.1 us: local(): lax.all_to_all(ordered, ('group', 'local'), split_axis=0, concat_axis=0,...]
    dot_general x8 -> x0, matrix products: 43.5 us -> none  [accumulate(): lax.dot_general(onehot, gradients, (((0,), (0,)), ((), ())), preferred_el...]
    pallas_call x0 -> x5, Pallas kernels: none -> 23.4 us  [the longest x4 20.1 us: slot_sums(): pl.pallas_call(body, out_shape=[jax.ShapeDtypeStruct((rows, width), jnp.f...]
    add x6 -> x7, other arithmetic: 21.9 us -> 4.85 us  [the longest x1 1.3 us: local(): own0 = own0 + back0 + next0]
    all_to_all x2 -> x0, starting transfers between devices: 16.8 us -> none  [the longest x1 10.8 us: local(): lax.all_to_all(ordered, ('group', 'local'), split_axis=0, concat_axis=0,...]
    all_to_all x0 -> x1, blocking collectives: none -> 15.8 us  [local(): lax.all_to_all(payload, 'group', split_axis=0, concat_axis=0, tiled=True)]
    ppermute x0 -> x10, starting transfers between devices: none -> 15.5 us  [send(): return lax.ppermute(value, AXES, ring_pairs(n_group, n_local, stage, step))]
    unnamed x2 -> x19, local copies, waits for them, and re-layouts: 0.01 us -> 7.54 us
  transfers between devices with their start and end apart: 2 -> 10, of which waited for: 1 -> 5; matrix products, arithmetic and copies ran while one was open for 50% -> 7% of each run, Pallas kernels for 0% -> 20%
where the time goes in v1:
time: 76.9 us; the launch traced here: 76.5 us
  Pallas kernels  23.4 us (30%)
  blocking collectives  15.8 us (21%)
  starting transfers between devices  15.5 us (20%)
  local copies, waits for them, and re-layouts  8.47 us (11%)
  waiting for transfers between devices  6.74 us (9%)
  other arithmetic  5.73 us (7%)
  between operations  0.84 us (1%)
    pallas_call x4, Pallas kernels, slot_sums(): pl.pallas_call(body, out_shape=[jax.ShapeDtypeStruct((rows, width), jnp.f...  20.1 us
    all_to_all x1, blocking collectives, local(): lax.all_to_all(payload, 'group', split_axis=0, concat_axis=0, tiled=True)  15.8 us
    ppermute x10, starting transfers between devices, send(): return lax.ppermute(value, AXES, ring_pairs(n_group, n_local, stage, step))  15.5 us
    unnamed x19, local copies, waits for them, and re-layouts  7.54 us
    ppermute x10, waiting for transfers between devices, send(): return lax.ppermute(value, AXES, ring_pairs(n_group, n_local, stage, step))  6.74 us
    pallas_call x1, Pallas kernels, apply_update(): pl.pallas_call(body, grid=(2, parts), out_shape=[jax.ShapeDtypeStruct(tab...  3.37 us
  transfers between devices with their start and end apart: 10, of which 5 were waited for; matrix products, arithmetic and copies ran while one was open for 7% of the time, Pallas kernels for 20%

profile of v1, /device:TPU:1, one launch (start us, length us, event | category | flops | bytes accessed | tf_op | source)
XLA Modules:
  0.0 76.5 jit_solution(2811667105631158579)
XLA Ops:
  0.7 0.1 pad_add_fusion.place_ref
  0.7 2.2 %copy-done.2 = bf16[8192,256]{1,0:T(8,128)(2,1)S(1)} copy-done((bf16[8192,256]{1,0:T(8,128)(2,1)S(1)}, bf16[8192,256]{1,0:T(8,128)(2,1)}, u32[]{:S(2)}) %copy-start.2) | copy-done | bytes 4194328
  2.9 0.8 %copy-done.5 = s32[2,8192]{1,0:T(2,128)S(1)} copy-done((s32[2,8192]{1,0:T(2,128)S(1)}, s32[2,8192]{1,0:T(2,128)}, u32[]{:S(2)}) %copy-start.5) | copy-done | bytes 65560
  3.8 5.0 %slot_sums.7 = (f32[512,256]{1,0:T(8,128)S(1)}, f32[512,256]{1,0:T(8,128)S(1)}) custom-call(s32[4]{0:T(128)S(1)} %pad_add_fusion.place_ref, s32[2,8192]{1,0:T(2,128)S(1)} %copy-done.5, bf16[8192,256]{1,0:T(8,128)(2,1)S(1)} %copy-done.2), custom_call_target="tpu_custom_call" | custom-call | flops 4294967296 | bytes 5242880 | tf_op jit(solution)/shard_map/slot_sums/pallas_call | solution.py:54
  8.8 2.5 %collective-permute-start.1 = (f32[512,256]{1,0:T(8,128)S(1)}, f32[512,256]{1,0:T(8,128)}, u32[]{:S(2)}, u32[]{:S(2)}) collective-permute-start(f32[512,256]{1,0:T(8,128)S(1)} %get-tuple-element.13), channel_id=1, source_target_pairs={{0,1},{1,2},{2,3},{3,0},{4,5},{5,6},{6,7},{7,4},{8,9},{9,10},{10,1... | collective-permute-start | bytes 1572872 | tf_op jit(solution)/shard_map/ppermute | solution.py:167
  11.4 5.0 %slot_sums.5 = (f32[512,256]{1,0:T(8,128)S(1)}, f32[512,256]{1,0:T(8,128)S(1)}) custom-call(s32[4]{0:T(128)S(1)} %pad_add_fusion.place_ref, s32[2,8192]{1,0:T(2,128)S(1)} %copy-done.5, bf16[8192,256]{1,0:T(8,128)(2,1)S(1)} %copy-done.2), custom_call_target="tpu_custom_call" | custom-call | flops 4294967296 | bytes 5242880 | tf_op jit(solution)/shard_map/slot_sums/pallas_call | solution.py:54
  16.4 2.2 %collective-permute-start = (f32[512,256]{1,0:T(8,128)S(1)}, f32[512,256]{1,0:T(8,128)}, u32[]{:S(2)}, u32[]{:S(2)}) collective-permute-start(f32[512,256]{1,0:T(8,128)S(1)} %get-tuple-element.11), channel_id=1, source_target_pairs={{0,3},{1,0},{2,1},{3,2},{4,7},{5,4},{6,5},{7,6},{8,11},{9,8},{10,9... | collective-permute-start | bytes 1572872 | tf_op jit(solution)/shard_map/ppermute | solution.py:167
  18.6 1.4 %collective-permute-start.5 = (f32[512,256]{1,0:T(8,128)S(1)}, f32[512,256]{1,0:T(8,128)S(1)}, u32[]{:S(2)}, u32[]{:S(2)}) collective-permute-start(f32[512,256]{1,0:T(8,128)S(1)} %get-tuple-element.17), channel_id=1, source_target_pairs={{0,3},{1,0},{2,1},{3,2},{4,7},{5,4},{6,5},{7,6},{8,11},{9,8},{10,9... | collective-permute-start | bytes 1572872 | tf_op jit(solution)/shard_map/ppermute | solution.py:167
  20.0 0.1 copy.16
  20.2 2.2 %copy-done.3 = bf16[8192,256]{1,0:T(8,128)(2,1)S(1)} copy-done((bf16[8192,256]{1,0:T(8,128)(2,1)S(1)}, bf16[8192,256]{1,0:T(8,128)(2,1)}, u32[]{:S(2)}) %copy-start.3) | copy-done | bytes 4194328
  22.4 5.0 %slot_sums.6 = (f32[512,256]{1,0:T(8,128)S(1)}, f32[512,256]{1,0:T(8,128)S(1)}) custom-call(s32[4]{0:T(128)S(1)} %pad_add_fusion.place_ref, s32[2,8192]{1,0:T(2,128)S(1)} %copy-done.6, bf16[8192,256]{1,0:T(8,128)(2,1)S(1)} %copy-done.3), custom_call_target="tpu_custom_call" | custom-call | flops 4294967296 | bytes 5242880 | tf_op jit(solution)/shard_map/slot_sums/pallas_call | solution.py:54
  27.4 1.1 %add.55 = f32[512,256]{1,0:T(8,128)S(1)} add(f32[512,256]{1,0:T(8,128)S(1)} %get-tuple-element.12, f32[512,256]{1,0:T(8,128)} %collective-permute-done.1) | non-fusion elementwise | flops 131072 | bytes 1572864 | tf_op jit(solution)/shard_map/add | solution.py:176
  28.6 0.7 copy.19
  29.3 1.2 %collective-permute-done.5 = f32[512,256]{1,0:T(8,128)S(1)} collective-permute-done((f32[512,256]{1,0:T(8,128)S(1)}, f32[512,256]{1,0:T(8,128)S(1)}, u32[]{:S(2)}, u32[]{:S(2)}) %collective-permute-start.5) | collective-permute-done | bytes 524320 | tf_op jit(solution)/shard_map/ppermute | solution.py:167
  30.6 3.5 %collective-permute-start.6 = (f32[512,256]{1,0:T(8,128)S(1)}, f32[512,256]{1,0:T(8,128)S(1)}, u32[]{:S(2)}, u32[]{:S(2)}) collective-permute-start(f32[512,256]{1,0:T(8,128)S(1)} %add.59), channel_id=1, source_target_pairs={{0,3},{1,0},{2,1},{3,2},{4,7},{5,4},{6,5},{7,6},{8,11},{9,8},{10,9... | collective-permute-start | bytes 1572872 | tf_op jit(solution)/shard_map/ppermute | solution.py:167
  34.2 2.2 %copy-done.4 = bf16[8192,256]{1,0:T(8,128)(2,1)S(1)} copy-done((bf16[8192,256]{1,0:T(8,128)(2,1)S(1)}, bf16[8192,256]{1,0:T(8,128)(2,1)}, u32[]{:S(2)}) %copy-start.4) | copy-done | bytes 4194328
  36.4 5.0 %slot_sums.4 = (f32[512,256]{1,0:T(8,128)S(1)}, f32[512,256]{1,0:T(8,128)S(1)}) custom-call(s32[4]{0:T(128)S(1)} %pad_add_fusion.place_ref, s32[2,8192]{1,0:T(2,128)S(1)} %copy-done.6, bf16[8192,256]{1,0:T(8,128)(2,1)S(1)} %copy-done.4), custom_call_target="tpu_custom_call" | custom-call | flops 4294967296 | bytes 5242880 | tf_op jit(solution)/shard_map/slot_sums/pallas_call | solution.py:54
  41.4 1.3 %add_add_fusion.1 = f32[512,256]{1,0:T(8,128)S(1)} fusion(f32[512,256]{1,0:T(8,128)} %collective-permute-done.2, f32[512,256]{1,0:T(8,128)S(1)} %get-tuple-element.10, f32[512,256]{1,0:T(8,128)} %collective-permute-done), kind=kLoop, calls=%fused_computation.1 | loop fusion | flops 262144 | bytes 2097152 | tf_op jit(solution)/shard_map/add | solution.py:179
  42.7 0.9 %collective-permute-start.3 = (f32[128,256]{1,0:T(8,128)S(1)}, f32[128,256]{1,0:T(8,128)S(1)}, u32[]{:S(2)}, u32[]{:S(2)}) collective-permute-start(f32[128,256]{1,0:T(8,128)S(1)} %slice.50), channel_id=1, source_target_pairs={{0,4},{1,5},{2,6},{3,7},{4,8},{5,9},{6,10},{7,11},{8,12},{9,13},{1... | collective-permute-start | bytes 393224 | tf_op jit(solution)/shard_map/ppermute | solution.py:167
  43.6 1.2 %add_add_fusion = f32[512,256]{1,0:T(8,128)S(1)} fusion(f32[512,256]{1,0:T(8,128)S(1)} %collective-permute-done.6, f32[512,256]{1,0:T(8,128)S(1)} %get-tuple-element.14, f32[512,256]{1,0:T(8,128)} %collective-permute-done.4), kind=kLoop, calls=%fused_computation | loop fusion | flops 262144 | bytes 2097152 | tf_op jit(solution)/shard_map/add | solution.py:180
  44.8 1.9 %collective-permute-start.8 = (f32[128,256]{1,0:T(8,128)S(1)}, f32[128,256]{1,0:T(8,128)S(1)}, u32[]{:S(2)}, u32[]{:S(2)}) collective-permute-start(f32[128,256]{1,0:T(8,128)S(1)} %get-tuple-element.23), channel_id=1, source_target_pairs={{0,12},{1,13},{2,14},{3,15},{4,0},{5,1},{6,2},{7,3},{8,4},{9,5},{1... | collective-permute-start | bytes 393224 | tf_op jit(solution)/shard_map/ppermute | solution.py:167
  46.7 1.1 %collective-permute-done.3 = f32[128,256]{1,0:T(8,128)S(1)} collective-permute-done((f32[128,256]{1,0:T(8,128)S(1)}, f32[128,256]{1,0:T(8,128)S(1)}, u32[]{:S(2)}, u32[]{:S(2)}) %collective-permute-start.3) | collective-permute-done | bytes 131104 | tf_op jit(solution)/shard_map/ppermute | solution.py:167
  47.9 0.1 collective-permute-start.7
  48.0 1.0 %collective-permute-done.8 = f32[128,256]{1,0:T(8,128)S(1)} collective-permute-done((f32[128,256]{1,0:T(8,128)S(1)}, f32[128,256]{1,0:T(8,128)S(1)}, u32[]{:S(2)}, u32[]{:S(2)}) %collective-permute-start.8) | collective-permute-done | bytes 131104 | tf_op jit(solution)/shard_map/ppermute | solution.py:167
  49.0 0.7 pad_maximum_fusion.1
  49.7 2.8 %collective-permute-start.9 = (f32[256,256]{1,0:T(8,128)}, f32[256,256]{1,0:T(8,128)}, u32[]{:S(2)}, u32[]{:S(2)}) collective-permute-start(f32[256,256]{1,0:T(8,128)} %pad_maximum_fusion.1), channel_id=1, source_target_pairs={{0,12},{1,13},{2,14},{3,15},{4,0},{5,1},{6,2},{7,3},{8,4},{9,5},{1... | collective-permute-start | bytes 786440 | tf_op jit(solution)/shard_map/ppermute | solution.py:167
  52.6 0.1 copy.21
  52.7 1.8 %collective-permute-done.7 = f32[256,256]{1,0:T(8,128)} collective-permute-done((f32[256,256]{1,0:T(8,128)S(1)}, f32[256,256]{1,0:T(8,128)}, u32[]{:S(2)}, u32[]{:S(2)}) %collective-permute-start.7) | collective-permute-done | bytes 262176 | tf_op jit(solution)/shard_map/ppermute | solution.py:167
  54.5 1.6 %collective-permute-done.9 = f32[256,256]{1,0:T(8,128)} collective-permute-done((f32[256,256]{1,0:T(8,128)}, f32[256,256]{1,0:T(8,128)}, u32[]{:S(2)}, u32[]{:S(2)}) %collective-permute-start.9) | collective-permute-done | bytes 262176 | tf_op jit(solution)/shard_map/ppermute | solution.py:167
  56.1 1.2 %slice_add_fusion.2 = (f32[128,256]{1,0:T(8,128)S(1)}, f32[128,256]{1,0:T(8,128)S(1)}) fusion(f32[256,256]{1,0:T(8,128)} %collective-permute-done.9, f32[256,256]{1,0:T(8,128)} %collective-permute-done.7, f32[512,256]{1,0:T(8,128)S(1)} %add_add_fusion.1, f32[512,256]{1,0:T(8,128)S(1)} %add_add_fusion), kind=kLoop, calls=%fused_computation.8 | loop fusion | flops 131072 | bytes 1048576 | tf_op jit(solution)/shard_map/add | solution.py:189
  57.3 15.8 %all_to_all.11 = f32[8,16,640]{2,1,0:T(8,128)S(1)} all-to-all(f32[8,16,640]{2,1,0:T(8,128)S(1)} %bitcast.8), channel_id=1, replica_groups=mesh['group'=8,'local'=16] {'group'}, dimensions={0} | all-to-all | bytes 655360 | tf_op jit(solution)/shard_map/all_to_all | solution.py:195
  73.1 3.4 %apply_update.1 = (f32[2,1024,256]{2,1,0:T(8,128)}, f32[2,1024]{1,0:T(2,128)}) custom-call(f32[128,640]{1,0:T(8,128)S(1)} %bitcast.7, f32[2,1024,256]{2,1,0:T(8,128)S(1)} %copy-done, f32[2,1024]{1,0:T(2,128)S(1)} %copy-done.1), custom_call_target="tpu_custom_call" | custom-call | tf_op jit(solution)/shard_map/apply_update/pallas_call | solution.py:128
  (32 shorter events, 0.4 us)
Async XLA Ops:
  0.7 2.2 %copy-start.2 = (bf16[8192,256]{1,0:T(8,128)(2,1)S(1)}, bf16[8192,256]{1,0:T(8,128)(2,1)}, u32[]{:S(2)}) copy-start(bf16[8192,256]{1,0:T(8,128)(2,1)} %grads_ref.7) | copy-start | bytes 12582916
  2.9 0.8 %copy-start.5 = (s32[2,8192]{1,0:T(2,128)S(1)}, s32[2,8192]{1,0:T(2,128)}, u32[]{:S(2)}) copy-start(s32[2,8192]{1,0:T(2,128)} %index_ref.7) | copy-start | bytes 196612
  8.8 11.3 %copy-start.8 = (s32[2,128]{1,0:T(2,128)S(1)}, s32[2,128]{1,0:T(2,128)}, u32[]{:S(2)}) copy-start(s32[2,128]{1,0:T(2,128)} %param.7) | copy-start | bytes 3076
  8.8 11.4 %copy-start.6 = (s32[2,8192]{1,0:T(2,128)S(1)}, s32[2,8192]{1,0:T(2,128)}, u32[]{:S(2)}) copy-start(s32[2,8192]{1,0:T(2,128)} %index_ref.7) | copy-start | bytes 196612
  8.8 18.6 %collective-permute-start.1 = (f32[512,256]{1,0:T(8,128)S(1)}, f32[512,256]{1,0:T(8,128)}, u32[]{:S(2)}, u32[]{:S(2)}) collective-permute-start(f32[512,256]{1,0:T(8,128)S(1)} %get-tuple-element.13), channel_id=1, source_target_pairs={{0,1},{1,2},{2,3},{3,0},{4,5},{5,6},{6,7},{7,4},{8,9},{9,10},{10,1... | collective-permute-start | bytes 1572872 | tf_op jit(solution)/shard_map/ppermute | solution.py:167
  16.4 25.0 %collective-permute-start = (f32[512,256]{1,0:T(8,128)S(1)}, f32[512,256]{1,0:T(8,128)}, u32[]{:S(2)}, u32[]{:S(2)}) collective-permute-start(f32[512,256]{1,0:T(8,128)S(1)} %get-tuple-element.11), channel_id=1, source_target_pairs={{0,3},{1,0},{2,1},{3,2},{4,7},{5,4},{6,5},{7,6},{8,11},{9,8},{10,9... | collective-permute-start | bytes 1572872 | tf_op jit(solution)/shard_map/ppermute | solution.py:167
  18.6 12.0 %collective-permute-start.5 = (f32[512,256]{1,0:T(8,128)S(1)}, f32[512,256]{1,0:T(8,128)S(1)}, u32[]{:S(2)}, u32[]{:S(2)}) collective-permute-start(f32[512,256]{1,0:T(8,128)S(1)} %get-tuple-element.17), channel_id=1, source_target_pairs={{0,3},{1,0},{2,1},{3,2},{4,7},{5,4},{6,5},{7,6},{8,11},{9,8},{10,9... | collective-permute-start | bytes 1572872 | tf_op jit(solution)/shard_map/ppermute | solution.py:167
  20.0 23.6 %collective-permute-start.4 = (f32[512,256]{1,0:T(8,128)S(1)}, f32[512,256]{1,0:T(8,128)}, u32[]{:S(2)}, u32[]{:S(2)}) collective-permute-start(f32[512,256]{1,0:T(8,128)S(1)} %get-tuple-element.15), channel_id=1, source_target_pairs={{0,1},{1,2},{2,3},{3,0},{4,5},{5,6},{6,7},{7,4},{8,9},{9,10},{10,1... | collective-permute-start | bytes 1572872 | tf_op jit(solution)/shard_map/ppermute | solution.py:167
  20.2 2.2 %copy-start.3 = (bf16[8192,256]{1,0:T(8,128)(2,1)S(1)}, bf16[8192,256]{1,0:T(8,128)(2,1)}, u32[]{:S(2)}) copy-start(bf16[8192,256]{1,0:T(8,128)(2,1)} %grads_ref.7) | copy-start | bytes 12582916
  28.5 12.9 %collective-permute-start.2 = (f32[512,256]{1,0:T(8,128)S(1)}, f32[512,256]{1,0:T(8,128)}, u32[]{:S(2)}, u32[]{:S(2)}) collective-permute-start(f32[512,256]{1,0:T(8,128)S(1)} %add.55), channel_id=1, source_target_pairs={{0,1},{1,2},{2,3},{3,0},{4,5},{5,6},{6,7},{7,4},{8,9},{9,10},{10,1... | collective-permute-start | bytes 1572872 | tf_op jit(solution)/shard_map/ppermute | solution.py:167
  30.6 13.0 %collective-permute-start.6 = (f32[512,256]{1,0:T(8,128)S(1)}, f32[512,256]{1,0:T(8,128)S(1)}, u32[]{:S(2)}, u32[]{:S(2)}) collective-permute-start(f32[512,256]{1,0:T(8,128)S(1)} %add.59), channel_id=1, source_target_pairs={{0,3},{1,0},{2,1},{3,2},{4,7},{5,4},{6,5},{7,6},{8,11},{9,8},{10,9... | collective-permute-start | bytes 1572872 | tf_op jit(solution)/shard_map/ppermute | solution.py:167
  34.2 2.2 %copy-start.4 = (bf16[8192,256]{1,0:T(8,128)(2,1)S(1)}, bf16[8192,256]{1,0:T(8,128)(2,1)}, u32[]{:S(2)}) copy-start(bf16[8192,256]{1,0:T(8,128)(2,1)} %grads_ref.7) | copy-start | bytes 12582916
  42.7 5.1 %collective-permute-start.3 = (f32[128,256]{1,0:T(8,128)S(1)}, f32[128,256]{1,0:T(8,128)S(1)}, u32[]{:S(2)}, u32[]{:S(2)}) collective-permute-start(f32[128,256]{1,0:T(8,128)S(1)} %slice.50), channel_id=1, source_target_pairs={{0,4},{1,5},{2,6},{3,7},{4,8},{5,9},{6,10},{7,11},{8,12},{9,13},{1... | collective-permute-start | bytes 393224 | tf_op jit(solution)/shard_map/ppermute | solution.py:167
  43.6 8.9 %copy-start.7 = (pred[2,128]{0,1:T(8,128)(4,1)S(1)}, pred[2,128]{0,1:T(8,128)(4,1)}, u32[]{:S(2)}) copy-start(pred[2,128]{0,1:T(8,128)(4,1)} %copy.19) | copy-start | bytes 772
  44.8 4.2 %collective-permute-start.8 = (f32[128,256]{1,0:T(8,128)S(1)}, f32[128,256]{1,0:T(8,128)S(1)}, u32[]{:S(2)}, u32[]{:S(2)}) collective-permute-start(f32[128,256]{1,0:T(8,128)S(1)} %get-tuple-element.23), channel_id=1, source_target_pairs={{0,12},{1,13},{2,14},{3,15},{4,0},{5,1},{6,2},{7,3},{8,4},{9,5},{1... | collective-permute-start | bytes 393224 | tf_op jit(solution)/shard_map/ppermute | solution.py:167
  47.8 25.2 %copy-start = (f32[2,1024,256]{2,1,0:T(8,128)S(1)}, f32[2,1024,256]{2,1,0:T(8,128)}, u32[]{:S(2)}) copy-start(f32[2,1024,256]{2,1,0:T(8,128)} %tables_ref.1) | copy-start | bytes 6291460
  47.9 25.2 %copy-start.1 = (f32[2,1024]{1,0:T(2,128)S(1)}, f32[2,1024]{1,0:T(2,128)}, u32[]{:S(2)}) copy-start(f32[2,1024]{1,0:T(2,128)} %accums_ref.1) | copy-start | bytes 24580
  47.9 6.6 %collective-permute-start.7 = (f32[256,256]{1,0:T(8,128)S(1)}, f32[256,256]{1,0:T(8,128)}, u32[]{:S(2)}, u32[]{:S(2)}) collective-permute-start(f32[256,256]{1,0:T(8,128)S(1)} %pad_maximum_fusion), channel_id=1, source_target_pairs={{0,4},{1,5},{2,6},{3,7},{4,8},{5,9},{6,10},{7,11},{8,12},{9,13},{1... | collective-permute-start | bytes 786440 | tf_op jit(solution)/shard_map/ppermute | solution.py:167
  49.7 6.4 %collective-permute-start.9 = (f32[256,256]{1,0:T(8,128)}, f32[256,256]{1,0:T(8,128)}, u32[]{:S(2)}, u32[]{:S(2)}) collective-permute-start(f32[256,256]{1,0:T(8,128)} %pad_maximum_fusion.1), channel_id=1, source_target_pairs={{0,12},{1,13},{2,14},{3,15},{4,0},{5,1},{6,2},{7,3},{8,4},{9,5},{1... | collective-permute-start | bytes 786440 | tf_op jit(solution)/shard_map/ppermute | solution.py:167

commit v2 on v0

v2 whole, which is shorter than its diff:
```python
import jax
import jax.numpy as jnp
from jax import lax
from jax.experimental import pallas as pl
from jax.experimental.pallas import tpu as pltpu
from jax.sharding import PartitionSpec as P

learning_rate = 0.1
epsilon = 1e-08

AXES = ("group", "local")
SIDE = 4
CORES = 2
LANES = 128
VMEM_BYTES = 16 << 20
FIRST_BYTES = 48 << 20
IN_VMEM = pl.BlockSpec(memory_space=pltpu.VMEM)
IN_SMEM = pl.BlockSpec(memory_space=pltpu.SMEM)
IN_HBM = pl.BlockSpec(memory_space=pltpu.HBM)


def ring_pairs(n_group, n_local, stage, step):
    pairs = []
    for group in range(n_group):
        for place in range(n_local):
            z, x = divmod(place, SIDE)
            if (group % CORES + stage) % 2 == 0:
                x = (x + step) % SIDE
            else:
                z = (z + step) % SIDE
            pairs.append((group * n_local + place, group * n_local + z * SIDE + x))
    return pairs


def call(body, name, out_shape, in_specs, out_specs=None, scratch=(), cost=None, vmem=VMEM_BYTES):
    return pl.pallas_call(
        body,
        out_shape=out_shape,
        in_specs=in_specs,
        out_specs=[IN_VMEM] * len(out_shape) if out_specs is None else out_specs,
        scratch_shapes=scratch,
        compiler_params=pltpu.CompilerParams(vmem_limit_bytes=vmem),
        cost_estimate=cost,
        name=name,
    )


def f32(*shape):
    return jax.ShapeDtypeStruct(shape, jnp.float32)


def kernel_cost(rows, count, width):
    return pl.CostEstimate(
        flops=4 * rows * count * width // 10, bytes_accessed=count * width // 5, transcendentals=0
    )


def add_block(codes, grads, offsets, start, out_refs):
    rows = out_refs[0].shape[0]
    for table in range(2):
        target = lax.broadcasted_iota(jnp.int32, (rows, grads.shape[0]), 0) + offsets[table] * rows
        hit = target == codes[table : table + 1]
        onehot = jnp.where(hit, jnp.float32(1), jnp.float32(0)).astype(jnp.bfloat16)
        piece = jnp.dot(onehot, grads, preferred_element_type=jnp.float32)
        if start == 0:
            out_refs[table][...] = piece
        else:
            out_refs[table][...] += piece


def first_sums(place, slot_index, lookup_grads, offsets):
    count, width = lookup_grads.shape
    rows = SIDE * LANES
    block = 1024
    blocks = count // block

    def body(place_ref, index_hbm, grads_hbm, out0, out1, grads_ref, codes_ref, index_ref, sems):
        copies = [pltpu.make_async_copy(index_hbm, index_ref, sems.at[blocks])]
        for i in range(blocks):
            piece = pl.ds(i * block, block)
            copies.append(
                pltpu.make_async_copy(grads_hbm.at[piece], grads_ref.at[piece], sems.at[i])
            )
        for copy in copies:
            copy.start()
        copies[0].wait()
        index = index_ref[...]
        first = lax.shift_right_logical(index, place_ref[2]) & (SIDE - 1)
        second = lax.shift_right_logical(index, place_ref[3]) & (SIDE - 1)
        first = (first - place_ref[0]) & (SIDE - 1)
        second = (second - place_ref[1]) & (SIDE - 1)
        codes_ref[...] = first * rows + second * LANES + (index & (LANES - 1))
        for i in range(blocks):
            copies[1 + i].wait()
            piece = pl.ds(i * block, block)
            add_block(codes_ref[:, piece], grads_ref[piece, :], offsets, i, (out0, out1))

    return call(
        body,
        "first_sums",
        [
            f32(rows, width),
            f32(rows, width),
            jax.ShapeDtypeStruct(lookup_grads.shape, lookup_grads.dtype),
            jax.ShapeDtypeStruct(slot_index.shape, jnp.int32),
        ],
        [IN_SMEM, IN_HBM, IN_HBM],
        scratch=[
            pltpu.VMEM(slot_index.shape, jnp.int32),
            pltpu.SemaphoreType.DMA((blocks + 1,)),
        ],
        cost=kernel_cost(rows, count, width),
        vmem=FIRST_BYTES,
    )(place, slot_index, lookup_grads)


def slot_sums(codes, lookup_grads, offsets):
    count, width = lookup_grads.shape
    rows = SIDE * LANES
    block = 1024

    def body(codes_ref, grads_ref, out0, out1):
        for start in range(0, count, block):
            piece = pl.ds(start, block)
            add_block(codes_ref[:, piece], grads_ref[piece, :], offsets, start, (out0, out1))

    return call(
        body,
        "slot_sums",
        [f32(rows, width)] * 2,
        [IN_VMEM] * 2,
        cost=kernel_cost(rows, count, width),
    )(codes, lookup_grads)


def finish_first_ring(own0, back0, next0, own1, next1, back1):
    slots, width = LANES, own0.shape[1]

    def body(o0, b0, n0, o1, n1, b1, far0, far1, ahead, behind, own):
        def total(table, offset):
            piece = pl.ds(offset * slots, slots)
            refs = (o0, b0, n0) if table == 0 else (o1, n1, b1)
            return refs[0][piece, :] + refs[1][piece, :] + refs[2][piece, :]

        far0[...] = total(0, 2)
        far1[...] = total(1, 2)
        for table in range(2):
            piece = pl.ds(table * slots, slots)
            ahead[piece, :] = total(table, 1)
            behind[piece, :] = total(table, 3)
            own[piece, :] = total(table, 0)

    return call(
        body,
        "finish_first_ring",
        [f32(slots, width)] * 2 + [f32(2 * slots, width)] * 3,
        [IN_VMEM] * 6,
    )(own0, back0, next0, own1, next1, back1)


def add_far(ahead, far0, behind, far1):
    slots = LANES

    def body(a, f0, b, f1, new_a, new_b):
        low, high = pl.ds(0, slots), pl.ds(slots, slots)
        new_a[low, :] = a[low, :] + f0[...]
        new_a[high, :] = a[high, :]
        new_b[low, :] = b[low, :]
        new_b[high, :] = b[high, :] + f1[...]

    return call(body, "add_far", [f32(*ahead.shape)] * 2, [IN_VMEM] * 4)(ahead, far0, behind, far1)


def eye():
    shape = (LANES, LANES)
    return lax.broadcasted_iota(jnp.int32, shape, 0) == lax.broadcasted_iota(jnp.int32, shape, 1)


def turn(vector, diagonal):
    axis = 1 if vector.shape[0] == 1 else 0
    square = jnp.where(diagonal, jnp.broadcast_to(vector, (LANES, LANES)), 0.0)
    return jnp.sum(square, axis=axis, keepdims=True)


def finish_second_ring(own, ahead, behind, unique_rows, rows_dev):
    slots, width = LANES, own.shape[1]

    def body(o, a, b, unique_ref, payload):
        diagonal = eye()
        for table in range(2):
            piece = pl.ds(table * slots, slots)
            payload[:, pl.ds(table * width, width)] = o[piece, :] + a[piece, :] + b[piece, :]
            numbers = unique_ref[table : table + 1, :]
            numbers = jnp.where(numbers < 0, -1, numbers & (rows_dev - 1)).astype(jnp.float32)
            column = pl.ds((2 * width) + table * LANES, LANES)
            payload[:, column] = jnp.broadcast_to(turn(numbers, diagonal), (slots, LANES))

    return call(body, "finish_second_ring", [f32(slots, 2 * width + 2 * LANES)], [IN_VMEM] * 4)(
        own, ahead, behind, unique_rows
    )[0]


def apply_update(arrived, tables, accums):
    rows_dev, width = tables.shape[1:]
    rows = 256
    count = rows_dev // rows

    def body(arrived_ref, tables_ref, accums_ref, new_tables_hbm, new_accums_ref, done_ref, sems):
        diagonal = eye()
        copies = []
        for table in range(2):
            values = arrived_ref[:, table * width : (table + 1) * width]
            high = values.astype(jnp.bfloat16)
            rest = values - high.astype(jnp.float32)
            middle = rest.astype(jnp.bfloat16)
            low = (rest - middle.astype(jnp.float32)).astype(jnp.bfloat16)
            pieces = jnp.concatenate([high, middle, low], axis=0)
            first = 2 * width + table * LANES
            numbers = jnp.where(diagonal, arrived_ref[:, first : first + LANES], 0.0)
            numbers = jnp.sum(numbers, axis=0, keepdims=True).astype(jnp.int32)
            for block in range(count):
                base = block * rows
                hit = lax.broadcasted_iota(jnp.int32, (rows, LANES), 0) + base == numbers
                onehot = jnp.where(hit, jnp.float32(1), jnp.float32(0)).astype(jnp.bfloat16)
                onehot = jnp.concatenate([onehot] * 3, axis=1)
                row_grads = jnp.dot(onehot, pieces, preferred_element_type=jnp.float32)
                squares = jnp.sum(row_grads * row_grads, axis=1, keepdims=True)
                for start in range(0, rows, LANES):
                    place = pl.ds(base + start, LANES)
                    square = turn(squares[start : start + LANES], diagonal)
                    accum = accums_ref[table : table + 1, place] + square * (1.0 / width)
                    new_accums_ref[table : table + 1, place] = accum
                    scale = turn(learning_rate / (jnp.sqrt(accum) + epsilon), diagonal)
                    step = row_grads[start : start + LANES] * scale
                    done_ref[table, place, :] = tables_ref[table, place, :] - step
                place = pl.ds(base, rows)
                copies.append(
                    pltpu.make_async_copy(
                        done_ref.at[table, place],
                        new_tables_hbm.at[table, place],
                        sems.at[table * count + block],
                    )
                )
                copies[-1].start()
        for copy in copies:
            copy.wait()

    return call(
        body,
        "apply_update",
        [f32(*tables.shape), f32(*accums.shape)],
        [IN_VMEM] * 3,
        [IN_HBM, IN_VMEM],
        [pltpu.VMEM(tables.shape, jnp.float32), pltpu.SemaphoreType.DMA((2 * count,))],
    )(arrived, tables, accums)


def local(lookup_grads, slot_index, unique_rows, tables, accums):
    n_group = lax.axis_size("group")
    n_local = lax.axis_size("local")
    even = lax.axis_index("group") & 1 == 0
    z = lax.shift_right_logical(lax.axis_index("local"), 2)
    x = lax.axis_index("local") & (SIDE - 1)
    place = jnp.stack(
        [
            jnp.where(even, x, z),
            jnp.where(even, z, x),
            jnp.where(even, 7, 9),
            jnp.where(even, 9, 7),
        ]
    ).astype(jnp.int32)

    def send(value, stage, step):
        return lax.ppermute(value, AXES, ring_pairs(n_group, n_local, stage, step))

    far0, far1, grads, codes = first_sums(place, slot_index, lookup_grads, (2, 2))
    far0 = send(far0, 0, 1)
    far1 = send(far1, 0, -1)
    back0, next1 = slot_sums(codes, grads, (3, 1))
    next1 = send(next1, 0, 1)
    back0 = send(back0, 0, -1)
    next0, back1 = slot_sums(codes, grads, (1, 3))
    next0 = send(next0 + far0, 0, 1)
    back1 = send(back1 + far1, 0, -1)
    own0, own1 = slot_sums(codes, grads, (0, 0))

    far0, far1, ahead, behind, own = finish_first_ring(own0, back0, next0, own1, next1, back1)
    far0 = send(far0, 1, 1)
    far1 = send(far1, 1, -1)
    ahead, behind = add_far(ahead, far0, behind, far1)
    ahead = send(ahead, 1, 1)
    behind = send(behind, 1, -1)
    payload = finish_second_ring(own, ahead, behind, unique_rows, tables.shape[1])

    arrived = lax.all_to_all(payload, "group", split_axis=0, concat_axis=0, tiled=True)
    new_tables, new_accums = apply_update(arrived, tables, accums)
    return (new_tables, new_accums)


def solution(mesh):
    return jax.shard_map(
        local,
        mesh=mesh,
        in_specs=(
            P(("group", "local"), None),
            P(None, ("group", "local")),
            P(None, ("group", "local")),
            P(None, ("group", "local"), None),
            P(None, ("group", "local")),
        ),
        out_specs=(P(None, ("group", "local"), None), P(None, ("group", "local"))),
        check_vma=False,
    )
```

time: 160 us -> 71.2 us (0.45)
  matrix products: 43.5 us -> 0 us
  waiting for transfers between devices: 51.1 us -> 11.1 us
  other arithmetic: 31.9 us -> 0.21 us
  Pallas kernels: 0 us -> 22.9 us
  blocking collectives: 0 us -> 18.8 us
  local copies, waits for them, and re-layouts: 15 us -> 0.86 us
    all_to_all x2 -> x0, waiting for transfers between devices: 51.1 us -> none  [the longest x1 51.1 us: local(): lax.all_to_all(ordered, ('group', 'local'), split_axis=0, concat_axis=0,...]
    dot_general x8 -> x0, matrix products: 43.5 us -> none  [accumulate(): lax.dot_general(onehot, gradients, (((0,), (0,)), ((), ())), preferred_el...]
    pallas_call x0 -> x8, Pallas kernels: none -> 22.9 us  [the longest x3 13.4 us: slot_sums(): call(body, 'slot_sums', [f32(rows, width)] * 2, [IN_VMEM] * 2, cost=kerne...]
    add x6 -> x2, other arithmetic: 21.9 us -> 0.14 us  [the longest x1 0.07 us: local(): back1 = send(back1 + far1, 0, -1)]
    all_to_all x0 -> x1, blocking collectives: none -> 18.8 us  [local(): lax.all_to_all(payload, 'group', split_axis=0, concat_axis=0, tiled=True)]
    all_to_all x2 -> x0, starting transfers between devices: 16.8 us -> none  [the longest x1 10.8 us: local(): lax.all_to_all(ordered, ('group', 'local'), split_axis=0, concat_axis=0,...]
    ppermute x0 -> x10, starting transfers between devices: none -> 16.3 us  [send(): return lax.ppermute(value, AXES, ring_pairs(n_group, n_local, stage, step))]
    ppermute x0 -> x10, waiting for transfers between devices: none -> 11.1 us  [send(): return lax.ppermute(value, AXES, ring_pairs(n_group, n_local, stage, step))]
  transfers between devices with their start and end apart: 2 -> 10, of which waited for: 1 -> 4; matrix products, arithmetic and copies ran while one was open for 50% -> 0% of each run, Pallas kernels for 0% -> 19%
where the time goes in v2:
time: 71.2 us; the launch traced here: 71 us
  Pallas kernels  22.9 us (32%)
  blocking collectives  18.8 us (26%)
  starting transfers between devices  16.3 us (23%)
  waiting for transfers between devices  11.1 us (16%)
  between operations  0.91 us (1%)
  local copies, waits for them, and re-layouts  0.86 us (1%)
    all_to_all x1, blocking collectives, local(): lax.all_to_all(payload, 'group', split_axis=0, concat_axis=0, tiled=True)  18.8 us
    ppermute x10, starting transfers between devices, send(): return lax.ppermute(value, AXES, ring_pairs(n_group, n_local, stage, step))  16.3 us
    pallas_call x3, Pallas kernels, slot_sums(): call(body, 'slot_sums', [f32(rows, width)] * 2, [IN_VMEM] * 2, cost=kerne...  13.4 us
    ppermute x10, waiting for transfers between devices, send(): return lax.ppermute(value, AXES, ring_pairs(n_group, n_local, stage, step))  11.1 us
    pallas_call x1, Pallas kernels, first_sums(): call(body, 'first_sums', [f32(rows, width), f32(rows, width), jax.ShapeDt...  6.6 us
    pallas_call x1, Pallas kernels, apply_update(): call(body, 'apply_update', [f32(*tables.shape), f32(*accums.shape)], [IN_...  2.58 us
  transfers between devices with their start and end apart: 10, of which 4 were waited for; matrix products, arithmetic and copies ran while one was open for 0% of the time, Pallas kernels for 19%

profile of v2, /device:TPU:1, one launch (start us, length us, event | category | flops | bytes accessed | tf_op | source)
XLA Modules:
  0.0 71.0 jit_solution(17391235364705893459)
XLA Ops:
  0.6 0.1 pad_add_fusion.place_ref
  0.7 0.8 %copy-done.1 = s32[2,8192]{1,0:T(2,128)S(1)} copy-done((s32[2,8192]{1,0:T(2,128)S(1)}, s32[2,8192]{1,0:T(2,128)}, u32[]{:S(2)}) %copy-start.1) | copy-done | bytes 65560
  1.6 6.6 %first_sums.1 = (f32[512,256]{1,0:T(8,128)S(1)}, f32[512,256]{1,0:T(8,128)S(1)}, bf16[8192,256]{1,0:T(8,128)(2,1)S(1)}, s32[2,8192]{1,0:T(2,128)S(1)}) custom-call(s32[4]{0:T(128)S(1)} %pad_add_fusion.place_ref, s32[2,8192]{1,0:T(2,128)S(1)} %copy-done.1, bf16[8192,256]{1,0:T(8,128)(2,1)} %grads_hbm.1), custom_call_target="tpu_custom_call" | custom-call | flops 429496736 | bytes 419430 | tf_op jit(solution)/shard_map/first_sums/pallas_call | solution.py:98
  8.2 4.7 %collective-permute-start.4 = (f32[512,256]{1,0:T(8,128)S(1)}, f32[512,256]{1,0:T(8,128)S(1)}, u32[]{:S(2)}, u32[]{:S(2)}) collective-permute-start(f32[512,256]{1,0:T(8,128)S(1)} %get-tuple-element.28), channel_id=1, source_target_pairs={{0,3},{1,0},{2,1},{3,2},{4,7},{5,4},{6,5},{7,6},{8,11},{9,8},{10,9... | collective-permute-start | bytes 1572872 | tf_op jit(solution)/shard_map/ppermute | solution.py:274
  12.8 0.0 collective-permute-start.1
  12.8 4.5 %slot_sums.4 = (f32[512,256]{1,0:T(8,128)S(1)}, f32[512,256]{1,0:T(8,128)S(1)}) custom-call(s32[2,8192]{1,0:T(2,128)S(1)} %get-tuple-element.19.codes_ref, bf16[8192,256]{1,0:T(8,128)(2,1)S(1)} %get-tuple-element.20.grads_ref), custom_call_target="tpu_custom_call" | custom-call | flops 429496736 | bytes 419430 | tf_op jit(solution)/shard_map/slot_sums/pallas_call | solution.py:127
  17.3 2.8 %collective-permute-start = (f32[512,256]{1,0:T(8,128)S(1)}, f32[512,256]{1,0:T(8,128)S(1)}, u32[]{:S(2)}, u32[]{:S(2)}) collective-permute-start(f32[512,256]{1,0:T(8,128)S(1)} %get-tuple-element.22), channel_id=1, source_target_pairs={{0,3},{1,0},{2,1},{3,2},{4,7},{5,4},{6,5},{7,6},{8,11},{9,8},{10,9... | collective-permute-start | bytes 1572872 | tf_op jit(solution)/shard_map/ppermute | solution.py:274
  20.1 4.5 %slot_sums.5 = (f32[512,256]{1,0:T(8,128)S(1)}, f32[512,256]{1,0:T(8,128)S(1)}) custom-call(s32[2,8192]{1,0:T(2,128)S(1)} %get-tuple-element.19.codes_ref, bf16[8192,256]{1,0:T(8,128)(2,1)S(1)} %get-tuple-element.20.grads_ref), custom_call_target="tpu_custom_call" | custom-call | flops 429496736 | bytes 419430 | tf_op jit(solution)/shard_map/slot_sums/pallas_call | solution.py:127
  24.5 0.0 collective-permute-done.4
  24.5 0.1 add.7
  24.6 2.7 %collective-permute-start.5 = (f32[512,256]{1,0:T(8,128)S(1)}, f32[512,256]{1,0:T(8,128)S(1)}, u32[]{:S(2)}, u32[]{:S(2)}) collective-permute-start(f32[512,256]{1,0:T(8,128)S(1)} %add.7), channel_id=1, source_target_pairs={{0,3},{1,0},{2,1},{3,2},{4,7},{5,4},{6,5},{7,6},{8,11},{9,8},{10,9... | collective-permute-start | bytes 1572872 | tf_op jit(solution)/shard_map/ppermute | solution.py:274
  27.4 0.0 collective-permute-done.1
  27.4 0.1 add.6
  27.4 0.0 copy-start.3
  27.4 0.0 copy-start
  27.5 0.0 copy-start.2
  27.5 0.3 collective-permute-start.2
  27.7 4.5 %slot_sums.3 = (f32[512,256]{1,0:T(8,128)S(1)}, f32[512,256]{1,0:T(8,128)S(1)}) custom-call(s32[2,8192]{1,0:T(2,128)S(1)} %get-tuple-element.19.codes_ref, bf16[8192,256]{1,0:T(8,128)(2,1)S(1)} %get-tuple-element.20.grads_ref), custom_call_target="tpu_custom_call" | custom-call | flops 429496736 | bytes 419430 | tf_op jit(solution)/shard_map/slot_sums/pallas_call | solution.py:127
  32.2 0.0 collective-permute-done.b0
  32.2 0.0 collective-permute-done.3.n1
  32.2 1.2 %collective-permute-done.5.b1 = f32[512,256]{1,0:T(8,128)S(1)} collective-permute-done((f32[512,256]{1,0:T(8,128)S(1)}, f32[512,256]{1,0:T(8,128)S(1)}, u32[]{:S(2)}, u32[]{:S(2)}) %collective-permute-start.5) | collective-permute-done | bytes 524320 | tf_op jit(solution)/shard_map/ppermute | solution.py:274
  33.5 3.8 %collective-permute-done.2.n0 = f32[512,256]{1,0:T(8,128)S(1)} collective-permute-done((f32[512,256]{1,0:T(8,128)S(1)}, f32[512,256]{1,0:T(8,128)S(1)}, u32[]{:S(2)}, u32[]{:S(2)}) %collective-permute-start.2) | collective-permute-done | bytes 524320 | tf_op jit(solution)/shard_map/ppermute | solution.py:274
  37.3 0.2 finish_first_ring.1
  37.4 1.0 %collective-permute-start.6 = (f32[128,256]{1,0:T(8,128)S(1)}, f32[128,256]{1,0:T(8,128)S(1)}, u32[]{:S(2)}, u32[]{:S(2)}) collective-permute-start(f32[128,256]{1,0:T(8,128)S(1)} %get-tuple-element.31), channel_id=1, source_target_pairs={{0,4},{1,5},{2,6},{3,7},{4,8},{5,9},{6,10},{7,11},{8,12},{9,13},{1... | collective-permute-start | bytes 393224 | tf_op jit(solution)/shard_map/ppermute | solution.py:274
  38.4 1.8 %collective-permute-start.7 = (f32[128,256]{1,0:T(8,128)S(1)}, f32[128,256]{1,0:T(8,128)S(1)}, u32[]{:S(2)}, u32[]{:S(2)}) collective-permute-start(f32[128,256]{1,0:T(8,128)S(1)} %get-tuple-element.33), channel_id=1, source_target_pairs={{0,12},{1,13},{2,14},{3,15},{4,0},{5,1},{6,2},{7,3},{8,4},{9,5},{1... | collective-permute-start | bytes 393224 | tf_op jit(solution)/shard_map/ppermute | solution.py:274
  40.2 2.4 %collective-permute-done.6.f0 = f32[128,256]{1,0:T(8,128)S(1)} collective-permute-done((f32[128,256]{1,0:T(8,128)S(1)}, f32[128,256]{1,0:T(8,128)S(1)}, u32[]{:S(2)}, u32[]{:S(2)}) %collective-permute-start.6) | collective-permute-done | bytes 131104 | tf_op jit(solution)/shard_map/ppermute | solution.py:274
  42.6 1.3 %collective-permute-start.8 = (f32[256,256]{1,0:T(8,128)S(1)}, f32[256,256]{1,0:T(8,128)S(1)}, u32[]{:S(2)}, u32[]{:S(2)}) collective-permute-start(f32[256,256]{1,0:T(8,128)S(1)} %get-tuple-element.34), channel_id=1, source_target_pairs={{0,4},{1,5},{2,6},{3,7},{4,8},{5,9},{6,10},{7,11},{8,12},{9,13},{1... | collective-permute-start | bytes 786440 | tf_op jit(solution)/shard_map/ppermute | solution.py:274
  43.8 1.8 %collective-permute-start.9 = (f32[256,256]{1,0:T(8,128)S(1)}, f32[256,256]{1,0:T(8,128)S(1)}, u32[]{:S(2)}, u32[]{:S(2)}) collective-permute-start(f32[256,256]{1,0:T(8,128)S(1)} %get-tuple-element.35), channel_id=1, source_target_pairs={{0,12},{1,13},{2,14},{3,15},{4,0},{5,1},{6,2},{7,3},{8,4},{9,5},{1... | collective-permute-start | bytes 786440 | tf_op jit(solution)/shard_map/ppermute | solution.py:274
  45.7 3.7 %collective-permute-done.8.a = f32[256,256]{1,0:T(8,128)S(1)} collective-permute-done((f32[256,256]{1,0:T(8,128)S(1)}, f32[256,256]{1,0:T(8,128)S(1)}, u32[]{:S(2)}, u32[]{:S(2)}) %collective-permute-start.8) | collective-permute-done | bytes 262176 | tf_op jit(solution)/shard_map/ppermute | solution.py:274
  49.4 0.1 finish_second_ring.1
  49.5 18.8 %all_to_all.11 = f32[8,16,768]{2,1,0:T(8,128)S(1)} all-to-all(f32[8,16,768]{2,1,0:T(8,128)S(1)} %bitcast.7), channel_id=1, replica_groups=mesh['group'=8,'local'=16] {'group'}, dimensions={0} | all-to-all | bytes 786432 | tf_op jit(solution)/shard_map/all_to_all | solution.py:295
  68.3 2.6 %apply_update.1 = (f32[2,1024,256]{2,1,0:T(8,128)}, f32[2,1024]{1,0:T(2,128)}) custom-call(f32[128,768]{1,0:T(8,128)S(1)} %bitcast.6, f32[2,1024,256]{2,1,0:T(8,128)S(1)} %copy-done, f32[2,1024]{1,0:T(2,128)S(1)} %copy-done.2), custom_call_target="tpu_custom_call" | custom-call | tf_op jit(solution)/shard_map/apply_update/pallas_call | solution.py:248
  (8 shorter events, 0.1 us)
Async XLA Ops:
  0.7 0.8 %copy-start.1 = (s32[2,8192]{1,0:T(2,128)S(1)}, s32[2,8192]{1,0:T(2,128)}, u32[]{:S(2)}) copy-start(s32[2,8192]{1,0:T(2,128)} %index_hbm.1) | copy-start | bytes 196612
  8.2 16.4 %collective-permute-start.4 = (f32[512,256]{1,0:T(8,128)S(1)}, f32[512,256]{1,0:T(8,128)S(1)}, u32[]{:S(2)}, u32[]{:S(2)}) collective-permute-start(f32[512,256]{1,0:T(8,128)S(1)} %get-tuple-element.28), channel_id=1, source_target_pairs={{0,3},{1,0},{2,1},{3,2},{4,7},{5,4},{6,5},{7,6},{8,11},{9,8},{10,9... | collective-permute-start | bytes 1572872 | tf_op jit(solution)/shard_map/ppermute | solution.py:274
  12.8 14.5 %collective-permute-start.1 = (f32[512,256]{1,0:T(8,128)S(1)}, f32[512,256]{1,0:T(8,128)S(1)}, u32[]{:S(2)}, u32[]{:S(2)}) collective-permute-start(f32[512,256]{1,0:T(8,128)S(1)} %get-tuple-element.24), channel_id=1, source_target_pairs={{0,1},{1,2},{2,3},{3,0},{4,5},{5,6},{6,7},{7,4},{8,9},{9,10},{10,1... | collective-permute-start | bytes 1572872 | tf_op jit(solution)/shard_map/ppermute | solution.py:274
  17.3 14.9 %collective-permute-start = (f32[512,256]{1,0:T(8,128)S(1)}, f32[512,256]{1,0:T(8,128)S(1)}, u32[]{:S(2)}, u32[]{:S(2)}) collective-permute-start(f32[512,256]{1,0:T(8,128)S(1)} %get-tuple-element.22), channel_id=1, source_target_pairs={{0,3},{1,0},{2,1},{3,2},{4,7},{5,4},{6,5},{7,6},{8,11},{9,8},{10,9... | collective-permute-start | bytes 1572872 | tf_op jit(solution)/shard_map/ppermute | solution.py:274
  20.0 12.2 %collective-permute-start.3 = (f32[512,256]{1,0:T(8,128)S(1)}, f32[512,256]{1,0:T(8,128)S(1)}, u32[]{:S(2)}, u32[]{:S(2)}) collective-permute-start(f32[512,256]{1,0:T(8,128)S(1)} %get-tuple-element.26), channel_id=1, source_target_pairs={{0,1},{1,2},{2,3},{3,0},{4,5},{5,6},{6,7},{7,4},{8,9},{9,10},{10,1... | collective-permute-start | bytes 1572872 | tf_op jit(solution)/shard_map/ppermute | solution.py:274
  24.6 8.9 %collective-permute-start.5 = (f32[512,256]{1,0:T(8,128)S(1)}, f32[512,256]{1,0:T(8,128)S(1)}, u32[]{:S(2)}, u32[]{:S(2)}) collective-permute-start(f32[512,256]{1,0:T(8,128)S(1)} %add.7), channel_id=1, source_target_pairs={{0,3},{1,0},{2,1},{3,2},{4,7},{5,4},{6,5},{7,6},{8,11},{9,8},{10,9... | collective-permute-start | bytes 1572872 | tf_op jit(solution)/shard_map/ppermute | solution.py:274
  27.4 21.9 %copy-start.3 = (s32[2,128]{1,0:T(2,128)S(1)}, s32[2,128]{1,0:T(2,128)}, u32[]{:S(2)}) copy-start(s32[2,128]{1,0:T(2,128)} %unique_ref.1) | copy-start | bytes 3076
  27.4 40.9 %copy-start = (f32[2,1024,256]{2,1,0:T(8,128)S(1)}, f32[2,1024,256]{2,1,0:T(8,128)}, u32[]{:S(2)}) copy-start(f32[2,1024,256]{2,1,0:T(8,128)} %tables_ref.1) | copy-start | bytes 6291460
  27.5 40.8 %copy-start.2 = (f32[2,1024]{1,0:T(2,128)S(1)}, f32[2,1024]{1,0:T(2,128)}, u32[]{:S(2)}) copy-start(f32[2,1024]{1,0:T(2,128)} %accums_ref.1) | copy-start | bytes 24580
  27.5 9.8 %collective-permute-start.2 = (f32[512,256]{1,0:T(8,128)S(1)}, f32[512,256]{1,0:T(8,128)S(1)}, u32[]{:S(2)}, u32[]{:S(2)}) collective-permute-start(f32[512,256]{1,0:T(8,128)S(1)} %add.6), channel_id=1, source_target_pairs={{0,1},{1,2},{2,3},{3,0},{4,5},{5,6},{6,7},{7,4},{8,9},{9,10},{10,1... | collective-permute-start | bytes 1572872 | tf_op jit(solution)/shard_map/ppermute | solution.py:274
  37.4 5.1 %collective-permute-start.6 = (f32[128,256]{1,0:T(8,128)S(1)}, f32[128,256]{1,0:T(8,128)S(1)}, u32[]{:S(2)}, u32[]{:S(2)}) collective-permute-start(f32[128,256]{1,0:T(8,128)S(1)} %get-tuple-element.31), channel_id=1, source_target_pairs={{0,4},{1,5},{2,6},{3,7},{4,8},{5,9},{6,10},{7,11},{8,12},{9,13},{1... | collective-permute-start | bytes 393224 | tf_op jit(solution)/shard_map/ppermute | solution.py:274
  38.4 4.1 %collective-permute-start.7 = (f32[128,256]{1,0:T(8,128)S(1)}, f32[128,256]{1,0:T(8,128)S(1)}, u32[]{:S(2)}, u32[]{:S(2)}) collective-permute-start(f32[128,256]{1,0:T(8,128)S(1)} %get-tuple-element.33), channel_id=1, source_target_pairs={{0,12},{1,13},{2,14},{3,15},{4,0},{5,1},{6,2},{7,3},{8,4},{9,5},{1... | collective-permute-start | bytes 393224 | tf_op jit(solution)/shard_map/ppermute | solution.py:274
  42.6 6.8 %collective-permute-start.8 = (f32[256,256]{1,0:T(8,128)S(1)}, f32[256,256]{1,0:T(8,128)S(1)}, u32[]{:S(2)}, u32[]{:S(2)}) collective-permute-start(f32[256,256]{1,0:T(8,128)S(1)} %get-tuple-element.34), channel_id=1, source_target_pairs={{0,4},{1,5},{2,6},{3,7},{4,8},{5,9},{6,10},{7,11},{8,12},{9,13},{1... | collective-permute-start | bytes 786440 | tf_op jit(solution)/shard_map/ppermute | solution.py:274
  43.8 5.5 %collective-permute-start.9 = (f32[256,256]{1,0:T(8,128)S(1)}, f32[256,256]{1,0:T(8,128)S(1)}, u32[]{:S(2)}, u32[]{:S(2)}) collective-permute-start(f32[256,256]{1,0:T(8,128)S(1)} %get-tuple-element.35), channel_id=1, source_target_pairs={{0,12},{1,13},{2,14},{3,15},{4,0},{5,1},{6,2},{7,3},{8,4},{9,5},{1... | collective-permute-start | bytes 786440 | tf_op jit(solution)/shard_map/ppermute | solution.py:274

commit v3 on v2

v3 whole, which is shorter than its diff:
```python
import jax
import jax.numpy as jnp
from jax import lax
from jax.experimental import pallas as pl
from jax.experimental.pallas import tpu as pltpu
from jax.sharding import PartitionSpec as P

learning_rate = 0.1
epsilon = 1e-08

AXES = ("group", "local")
SIDE = 4
CORES = 2
LANES = 128
VMEM_BYTES = 16 << 20
FIRST_BYTES = 48 << 20
IN_VMEM = pl.BlockSpec(memory_space=pltpu.VMEM)
IN_SMEM = pl.BlockSpec(memory_space=pltpu.SMEM)
IN_HBM = pl.BlockSpec(memory_space=pltpu.HBM)


def ring_pairs(n_group, n_local, step):
    pairs = []
    for group in range(n_group):
        for place in range(n_local):
            z, x = divmod(place, SIDE)
            if group % CORES == 0:
                x = (x + step) % SIDE
            else:
                z = (z + step) % SIDE
            pairs.append((group * n_local + place, group * n_local + z * SIDE + x))
    return pairs


def second_groups(n_group, n_local):
    groups = []
    for core in range(CORES):
        for first in range(SIDE):
            members = []
            for chip in range(n_group // CORES):
                for second in range(SIDE):
                    z, x = (second, first) if core == 0 else (first, second)
                    members.append((chip * CORES + core) * n_local + z * SIDE + x)
            groups.append(members)
    return groups


def call(body, name, out_shape, in_specs, out_specs=None, scratch=(), cost=None, vmem=VMEM_BYTES):
    return pl.pallas_call(
        body,
        out_shape=out_shape,
        in_specs=in_specs,
        out_specs=[IN_VMEM] * len(out_shape) if out_specs is None else out_specs,
        scratch_shapes=scratch,
        compiler_params=pltpu.CompilerParams(vmem_limit_bytes=vmem),
        cost_estimate=cost,
        name=name,
    )


def f32(*shape):
    return jax.ShapeDtypeStruct(shape, jnp.float32)


def kernel_cost(rows, count, width):
    return pl.CostEstimate(
        flops=4 * rows * count * width // 10, bytes_accessed=count * width // 5, transcendentals=0
    )


def add_block(codes, grads, targets, start, out_refs):
    rows = out_refs[0].shape[0]
    for (table, offset), out_ref in zip(targets, out_refs):
        target = lax.broadcasted_iota(jnp.int32, (rows, grads.shape[0]), 0) + offset * rows
        hit = target == codes[table : table + 1]
        onehot = jnp.where(hit, jnp.float32(1), jnp.float32(0)).astype(jnp.bfloat16)
        piece = jnp.dot(onehot, grads, preferred_element_type=jnp.float32)
        if start == 0:
            out_ref[...] = piece
        else:
            out_ref[...] += piece


def first_sums(place, slot_index, lookup_grads, targets):
    count, width = lookup_grads.shape
    rows = SIDE * LANES
    block = 1024
    blocks = count // block

    def body(place_ref, index_ref, grads_hbm, *refs):
        out_refs = refs[: len(targets)]
        grads_ref, codes_ref, sems = refs[len(targets) :]
        copies = []
        for i in range(blocks):
            piece = pl.ds(i * block, block)
            copies.append(
                pltpu.make_async_copy(grads_hbm.at[piece], grads_ref.at[piece], sems.at[i])
            )
        for copy in copies:
            copy.start()
        index = index_ref[...]
        first = lax.shift_right_logical(index, place_ref[2]) & (SIDE - 1)
        second = lax.shift_right_logical(index, place_ref[3]) & (SIDE - 1)
        first = (first - place_ref[0]) & (SIDE - 1)
        codes_ref[...] = first * rows + second * LANES + (index & (LANES - 1))
        for i in range(blocks):
            copies[i].wait()
            piece = pl.ds(i * block, block)
            add_block(codes_ref[:, piece], grads_ref[piece, :], targets, i, out_refs)

    return call(
        body,
        "first_sums",
        [
            *[f32(rows, width) for _ in targets],
            jax.ShapeDtypeStruct(lookup_grads.shape, lookup_grads.dtype),
            jax.ShapeDtypeStruct(slot_index.shape, jnp.int32),
        ],
        [IN_SMEM, IN_VMEM, IN_HBM],
        scratch=[
            pltpu.SemaphoreType.DMA((blocks,)),
        ],
        cost=kernel_cost(rows, count, width),
        vmem=FIRST_BYTES,
    )(place, slot_index, lookup_grads)


def slot_sums(codes, lookup_grads, targets):
    count, width = lookup_grads.shape
    rows = SIDE * LANES
    block = 1024

    def body(codes_ref, grads_ref, *out_refs):
        for start in range(0, count, block):
            piece = pl.ds(start, block)
            add_block(codes_ref[:, piece], grads_ref[piece, :], targets, start, out_refs)

    return call(
        body,
        "slot_sums",
        [f32(rows, width) for _ in targets],
        [IN_VMEM] * 2,
        cost=kernel_cost(rows, count, width),
    )(codes, lookup_grads)


def finish_first_ring(place, unique_rows, own0, back0, next0, own1, next1, back1):
    rows, width = own0.shape
    chips = SIDE
    block = rows // SIDE // chips
    tiles = 2 * width // LANES

    def body(place_ref, unique_ref, o0, b0, n0, o1, n1, b1, spread):
        numbers = unique_ref[...].astype(jnp.float32) + 1.0
        numbers = jnp.concatenate([numbers, jnp.zeros((6, LANES), jnp.float32)], axis=0)
        for second in range(SIDE):
            mine = jnp.where(place_ref[1] == second, numbers, 0.0)
            for chip in range(chips):
                member = chip * SIDE + second
                piece = pl.ds((second * chips + chip) * block, block)
                for table, refs in enumerate([(o0, b0, n0), (o1, n1, b1)]):
                    total = refs[0][piece, :] + refs[1][piece, :] + refs[2][piece, :]
                    for tile in range(tiles // 2):
                        spot = pl.ds((table * (tiles // 2) + tile) * block, block)
                        spread[member, spot, :] = total[:, tile * LANES : (tile + 1) * LANES]
                spread[member, pl.ds(tiles * block, 8), :] = mine

    return call(
        body,
        "finish_first_ring",
        [f32(SIDE * chips, tiles * block + 8, LANES)],
        [IN_SMEM] + [IN_VMEM] * 7,
    )(place, unique_rows, own0, back0, next0, own1, next1, back1)[0]


def finish_second_ring(place, spread):
    members, rows, lanes = spread.shape
    chips = members // SIDE
    half = LANES // 8
    tiles = (rows - 8) // (CORES * half)

    def body(place_ref, spread_ref, kept, given):
        core = place_ref[4] & 1

        def total(chip, piece):
            pieces = [spread_ref[chip * SIDE + second, piece, :] for second in range(SIDE)]
            return (pieces[0] + pieces[1]) + (pieces[2] + pieces[3])

        for chip in range(chips):
            for tile in range(tiles):
                low = total(chip, pl.ds(tile * CORES * half, half))
                high = total(chip, pl.ds(tile * CORES * half + half, half))
                spot = pl.ds(tile * half, half)
                kept[chip, spot, :] = jnp.where(core == 0, low, high)
                given[chip, spot, :] = jnp.where(core == 0, high, low)
            numbers = total(chip, pl.ds(rows - 8, 8))
            kept[chip, pl.ds(tiles * half, 8), :] = numbers
            given[chip, pl.ds(tiles * half, 8), :] = numbers

    return call(
        body, "finish_second_ring", [f32(chips, tiles * half + 8, lanes)] * 2, [IN_SMEM, IN_VMEM]
    )(place, spread)


def eye():
    shape = (LANES, LANES)
    return lax.broadcasted_iota(jnp.int32, shape, 0) == lax.broadcasted_iota(jnp.int32, shape, 1)


def turn(vector, diagonal):
    axis = 1 if vector.shape[0] == 1 else 0
    square = jnp.where(diagonal, jnp.broadcast_to(vector, (LANES, LANES)), 0.0)
    return jnp.sum(square, axis=axis, keepdims=True)


def apply_update(place, kept, swapped, tables, accums):
    rows_dev, width = tables.shape[1:]
    rows = 256
    count = rows_dev // rows

    chips, slots = kept.shape[:2]
    bucket = LANES // (CORES * chips)
    slots -= 8
    tiles = width // LANES

    def body(place_ref, kept_ref, swapped_ref, tables_ref, accums_ref, *refs):
        new_tables_hbm, new_accums_ref, done_ref, sems = refs
        diagonal = eye()
        copies = []
        sources = [(ref, chip) for ref in (kept_ref, swapped_ref) for chip in range(chips)]
        group = place_ref[4]
        lane = lax.broadcasted_iota(jnp.int32, (8, LANES), 1) // bucket
        local_rows = jnp.zeros((8, LANES), jnp.int32)
        for spot, (ref, chip) in enumerate(sources):
            listed = ref[chip, pl.ds(slots, 8), :].astype(jnp.int32)
            listed = pltpu.roll(listed, ((spot - group) * bucket) & (LANES - 1), 1)
            local_rows = jnp.where(lane == spot, listed, local_rows)
        local_rows = jnp.where(local_rows == 0, -1, (local_rows - 1) & (rows_dev - 1))
        for table in range(2):
            columns = []
            for tile in range(table * tiles, (table + 1) * tiles):
                spot = pl.ds(tile * bucket, bucket)
                columns.append(jnp.concatenate([ref[chip, spot, :] for ref, chip in sources]))
            values = jnp.concatenate(columns, axis=1)
            high = values.astype(jnp.bfloat16)
            rest = values - high.astype(jnp.float32)
            middle = rest.astype(jnp.bfloat16)
            low = (rest - middle.astype(jnp.float32)).astype(jnp.bfloat16)
            pieces = jnp.concatenate([high, middle, low], axis=0)
            for block in range(count):
                base = block * rows
                hit = lax.broadcasted_iota(jnp.int32, (rows, LANES), 0) + base == local_rows[table : table + 1]
                onehot = jnp.where(hit, jnp.float32(1), jnp.float32(0)).astype(jnp.bfloat16)
                onehot = jnp.concatenate([onehot] * 3, axis=1)
                row_grads = jnp.dot(onehot, pieces, preferred_element_type=jnp.float32)
                squares = jnp.sum(row_grads * row_grads, axis=1, keepdims=True)
                for start in range(0, rows, LANES):
                    place = pl.ds(base + start, LANES)
                    square = turn(squares[start : start + LANES], diagonal)
                    accum = accums_ref[table : table + 1, place] + square * (1.0 / width)
                    new_accums_ref[table : table + 1, place] = accum
                    scale = turn(learning_rate / (jnp.sqrt(accum) + epsilon), diagonal)
                    step = row_grads[start : start + LANES] * scale
                    done_ref[table, place, :] = tables_ref[table, place, :] - step
                place = pl.ds(base, rows)
                copies.append(
                    pltpu.make_async_copy(
                        done_ref.at[table, place],
                        new_tables_hbm.at[table, place],
                        sems.at[table * count + block],
                    )
                )
                copies[-1].start()
        for copy in copies:
            copy.wait()

    return call(
        body,
        "apply_update",
        [f32(*tables.shape), f32(*accums.shape)],
        [IN_SMEM] + [IN_VMEM] * 4,
        [IN_HBM, IN_VMEM],
        [pltpu.VMEM(tables.shape, jnp.float32), pltpu.SemaphoreType.DMA((2 * count,))],
    )(place, kept, swapped, tables, accums)


def local(lookup_grads, slot_index, unique_rows, tables, accums):
    n_group = lax.axis_size("group")
    n_local = lax.axis_size("local")
    even = lax.axis_index("group") & 1 == 0
    z = lax.shift_right_logical(lax.axis_index("local"), 2)
    x = lax.axis_index("local") & (SIDE - 1)
    place = jnp.stack(
        [
            jnp.where(even, x, z),
            jnp.where(even, z, x),
            jnp.where(even, 7, 9),
            jnp.where(even, 9, 7),
            lax.axis_index("group"),
        ]
    ).astype(jnp.int32)

    def send(value, step):
        return lax.ppermute(value, AXES, ring_pairs(n_group, n_local, step))

    far0, far1, grads, codes = first_sums(place, slot_index, lookup_grads, [(0, 2), (1, 2)])
    far0 = send(far0, 1)
    far1 = send(far1, -1)
    back0, next1 = slot_sums(codes, grads, [(0, 3), (1, 1)])
    next1 = send(next1, 1)
    back0 = send(back0, -1)
    next0, back1 = slot_sums(codes, grads, [(0, 1), (1, 3)])
    next0 = send(next0 + far0, 1)
    back1 = send(back1 + far1, -1)
    own0, own1 = slot_sums(codes, grads, [(0, 0), (1, 0)])

    spread = finish_first_ring(place, unique_rows, own0, back0, next0, own1, next1, back1)
    spread = lax.all_to_all(
        spread,
        AXES,
        split_axis=0,
        concat_axis=0,
        axis_index_groups=second_groups(n_group, n_local),
        tiled=True,
    )
    kept, given = finish_second_ring(place, spread)

    swapped = lax.ppermute(given, "group", [(i, i ^ 1) for i in range(n_group)])
    new_tables, new_accums = apply_update(place, kept, swapped, tables, accums)
    return (new_tables, new_accums)


def solution(mesh):
    return jax.shard_map(
        local,
        mesh=mesh,
        in_specs=(
            P(("group", "local"), None),
            P(None, ("group", "local")),
            P(None, ("group", "local")),
            P(None, ("group", "local"), None),
            P(None, ("group", "local")),
        ),
        out_specs=(P(None, ("group", "local"), None), P(None, ("group", "local"))),
        check_vma=False,
    )
```

time: 71.2 us -> 66.9 us (0.940)
  waiting for transfers between devices: 11.1 us -> 6.04 us
  Pallas kernels: 22.9 us -> 24.5 us
  starting transfers between devices: 16.3 us -> 15.3 us
    ppermute x10 -> x7, waiting for transfers between devices: 11.1 us -> 6.04 us  [the longest x6 5.04 us: send(): return lax.ppermute(value, AXES, ring_pairs(n_group, n_local, step))]
    ppermute x10 -> x7, starting transfers between devices: 16.3 us -> 15.3 us  [the longest x6 10.4 us: send(): return lax.ppermute(value, AXES, ring_pairs(n_group, n_local, step))]
    pallas_call x7 -> x6, Pallas kernels: 20.3 us -> 21.3 us  [the longest x3 13.4 us: slot_sums(): call(body, 'slot_sums', [f32(rows, width) for _ in targets], [IN_VMEM] *...]
  transfers between devices with their start and end apart: 10 -> 7, of which waited for: 4 -> 3; matrix products, arithmetic and copies ran while one was open for 0% -> 0% of each run, Pallas kernels for 19% -> 20%
where the time goes in v3:
time: 66.9 us; the launch traced here: 66.7 us
  Pallas kernels  24.5 us (37%)
  blocking collectives  18.9 us (28%)
  starting transfers between devices  15.3 us (23%)
  waiting for transfers between devices  6.04 us (9%)
  local copies, waits for them, and re-layouts  0.94 us (1%)
  between operations  0.9 us (1%)
    all_to_all x1, blocking collectives, local(): lax.all_to_all(spread, AXES, split_axis=0, concat_axis=0, axis_index_grou...  18.9 us
    pallas_call x3, Pallas kernels, slot_sums(): call(body, 'slot_sums', [f32(rows, width) for _ in targets], [IN_VMEM] *...  13.4 us
    ppermute x6, starting transfers between devices, send(): return lax.ppermute(value, AXES, ring_pairs(n_group, n_local, step))  10.4 us
    pallas_call x1, Pallas kernels, first_sums(): call(body, 'first_sums', [*[f32(rows, width) for _ in targets], jax.Shape...  6.5 us
    ppermute x6, waiting for transfers between devices, send(): return lax.ppermute(value, AXES, ring_pairs(n_group, n_local, step))  5.04 us
    ppermute x1, starting transfers between devices, local(): swapped = lax.ppermute(given, 'group', [(i, i ^ 1) for i in range(n_group)])  4.91 us
    pallas_call x1, Pallas kernels, apply_update(): call(body, 'apply_update', [f32(*tables.shape), f32(*accums.shape)], [IN_...  3.23 us
  transfers between devices with their start and end apart: 7, of which 3 were waited for; matrix products, arithmetic and copies ran while one was open for 0% of the time, Pallas kernels for 20%

profile of v3, /device:TPU:1, one launch (start us, length us, event | category | flops | bytes accessed | tf_op | source)
XLA Modules:
  0.0 66.7 jit_solution(1191470763055970481)
XLA Ops:
  0.6 0.1 stack.23.place_ref
  0.7 0.8 %copy-done.1 = s32[2,8192]{1,0:T(2,128)S(1)} copy-done((s32[2,8192]{1,0:T(2,128)S(1)}, s32[2,8192]{1,0:T(2,128)}, u32[]{:S(2)}) %copy-start.1) | copy-done | bytes 65560
  1.6 6.5 %first_sums.1 = (f32[512,256]{1,0:T(8,128)S(1)}, f32[512,256]{1,0:T(8,128)S(1)}, bf16[8192,256]{1,0:T(8,128)(2,1)S(1)}, s32[2,8192]{1,0:T(2,128)S(1)}) custom-call(s32[5]{0:T(128)S(1)} %stack.23.place_ref, s32[2,8192]{1,0:T(2,128)S(1)} %copy-done.1, bf16[8192,256]{1,0:T(8,128)(2,1)} %grads_hbm.1), custom_call_target="tpu_custom_call" | custom-call | flops 429496736 | bytes 419430 | tf_op jit(solution)/shard_map/first_sums/pallas_call | solution.py:111
  8.1 4.7 %collective-permute-start.4 = (f32[512,256]{1,0:T(8,128)S(1)}, f32[512,256]{1,0:T(8,128)S(1)}, u32[]{:S(2)}, u32[]{:S(2)}) collective-permute-start(f32[512,256]{1,0:T(8,128)S(1)} %get-tuple-element.23), channel_id=1, source_target_pairs={{0,3},{1,0},{2,1},{3,2},{4,7},{5,4},{6,5},{7,6},{8,11},{9,8},{10,9... | collective-permute-start | bytes 1572872 | tf_op jit(solution)/shard_map/ppermute | solution.py:304
  12.7 0.0 collective-permute-start.1
  12.7 4.5 %slot_sums.4 = (f32[512,256]{1,0:T(8,128)S(1)}, f32[512,256]{1,0:T(8,128)S(1)}) custom-call(s32[2,8192]{1,0:T(2,128)S(1)} %get-tuple-element.14.codes_ref, bf16[8192,256]{1,0:T(8,128)(2,1)S(1)} %get-tuple-element.15.grads_ref), custom_call_target="tpu_custom_call" | custom-call | flops 429496736 | bytes 419430 | tf_op jit(solution)/shard_map/slot_sums/pallas_call | solution.py:138
  17.2 2.7 %collective-permute-start = (f32[512,256]{1,0:T(8,128)S(1)}, f32[512,256]{1,0:T(8,128)S(1)}, u32[]{:S(2)}, u32[]{:S(2)}) collective-permute-start(f32[512,256]{1,0:T(8,128)S(1)} %get-tuple-element.17), channel_id=1, source_target_pairs={{0,3},{1,0},{2,1},{3,2},{4,7},{5,4},{6,5},{7,6},{8,11},{9,8},{10,9... | collective-permute-start | bytes 1572872 | tf_op jit(solution)/shard_map/ppermute | solution.py:304
  20.0 0.0 collective-permute-start.3
  20.0 4.5 %slot_sums.5 = (f32[512,256]{1,0:T(8,128)S(1)}, f32[512,256]{1,0:T(8,128)S(1)}) custom-call(s32[2,8192]{1,0:T(2,128)S(1)} %get-tuple-element.14.codes_ref, bf16[8192,256]{1,0:T(8,128)(2,1)S(1)} %get-tuple-element.15.grads_ref), custom_call_target="tpu_custom_call" | custom-call | flops 429496736 | bytes 419430 | tf_op jit(solution)/shard_map/slot_sums/pallas_call | solution.py:138
  24.4 0.0 collective-permute-done.4
  24.5 0.1 add.7
  24.5 2.8 %collective-permute-start.5 = (f32[512,256]{1,0:T(8,128)S(1)}, f32[512,256]{1,0:T(8,128)S(1)}, u32[]{:S(2)}, u32[]{:S(2)}) collective-permute-start(f32[512,256]{1,0:T(8,128)S(1)} %add.7), channel_id=1, source_target_pairs={{0,3},{1,0},{2,1},{3,2},{4,7},{5,4},{6,5},{7,6},{8,11},{9,8},{10,9... | collective-permute-start | bytes 1572872 | tf_op jit(solution)/shard_map/ppermute | solution.py:304
  27.3 0.0 collective-permute-done.1
  27.3 0.1 add.6
  27.4 0.0 copy-start.3
  27.4 0.3 collective-permute-start.2
  27.6 4.5 %slot_sums.3 = (f32[512,256]{1,0:T(8,128)S(1)}, f32[512,256]{1,0:T(8,128)S(1)}) custom-call(s32[2,8192]{1,0:T(2,128)S(1)} %get-tuple-element.14.codes_ref, bf16[8192,256]{1,0:T(8,128)(2,1)S(1)} %get-tuple-element.15.grads_ref), custom_call_target="tpu_custom_call" | custom-call | flops 429496736 | bytes 419430 | tf_op jit(solution)/shard_map/slot_sums/pallas_call | solution.py:138
  32.1 0.0 collective-permute-done.b0
  32.1 0.0 collective-permute-done.3.n1
  32.1 1.3 %collective-permute-done.5.b1 = f32[512,256]{1,0:T(8,128)S(1)} collective-permute-done((f32[512,256]{1,0:T(8,128)S(1)}, f32[512,256]{1,0:T(8,128)S(1)}, u32[]{:S(2)}, u32[]{:S(2)}) %collective-permute-start.5) | collective-permute-done | bytes 524320 | tf_op jit(solution)/shard_map/ppermute | solution.py:304
  33.4 3.7 %collective-permute-done.2.n0 = f32[512,256]{1,0:T(8,128)S(1)} collective-permute-done((f32[512,256]{1,0:T(8,128)S(1)}, f32[512,256]{1,0:T(8,128)S(1)}, u32[]{:S(2)}, u32[]{:S(2)}) %collective-permute-start.2) | collective-permute-done | bytes 524320 | tf_op jit(solution)/shard_map/ppermute | solution.py:304
  37.2 0.0 copy-done.3
  37.2 0.8 %finish_first_ring.1 = f32[16,136,128]{2,1,0:T(8,128)S(1)} custom-call(s32[5]{0:T(128)S(1)} %stack.23.place_ref, s32[2,128]{1,0:T(2,128)S(1)} %copy-done.3, f32[512,256]{1,0:T(8,128)S(1)} %get-tuple-element.16.o0, f32[512,256]{1,0:T(8,128)S(1)} %collective-permute-done.b0, f32[512,256]{1,0:T(8,128)S(1)} %collective-permute-done.2.n0, ...), custom_call_target="tpu_custom_call" | custom-call | tf_op jit(solution)/shard_map/finish_first_ring/pallas_call | solution.py:168
  37.9 0.0 copy-start
  37.9 0.0 copy-start.2
  37.9 18.9 %all_to_all.5.spread_ref = f32[16,136,128]{2,1,0:T(8,128)S(1)} all-to-all(f32[16,136,128]{2,1,0:T(8,128)S(1)} %finish_first_ring.1), channel_id=1, replica_groups={{0,4,8,12,32,36,40,44,64,68,72,76,96,100,104,108},{1,5,9,13,33,37,41,45..., dimensions={0} | all-to-all | bytes 2228224 | tf_op jit(solution)/shard_map/all_to_all | solution.py:318
  56.8 0.6 finish_second_ring.1
  57.4 4.9 %collective-permute-start.6 = (f32[4,72,128]{2,1,0:T(8,128)S(1)}, f32[4,72,128]{2,1,0:T(8,128)S(1)}, u32[]{:S(2)}, u32[]{:S(2)}) collective-permute-start(f32[4,72,128]{2,1,0:T(8,128)S(1)} %get-tuple-element.25), channel_id=1, source_target_pairs={{0,16},{16,0},{32,48},{48,32},{64,80},{80,64},{96,112},{112,96},{1... | collective-permute-start | bytes 442376 | tf_op jit(solution)/shard_map/ppermute | solution.py:328
  62.3 1.0 %collective-permute-done.6.swapped_ref = f32[4,72,128]{2,1,0:T(8,128)S(1)} collective-permute-done((f32[4,72,128]{2,1,0:T(8,128)S(1)}, f32[4,72,128]{2,1,0:T(8,128)S(1)}, u32[]{:S(2)}, u32[]{:S(2)}) %collective-permute-start.6) | collective-permute-done | bytes 147488 | tf_op jit(solution)/shard_map/ppermute | solution.py:328
  63.3 0.0 copy-done
  63.3 0.0 copy-done.2
  63.3 3.2 %apply_update.1 = (f32[2,1024,256]{2,1,0:T(8,128)}, f32[2,1024]{1,0:T(2,128)}) custom-call(s32[5]{0:T(128)S(1)} %stack.23.place_ref, f32[4,72,128]{2,1,0:T(8,128)S(1)} %get-tuple-element.24.kept_ref, f32[4,72,128]{2,1,0:T(8,128)S(1)} %collective-permute-done.6.swapped_ref, f32[2,1024,256]{2,1,0:T(8,128)S(1)} %copy-done, f32[2,1024]{1,0:T(2,128)S(1)} %copy-done.2), custom_call_target="tpu_custom_call" | custom-call | tf_op jit(solution)/shard_map/apply_update/pallas_call | solution.py:277
  (1 shorter events, 0.0 us)
Async XLA Ops:
  0.7 0.8 %copy-start.1 = (s32[2,8192]{1,0:T(2,128)S(1)}, s32[2,8192]{1,0:T(2,128)}, u32[]{:S(2)}) copy-start(s32[2,8192]{1,0:T(2,128)} %index_ref.1) | copy-start | bytes 196612
  8.1 16.4 %collective-permute-start.4 = (f32[512,256]{1,0:T(8,128)S(1)}, f32[512,256]{1,0:T(8,128)S(1)}, u32[]{:S(2)}, u32[]{:S(2)}) collective-permute-start(f32[512,256]{1,0:T(8,128)S(1)} %get-tuple-element.23), channel_id=1, source_target_pairs={{0,3},{1,0},{2,1},{3,2},{4,7},{5,4},{6,5},{7,6},{8,11},{9,8},{10,9... | collective-permute-start | bytes 1572872 | tf_op jit(solution)/shard_map/ppermute | solution.py:304
  12.7 14.6 %collective-permute-start.1 = (f32[512,256]{1,0:T(8,128)S(1)}, f32[512,256]{1,0:T(8,128)S(1)}, u32[]{:S(2)}, u32[]{:S(2)}) collective-permute-start(f32[512,256]{1,0:T(8,128)S(1)} %get-tuple-element.19), channel_id=1, source_target_pairs={{0,1},{1,2},{2,3},{3,0},{4,5},{5,6},{6,7},{7,4},{8,9},{9,10},{10,1... | collective-permute-start | bytes 1572872 | tf_op jit(solution)/shard_map/ppermute | solution.py:304
  17.2 14.9 %collective-permute-start = (f32[512,256]{1,0:T(8,128)S(1)}, f32[512,256]{1,0:T(8,128)S(1)}, u32[]{:S(2)}, u32[]{:S(2)}) collective-permute-start(f32[512,256]{1,0:T(8,128)S(1)} %get-tuple-element.17), channel_id=1, source_target_pairs={{0,3},{1,0},{2,1},{3,2},{4,7},{5,4},{6,5},{7,6},{8,11},{9,8},{10,9... | collective-permute-start | bytes 1572872 | tf_op jit(solution)/shard_map/ppermute | solution.py:304
  20.0 12.2 %collective-permute-start.3 = (f32[512,256]{1,0:T(8,128)S(1)}, f32[512,256]{1,0:T(8,128)S(1)}, u32[]{:S(2)}, u32[]{:S(2)}) collective-permute-start(f32[512,256]{1,0:T(8,128)S(1)} %get-tuple-element.21), channel_id=1, source_target_pairs={{0,1},{1,2},{2,3},{3,0},{4,5},{5,6},{6,7},{7,4},{8,9},{9,10},{10,1... | collective-permute-start | bytes 1572872 | tf_op jit(solution)/shard_map/ppermute | solution.py:304
  24.5 8.9 %collective-permute-start.5 = (f32[512,256]{1,0:T(8,128)S(1)}, f32[512,256]{1,0:T(8,128)S(1)}, u32[]{:S(2)}, u32[]{:S(2)}) collective-permute-start(f32[512,256]{1,0:T(8,128)S(1)} %add.7), channel_id=1, source_target_pairs={{0,3},{1,0},{2,1},{3,2},{4,7},{5,4},{6,5},{7,6},{8,11},{9,8},{10,9... | collective-permute-start | bytes 1572872 | tf_op jit(solution)/shard_map/ppermute | solution.py:304
  27.4 9.8 %copy-start.3 = (s32[2,128]{1,0:T(2,128)S(1)}, s32[2,128]{1,0:T(2,128)}, u32[]{:S(2)}) copy-start(s32[2,128]{1,0:T(2,128)} %unique_ref.1) | copy-start | bytes 3076
  27.4 9.8 %collective-permute-start.2 = (f32[512,256]{1,0:T(8,128)S(1)}, f32[512,256]{1,0:T(8,128)S(1)}, u32[]{:S(2)}, u32[]{:S(2)}) collective-permute-start(f32[512,256]{1,0:T(8,128)S(1)} %add.6), channel_id=1, source_target_pairs={{0,1},{1,2},{2,3},{3,0},{4,5},{5,6},{6,7},{7,4},{8,9},{9,10},{10,1... | collective-permute-start | bytes 1572872 | tf_op jit(solution)/shard_map/ppermute | solution.py:304
  37.9 25.4 %copy-start = (f32[2,1024,256]{2,1,0:T(8,128)S(1)}, f32[2,1024,256]{2,1,0:T(8,128)}, u32[]{:S(2)}) copy-start(f32[2,1024,256]{2,1,0:T(8,128)} %tables_ref.1) | copy-start | bytes 6291460
  37.9 25.4 %copy-start.2 = (f32[2,1024]{1,0:T(2,128)S(1)}, f32[2,1024]{1,0:T(2,128)}, u32[]{:S(2)}) copy-start(f32[2,1024]{1,0:T(2,128)} %accums_ref.1) | copy-start | bytes 24580
  57.4 5.9 %collective-permute-start.6 = (f32[4,72,128]{2,1,0:T(8,128)S(1)}, f32[4,72,128]{2,1,0:T(8,128)S(1)}, u32[]{:S(2)}, u32[]{:S(2)}) collective-permute-start(f32[4,72,128]{2,1,0:T(8,128)S(1)} %get-tuple-element.25), channel_id=1, source_target_pairs={{0,16},{16,0},{32,48},{48,32},{64,80},{80,64},{96,112},{112,96},{1... | collective-permute-start | bytes 442376 | tf_op jit(solution)/shard_map/ppermute | solution.py:328

commit v4 on v3

--- a/solution.py
+++ b/solution.py
@@ -15,7 +15,6 @@
 VMEM_BYTES = 16 << 20
 FIRST_BYTES = 48 << 20
 IN_VMEM = pl.BlockSpec(memory_space=pltpu.VMEM)
-IN_SMEM = pl.BlockSpec(memory_space=pltpu.SMEM)
 IN_HBM = pl.BlockSpec(memory_space=pltpu.HBM)
 
 
@@ -32,6 +31,14 @@
     return pairs
 
 
+def position():
+    group = lax.axis_index("group")
+    place = lax.axis_index("local")
+    z, x = lax.shift_right_logical(place, 2), place & (SIDE - 1)
+    even = group & (CORES - 1) == 0
+    return group, jnp.where(even, x, z), jnp.where(even, z, x), even
+
+
 def second_groups(n_group, n_local):
     groups = []
     for core in range(CORES):
@@ -81,13 +88,13 @@
             out_ref[...] += piece
 
 
-def first_sums(place, slot_index, lookup_grads, targets):
+def first_sums(slot_index, lookup_grads, targets):
     count, width = lookup_grads.shape
     rows = SIDE * LANES
     block = 1024
     blocks = count // block
 
-    def body(place_ref, index_ref, grads_hbm, *refs):
+    def body(index_ref, grads_hbm, *refs):
         out_refs = refs[: len(targets)]
         grads_ref, codes_ref, sems = refs[len(targets) :]
         copies = []
@@ -98,10 +105,11 @@
             )
         for copy in copies:
             copy.start()
+        _, own_first, _, even = position()
         index = index_ref[...]
-        first = lax.shift_right_logical(index, place_ref[2]) & (SIDE - 1)
-        second = lax.shift_right_logical(index, place_ref[3]) & (SIDE - 1)
-        first = (first - place_ref[0]) & (SIDE - 1)
+        first = lax.shift_right_logical(index, jnp.where(even, 7, 9)) & (SIDE - 1)
+        second = lax.shift_right_logical(index, jnp.where(even, 9, 7)) & (SIDE - 1)
+        first = (first - own_first) & (SIDE - 1)
         codes_ref[...] = first * rows + second * LANES + (index & (LANES - 1))
         for i in range(blocks):
             copies[i].wait()
@@ -116,13 +124,13 @@
             jax.ShapeDtypeStruct(lookup_grads.shape, lookup_grads.dtype),
             jax.ShapeDtypeStruct(slot_index.shape, jnp.int32),
         ],
-        [IN_SMEM, IN_VMEM, IN_HBM],
+        [IN_VMEM, IN_HBM],
         scratch=[
             pltpu.SemaphoreType.DMA((blocks,)),
         ],
         cost=kernel_cost(rows, count, width),
         vmem=FIRST_BYTES,
-    )(place, slot_index, lookup_grads)
+    )(slot_index, lookup_grads)
 
 
 def slot_sums(codes, lookup_grads, targets):
@@ -144,17 +152,18 @@
     )(codes, lookup_grads)
 
 
-def finish_first_ring(place, unique_rows, own0, back0, next0, own1, next1, back1):
+def finish_first_ring(unique_rows, own0, back0, next0, own1, next1, back1):
     rows, width = own0.shape
     chips = SIDE
     block = rows // SIDE // chips
     tiles = 2 * width // LANES
 
-    def body(place_ref, unique_ref, o0, b0, n0, o1, n1, b1, spread):
+    def body(unique_ref, o0, b0, n0, o1, n1, b1, spread):
+        own_second = position()[2]
         numbers = unique_ref[...].astype(jnp.float32) + 1.0
         numbers = jnp.concatenate([numbers, jnp.zeros((6, LANES), jnp.float32)], axis=0)
         for second in range(SIDE):
-            mine = jnp.where(place_ref[1] == second, numbers, 0.0)
+            mine = jnp.where(own_second == second, numbers, 0.0)
             for chip in range(chips):
                 member = chip * SIDE + second
                 piece = pl.ds((second * chips + chip) * block, block)
@@ -169,18 +178,18 @@
         body,
         "finish_first_ring",
         [f32(SIDE * chips, tiles * block + 8, LANES)],
-        [IN_SMEM] + [IN_VMEM] * 7,
-    )(place, unique_rows, own0, back0, next0, own1, next1, back1)[0]
-
-
-def finish_second_ring(place, spread):
+        [IN_VMEM] * 7,
+    )(unique_rows, own0, back0, next0, own1, next1, back1)[0]
+
+
+def finish_second_ring(spread):
     members, rows, lanes = spread.shape
     chips = members // SIDE
     half = LANES // 8
     tiles = (rows - 8) // (CORES * half)
 
-    def body(place_ref, spread_ref, kept, given):
-        core = place_ref[4] & 1
+    def body(spread_ref, kept, given):
+        even = position()[3]
 
         def total(chip, piece):
             pieces = [spread_ref[chip * SIDE + second, piece, :] for second in range(SIDE)]
@@ -191,15 +200,15 @@
                 low = total(chip, pl.ds(tile * CORES * half, half))
                 high = total(chip, pl.ds(tile * CORES * half + half, half))
                 spot = pl.ds(tile * half, half)
-                kept[chip, spot, :] = jnp.where(core == 0, low, high)
-                given[chip, spot, :] = jnp.where(core == 0, high, low)
+                kept[chip, spot, :] = jnp.where(even, low, high)
+                given[chip, spot, :] = jnp.where(even, high, low)
             numbers = total(chip, pl.ds(rows - 8, 8))
             kept[chip, pl.ds(tiles * half, 8), :] = numbers
             given[chip, pl.ds(tiles * half, 8), :] = numbers
 
     return call(
-        body, "finish_second_ring", [f32(chips, tiles * half + 8, lanes)] * 2, [IN_SMEM, IN_VMEM]
-    )(place, spread)
+        body, "finish_second_ring", [f32(chips, tiles * half + 8, lanes)] * 2, [IN_VMEM]
+    )(spread)
 
 
 def eye():
@@ -213,7 +222,7 @@
     return jnp.sum(square, axis=axis, keepdims=True)
 
 
-def apply_update(place, kept, swapped, tables, accums):
+def apply_update(kept, swapped, tables, accums):
     rows_dev, width = tables.shape[1:]
     rows = 256
     count = rows_dev // rows
@@ -223,12 +232,12 @@
     slots -= 8
     tiles = width // LANES
 
-    def body(place_ref, kept_ref, swapped_ref, tables_ref, accums_ref, *refs):
+    def body(kept_ref, swapped_ref, tables_ref, accums_ref, *refs):
         new_tables_hbm, new_accums_ref, done_ref, sems = refs
         diagonal = eye()
         copies = []
         sources = [(ref, chip) for ref in (kept_ref, swapped_ref) for chip in range(chips)]
-        group = place_ref[4]
+        group = position()[0]
         lane = lax.broadcasted_iota(jnp.int32, (8, LANES), 1) // bucket
         local_rows = jnp.zeros((8, LANES), jnp.int32)
         for spot, (ref, chip) in enumerate(sources):
@@ -278,32 +287,20 @@
         body,
         "apply_update",
         [f32(*tables.shape), f32(*accums.shape)],
-        [IN_SMEM] + [IN_VMEM] * 4,
+        [IN_VMEM] * 4,
         [IN_HBM, IN_VMEM],
         [pltpu.VMEM(tables.shape, jnp.float32), pltpu.SemaphoreType.DMA((2 * count,))],
-    )(place, kept, swapped, tables, accums)
+    )(kept, swapped, tables, accums)
 
 
 def local(lookup_grads, slot_index, unique_rows, tables, accums):
     n_group = lax.axis_size("group")
     n_local = lax.axis_size("local")
-    even = lax.axis_index("group") & 1 == 0
-    z = lax.shift_right_logical(lax.axis_index("local"), 2)
-    x = lax.axis_index("local") & (SIDE - 1)
-    place = jnp.stack(
-        [
-            jnp.where(even, x, z),
-            jnp.where(even, z, x),
-            jnp.where(even, 7, 9),
-            jnp.where(even, 9, 7),
-            lax.axis_index("group"),
-        ]
-    ).astype(jnp.int32)
 
     def send(value, step):
         return lax.ppermute(value, AXES, ring_pairs(n_group, n_local, step))
 
-    far0, far1, grads, codes = first_sums(place, slot_index, lookup_grads, [(0, 2), (1, 2)])
+    far0, far1, grads, codes = first_sums(slot_index, lookup_grads, [(0, 2), (1, 2)])
     far0 = send(far0, 1)
     far1 = send(far1, -1)
     back0, next1 = slot_sums(codes, grads, [(0, 3), (1, 1)])
@@ -314,7 +311,7 @@
     back1 = send(back1 + far1, -1)
     own0, own1 = slot_sums(codes, grads, [(0, 0), (1, 0)])
 
-    spread = finish_first_ring(place, unique_rows, own0, back0, next0, own1, next1, back1)
+    spread = finish_first_ring(unique_rows, own0, back0, next0, own1, next1, back1)
     spread = lax.all_to_all(
         spread,
         AXES,
@@ -323,10 +320,10 @@
         axis_index_groups=second_groups(n_group, n_local),
         tiled=True,
     )
-    kept, given = finish_second_ring(place, spread)
+    kept, given = finish_second_ring(spread)
 
     swapped = lax.ppermute(given, "group", [(i, i ^ 1) for i in range(n_group)])
-    new_tables, new_accums = apply_update(place, kept, swapped, tables, accums)
+    new_tables, new_accums = apply_update(kept, swapped, tables, accums)
     return (new_tables, new_accums)
 
 

time: 66.9 us -> 64.7 us (0.967)
  Pallas kernels: 24.5 us -> 22.4 us
  transfers between devices with their start and end apart: 7 -> 7, of which waited for: 3 -> 3; matrix products, arithmetic and copies ran while one was open for 0% -> 0% of each run, Pallas kernels for 20% -> 21%
where the time goes in v4:
time: 64.7 us; the launch traced here: 64.5 us
  Pallas kernels  22.4 us (35%)
  blocking collectives  18.9 us (29%)
  starting transfers between devices  15.3 us (24%)
  waiting for transfers between devices  6.04 us (9%)
  between operations  0.89 us (1%)
  local copies, waits for them, and re-layouts  0.85 us (1%)
    all_to_all x1, blocking collectives, local(): lax.all_to_all(spread, AXES, split_axis=0, concat_axis=0, axis_index_grou...  18.9 us
    pallas_call x3, Pallas kernels, slot_sums(): call(body, 'slot_sums', [f32(rows, width) for _ in targets], [IN_VMEM] *...  13.4 us
    ppermute x6, starting transfers between devices, send(): return lax.ppermute(value, AXES, ring_pairs(n_group, n_local, step))  10.4 us
    pallas_call x1, Pallas kernels, first_sums(): call(body, 'first_sums', [*[f32(rows, width) for _ in targets], jax.Shape...  5.96 us
    ppermute x6, waiting for transfers between devices, send(): return lax.ppermute(value, AXES, ring_pairs(n_group, n_local, step))  5.03 us
    ppermute x1, starting transfers between devices, local(): swapped = lax.ppermute(given, 'group', [(i, i ^ 1) for i in range(n_group)])  4.9 us
    pallas_call x1, Pallas kernels, apply_update(): call(body, 'apply_update', [f32(*tables.shape), f32(*accums.shape)], [IN_...  2.69 us
  transfers between devices with their start and end apart: 7, of which 3 were waited for; matrix products, arithmetic and copies ran while one was open for 0% of the time, Pallas kernels for 21%

profile of v4, /device:TPU:1, one launch (start us, length us, event | category | flops | bytes accessed | tf_op | source)
XLA Modules:
  0.0 64.5 jit_solution(1289804267666083104)
XLA Ops:
  0.6 0.0 copy-start.1
  0.6 0.8 %copy-done.1 = s32[2,8192]{1,0:T(2,128)S(1)} copy-done((s32[2,8192]{1,0:T(2,128)S(1)}, s32[2,8192]{1,0:T(2,128)}, u32[]{:S(2)}) %copy-start.1) | copy-done | bytes 65560
  1.5 6.0 %first_sums.1 = (f32[512,256]{1,0:T(8,128)S(1)}, f32[512,256]{1,0:T(8,128)S(1)}, bf16[8192,256]{1,0:T(8,128)(2,1)S(1)}, s32[2,8192]{1,0:T(2,128)S(1)}) custom-call(s32[2,8192]{1,0:T(2,128)S(1)} %copy-done.1, bf16[8192,256]{1,0:T(8,128)(2,1)} %grads_hbm.1), custom_call_target="tpu_custom_call" | custom-call | flops 429496736 | bytes 419430 | tf_op jit(solution)/shard_map/first_sums/pallas_call | solution.py:119
  7.4 4.7 %collective-permute-start.4 = (f32[512,256]{1,0:T(8,128)S(1)}, f32[512,256]{1,0:T(8,128)S(1)}, u32[]{:S(2)}, u32[]{:S(2)}) collective-permute-start(f32[512,256]{1,0:T(8,128)S(1)} %get-tuple-element.23), channel_id=1, source_target_pairs={{0,3},{1,0},{2,1},{3,2},{4,7},{5,4},{6,5},{7,6},{8,11},{9,8},{10,9... | collective-permute-start | bytes 1572872 | tf_op jit(solution)/shard_map/ppermute | solution.py:301
  12.1 0.0 collective-permute-start.1
  12.1 4.5 %slot_sums.4 = (f32[512,256]{1,0:T(8,128)S(1)}, f32[512,256]{1,0:T(8,128)S(1)}) custom-call(s32[2,8192]{1,0:T(2,128)S(1)} %get-tuple-element.14.codes_ref, bf16[8192,256]{1,0:T(8,128)(2,1)S(1)} %get-tuple-element.15.grads_ref), custom_call_target="tpu_custom_call" | custom-call | flops 429496736 | bytes 419430 | tf_op jit(solution)/shard_map/slot_sums/pallas_call | solution.py:146
  16.6 2.7 %collective-permute-start = (f32[512,256]{1,0:T(8,128)S(1)}, f32[512,256]{1,0:T(8,128)S(1)}, u32[]{:S(2)}, u32[]{:S(2)}) collective-permute-start(f32[512,256]{1,0:T(8,128)S(1)} %get-tuple-element.17), channel_id=1, source_target_pairs={{0,3},{1,0},{2,1},{3,2},{4,7},{5,4},{6,5},{7,6},{8,11},{9,8},{10,9... | collective-permute-start | bytes 1572872 | tf_op jit(solution)/shard_map/ppermute | solution.py:301
  19.3 0.0 collective-permute-start.3
  19.3 4.5 %slot_sums.5 = (f32[512,256]{1,0:T(8,128)S(1)}, f32[512,256]{1,0:T(8,128)S(1)}) custom-call(s32[2,8192]{1,0:T(2,128)S(1)} %get-tuple-element.14.codes_ref, bf16[8192,256]{1,0:T(8,128)(2,1)S(1)} %get-tuple-element.15.grads_ref), custom_call_target="tpu_custom_call" | custom-call | flops 429496736 | bytes 419430 | tf_op jit(solution)/shard_map/slot_sums/pallas_call | solution.py:146
  23.8 0.0 collective-permute-done.4
  23.8 0.1 add.7
  23.9 2.7 %collective-permute-start.5 = (f32[512,256]{1,0:T(8,128)S(1)}, f32[512,256]{1,0:T(8,128)S(1)}, u32[]{:S(2)}, u32[]{:S(2)}) collective-permute-start(f32[512,256]{1,0:T(8,128)S(1)} %add.7), channel_id=1, source_target_pairs={{0,3},{1,0},{2,1},{3,2},{4,7},{5,4},{6,5},{7,6},{8,11},{9,8},{10,9... | collective-permute-start | bytes 1572872 | tf_op jit(solution)/shard_map/ppermute | solution.py:301
  26.6 0.0 collective-permute-done.1
  26.6 0.1 add.6
  26.7 0.0 copy-start.3
  26.7 0.3 collective-permute-start.2
  27.0 4.5 %slot_sums.3 = (f32[512,256]{1,0:T(8,128)S(1)}, f32[512,256]{1,0:T(8,128)S(1)}) custom-call(s32[2,8192]{1,0:T(2,128)S(1)} %get-tuple-element.14.codes_ref, bf16[8192,256]{1,0:T(8,128)(2,1)S(1)} %get-tuple-element.15.grads_ref), custom_call_target="tpu_custom_call" | custom-call | flops 429496736 | bytes 419430 | tf_op jit(solution)/shard_map/slot_sums/pallas_call | solution.py:146
  31.5 0.0 collective-permute-done.b0
  31.5 0.0 collective-permute-done.3.n1
  31.5 1.3 %collective-permute-done.5.b1 = f32[512,256]{1,0:T(8,128)S(1)} collective-permute-done((f32[512,256]{1,0:T(8,128)S(1)}, f32[512,256]{1,0:T(8,128)S(1)}, u32[]{:S(2)}, u32[]{:S(2)}) %collective-permute-start.5) | collective-permute-done | bytes 524320 | tf_op jit(solution)/shard_map/ppermute | solution.py:301
  32.8 3.7 %collective-permute-done.2.n0 = f32[512,256]{1,0:T(8,128)S(1)} collective-permute-done((f32[512,256]{1,0:T(8,128)S(1)}, f32[512,256]{1,0:T(8,128)S(1)}, u32[]{:S(2)}, u32[]{:S(2)}) %collective-permute-start.2) | collective-permute-done | bytes 524320 | tf_op jit(solution)/shard_map/ppermute | solution.py:301
  36.5 0.0 copy-done.3
  36.5 0.2 finish_first_ring.1
  36.7 0.0 copy-start
  36.7 0.0 copy-start.2
  36.7 18.9 %all_to_all.5.spread_ref = f32[16,136,128]{2,1,0:T(8,128)S(1)} all-to-all(f32[16,136,128]{2,1,0:T(8,128)S(1)} %finish_first_ring.1), channel_id=1, replica_groups={{0,4,8,12,32,36,40,44,64,68,72,76,96,100,104,108},{1,5,9,13,33,37,41,45..., dimensions={0} | all-to-all | bytes 2228224 | tf_op jit(solution)/shard_map/all_to_all | solution.py:315
  55.6 0.1 finish_second_ring.1
  55.7 4.9 %collective-permute-start.6 = (f32[4,72,128]{2,1,0:T(8,128)S(1)}, f32[4,72,128]{2,1,0:T(8,128)S(1)}, u32[]{:S(2)}, u32[]{:S(2)}) collective-permute-start(f32[4,72,128]{2,1,0:T(8,128)S(1)} %get-tuple-element.25), channel_id=1, source_target_pairs={{0,16},{16,0},{32,48},{48,32},{64,80},{80,64},{96,112},{112,96},{1... | collective-permute-start | bytes 442376 | tf_op jit(solution)/shard_map/ppermute | solution.py:325
  60.6 1.0 %collective-permute-done.6.swapped_ref = f32[4,72,128]{2,1,0:T(8,128)S(1)} collective-permute-done((f32[4,72,128]{2,1,0:T(8,128)S(1)}, f32[4,72,128]{2,1,0:T(8,128)S(1)}, u32[]{:S(2)}, u32[]{:S(2)}) %collective-permute-start.6) | collective-permute-done | bytes 147488 | tf_op jit(solution)/shard_map/ppermute | solution.py:325
  61.6 0.0 copy-done
  61.6 0.0 copy-done.2
  61.6 2.7 %apply_update.1 = (f32[2,1024,256]{2,1,0:T(8,128)}, f32[2,1024]{1,0:T(2,128)}) custom-call(f32[4,72,128]{2,1,0:T(8,128)S(1)} %get-tuple-element.24.kept_ref, f32[4,72,128]{2,1,0:T(8,128)S(1)} %collective-permute-done.6.swapped_ref, f32[2,1024,256]{2,1,0:T(8,128)S(1)} %copy-done, f32[2,1024]{1,0:T(2,128)S(1)} %copy-done.2), custom_call_target="tpu_custom_call" | custom-call | tf_op jit(solution)/shard_map/apply_update/pallas_call | solution.py:286
Async XLA Ops:
  0.6 0.8 %copy-start.1 = (s32[2,8192]{1,0:T(2,128)S(1)}, s32[2,8192]{1,0:T(2,128)}, u32[]{:S(2)}) copy-start(s32[2,8192]{1,0:T(2,128)} %index_ref.1) | copy-start | bytes 196612
  7.4 16.4 %collective-permute-start.4 = (f32[512,256]{1,0:T(8,128)S(1)}, f32[512,256]{1,0:T(8,128)S(1)}, u32[]{:S(2)}, u32[]{:S(2)}) collective-permute-start(f32[512,256]{1,0:T(8,128)S(1)} %get-tuple-element.23), channel_id=1, source_target_pairs={{0,3},{1,0},{2,1},{3,2},{4,7},{5,4},{6,5},{7,6},{8,11},{9,8},{10,9... | collective-permute-start | bytes 1572872 | tf_op jit(solution)/shard_map/ppermute | solution.py:301
  12.1 14.5 %collective-permute-start.1 = (f32[512,256]{1,0:T(8,128)S(1)}, f32[512,256]{1,0:T(8,128)S(1)}, u32[]{:S(2)}, u32[]{:S(2)}) collective-permute-start(f32[512,256]{1,0:T(8,128)S(1)} %get-tuple-element.19), channel_id=1, source_target_pairs={{0,1},{1,2},{2,3},{3,0},{4,5},{5,6},{6,7},{7,4},{8,9},{9,10},{10,1... | collective-permute-start | bytes 1572872 | tf_op jit(solution)/shard_map/ppermute | solution.py:301
  16.6 14.9 %collective-permute-start = (f32[512,256]{1,0:T(8,128)S(1)}, f32[512,256]{1,0:T(8,128)S(1)}, u32[]{:S(2)}, u32[]{:S(2)}) collective-permute-start(f32[512,256]{1,0:T(8,128)S(1)} %get-tuple-element.17), channel_id=1, source_target_pairs={{0,3},{1,0},{2,1},{3,2},{4,7},{5,4},{6,5},{7,6},{8,11},{9,8},{10,9... | collective-permute-start | bytes 1572872 | tf_op jit(solution)/shard_map/ppermute | solution.py:301
  19.3 12.2 %collective-permute-start.3 = (f32[512,256]{1,0:T(8,128)S(1)}, f32[512,256]{1,0:T(8,128)S(1)}, u32[]{:S(2)}, u32[]{:S(2)}) collective-permute-start(f32[512,256]{1,0:T(8,128)S(1)} %get-tuple-element.21), channel_id=1, source_target_pairs={{0,1},{1,2},{2,3},{3,0},{4,5},{5,6},{6,7},{7,4},{8,9},{9,10},{10,1... | collective-permute-start | bytes 1572872 | tf_op jit(solution)/shard_map/ppermute | solution.py:301
  23.9 8.9 %collective-permute-start.5 = (f32[512,256]{1,0:T(8,128)S(1)}, f32[512,256]{1,0:T(8,128)S(1)}, u32[]{:S(2)}, u32[]{:S(2)}) collective-permute-start(f32[512,256]{1,0:T(8,128)S(1)} %add.7), channel_id=1, source_target_pairs={{0,3},{1,0},{2,1},{3,2},{4,7},{5,4},{6,5},{7,6},{8,11},{9,8},{10,9... | collective-permute-start | bytes 1572872 | tf_op jit(solution)/shard_map/ppermute | solution.py:301
  26.7 9.8 %copy-start.3 = (s32[2,128]{1,0:T(2,128)S(1)}, s32[2,128]{1,0:T(2,128)}, u32[]{:S(2)}) copy-start(s32[2,128]{1,0:T(2,128)} %unique_ref.1) | copy-start | bytes 3076
  26.7 9.8 %collective-permute-start.2 = (f32[512,256]{1,0:T(8,128)S(1)}, f32[512,256]{1,0:T(8,128)S(1)}, u32[]{:S(2)}, u32[]{:S(2)}) collective-permute-start(f32[512,256]{1,0:T(8,128)S(1)} %add.6), channel_id=1, source_target_pairs={{0,1},{1,2},{2,3},{3,0},{4,5},{5,6},{6,7},{7,4},{8,9},{9,10},{10,1... | collective-permute-start | bytes 1572872 | tf_op jit(solution)/shard_map/ppermute | solution.py:301
  36.7 24.9 %copy-start = (f32[2,1024,256]{2,1,0:T(8,128)S(1)}, f32[2,1024,256]{2,1,0:T(8,128)}, u32[]{:S(2)}) copy-start(f32[2,1024,256]{2,1,0:T(8,128)} %tables_ref.1) | copy-start | bytes 6291460
  36.7 24.9 %copy-start.2 = (f32[2,1024]{1,0:T(2,128)S(1)}, f32[2,1024]{1,0:T(2,128)}, u32[]{:S(2)}) copy-start(f32[2,1024]{1,0:T(2,128)} %accums_ref.1) | copy-start | bytes 24580
  55.7 5.9 %collective-permute-start.6 = (f32[4,72,128]{2,1,0:T(8,128)S(1)}, f32[4,72,128]{2,1,0:T(8,128)S(1)}, u32[]{:S(2)}, u32[]{:S(2)}) collective-permute-start(f32[4,72,128]{2,1,0:T(8,128)S(1)} %get-tuple-element.25), channel_id=1, source_target_pairs={{0,16},{16,0},{32,48},{48,32},{64,80},{80,64},{96,112},{112,96},{1... | collective-permute-start | bytes 442376 | tf_op jit(solution)/shard_map/ppermute | solution.py:325

commit v5 on v4

--- a/solution.py
+++ b/solution.py
@@ -13,7 +13,8 @@
 CORES = 2
 LANES = 128
 VMEM_BYTES = 16 << 20
-FIRST_BYTES = 48 << 20
+FIRST_BLOCKS = (1024, 3072, 4096)
+BLOCK = 1024
 IN_VMEM = pl.BlockSpec(memory_space=pltpu.VMEM)
 IN_HBM = pl.BlockSpec(memory_space=pltpu.HBM)
 
@@ -52,14 +53,14 @@
     return groups
 
 
-def call(body, name, out_shape, in_specs, out_specs=None, scratch=(), cost=None, vmem=VMEM_BYTES):
+def call(body, name, out_shape, in_specs, out_specs=None, scratch=(), cost=None):
     return pl.pallas_call(
         body,
         out_shape=out_shape,
         in_specs=in_specs,
         out_specs=[IN_VMEM] * len(out_shape) if out_specs is None else out_specs,
         scratch_shapes=scratch,
-        compiler_params=pltpu.CompilerParams(vmem_limit_bytes=vmem),
+        compiler_params=pltpu.CompilerParams(vmem_limit_bytes=VMEM_BYTES),
         cost_estimate=cost,
         name=name,
     )
@@ -91,29 +92,30 @@
 def first_sums(slot_index, lookup_grads, targets):
     count, width = lookup_grads.shape
     rows = SIDE * LANES
-    block = 1024
-    blocks = count // block
-
-    def body(index_ref, grads_hbm, *refs):
+    blocks = len(FIRST_BLOCKS)
+    pieces = [pl.ds(sum(FIRST_BLOCKS[:i]), FIRST_BLOCKS[i]) for i in range(blocks)]
+
+    def body(index_hbm, grads_hbm, *refs):
         out_refs = refs[: len(targets)]
-        grads_ref, codes_ref, sems = refs[len(targets) :]
+        grads_ref, codes_ref, index_ref, sems = refs[len(targets) :]
+        index_copy = pltpu.make_async_copy(index_hbm, index_ref, sems.at[blocks])
+        index_copy.start()
         copies = []
-        for i in range(blocks):
-            piece = pl.ds(i * block, block)
+        for i, piece in enumerate(pieces):
             copies.append(
                 pltpu.make_async_copy(grads_hbm.at[piece], grads_ref.at[piece], sems.at[i])
             )
         for copy in copies:
             copy.start()
         _, own_first, _, even = position()
+        index_copy.wait()
         index = index_ref[...]
         first = lax.shift_right_logical(index, jnp.where(even, 7, 9)) & (SIDE - 1)
         second = lax.shift_right_logical(index, jnp.where(even, 9, 7)) & (SIDE - 1)
         first = (first - own_first) & (SIDE - 1)
         codes_ref[...] = first * rows + second * LANES + (index & (LANES - 1))
-        for i in range(blocks):
+        for i, piece in enumerate(pieces):
             copies[i].wait()
-            piece = pl.ds(i * block, block)
             add_block(codes_ref[:, piece], grads_ref[piece, :], targets, i, out_refs)
 
     return call(
@@ -124,19 +126,22 @@
             jax.ShapeDtypeStruct(lookup_grads.shape, lookup_grads.dtype),
             jax.ShapeDtypeStruct(slot_index.shape, jnp.int32),
         ],
-        [IN_VMEM, IN_HBM],
+        [IN_HBM, IN_HBM],
         scratch=[
-            pltpu.SemaphoreType.DMA((blocks,)),
+            pltpu.VMEM(slot_index.shape, jnp.int32),
+            pltpu.SemaphoreType.DMA((blocks + 1,)),
         ],
         cost=kernel_cost(rows, count, width),
-        vmem=FIRST_BYTES,
-    )(slot_index, lookup_grads)
+    )(
+        pltpu.with_memory_space_constraint(slot_index, pltpu.HBM),
+        pltpu.with_memory_space_constraint(lookup_grads, pltpu.HBM),
+    )
 
 
 def slot_sums(codes, lookup_grads, targets):
     count, width = lookup_grads.shape
     rows = SIDE * LANES
-    block = 1024
+    block = BLOCK
 
     def body(codes_ref, grads_ref, *out_refs):
         for start in range(0, count, block):

time: 64.7 us -> 63.5 us (0.981)
  local copies, waits for them, and re-layouts: 0.85 us -> 0.02 us
    unnamed x8 -> x6, local copies, waits for them, and re-layouts: 0.85 us -> 0.02 us
where the time goes in v5:
time: 63.5 us; the launch traced here: 63.4 us
  Pallas kernels  22.1 us (35%)
  blocking collectives  18.9 us (30%)
  starting transfers between devices  15.3 us (24%)
  waiting for transfers between devices  6.04 us (10%)
  between operations  0.88 us (1%)
    all_to_all x1, blocking collectives, local(): lax.all_to_all(spread, AXES, split_axis=0, concat_axis=0, axis_index_grou...  18.9 us
    pallas_call x3, Pallas kernels, slot_sums(): call(body, 'slot_sums', [f32(rows, width) for _ in targets], [IN_VMEM] *...  13.4 us
    ppermute x6, starting transfers between devices, send(): return lax.ppermute(value, AXES, ring_pairs(n_group, n_local, step))  10.4 us
    pallas_call x1, Pallas kernels, first_sums(): call(body, 'first_sums', [*[f32(rows, width) for _ in targets], jax.Shape...  5.7 us
    ppermute x6, waiting for transfers between devices, send(): return lax.ppermute(value, AXES, ring_pairs(n_group, n_local, step))  5.04 us
    ppermute x1, starting transfers between devices, local(): swapped = lax.ppermute(given, 'group', [(i, i ^ 1) for i in range(n_group)])  4.9 us
    pallas_call x1, Pallas kernels, apply_update(): call(body, 'apply_update', [f32(*tables.shape), f32(*accums.shape)], [IN_...  2.69 us
  transfers between devices with their start and end apart: 7, of which 3 were waited for; matrix products, arithmetic and copies ran while one was open for 0% of the time, Pallas kernels for 21%

profile of v5, /device:TPU:1, one launch (start us, length us, event | category | flops | bytes accessed | tf_op | source)
XLA Modules:
  0.0 63.4 jit_solution(6807025281918505525)
XLA Ops:
  0.6 5.7 %first_sums.1 = (f32[512,256]{1,0:T(8,128)S(1)}, f32[512,256]{1,0:T(8,128)S(1)}, bf16[8192,256]{1,0:T(8,128)(2,1)S(1)}, s32[2,8192]{1,0:T(2,128)S(1)}) custom-call(s32[2,8192]{1,0:T(2,128)} %index_hbm.1, bf16[8192,256]{1,0:T(8,128)(2,1)} %grads_hbm.1), custom_call_target="tpu_custom_call" | custom-call | flops 429496736 | bytes 419430 | tf_op jit(solution)/shard_map/first_sums/pallas_call | solution.py:121
  6.3 4.7 %collective-permute-start.4 = (f32[512,256]{1,0:T(8,128)S(1)}, f32[512,256]{1,0:T(8,128)S(1)}, u32[]{:S(2)}, u32[]{:S(2)}) collective-permute-start(f32[512,256]{1,0:T(8,128)S(1)} %get-tuple-element.23), channel_id=1, source_target_pairs={{0,3},{1,0},{2,1},{3,2},{4,7},{5,4},{6,5},{7,6},{8,11},{9,8},{10,9... | collective-permute-start | bytes 1572872 | tf_op jit(solution)/shard_map/ppermute | solution.py:306
  11.0 0.0 collective-permute-start.1
  11.0 4.5 %slot_sums.4 = (f32[512,256]{1,0:T(8,128)S(1)}, f32[512,256]{1,0:T(8,128)S(1)}) custom-call(s32[2,8192]{1,0:T(2,128)S(1)} %get-tuple-element.14.codes_ref, bf16[8192,256]{1,0:T(8,128)(2,1)S(1)} %get-tuple-element.15.grads_ref), custom_call_target="tpu_custom_call" | custom-call | flops 429496736 | bytes 419430 | tf_op jit(solution)/shard_map/slot_sums/pallas_call | solution.py:151
  15.5 2.7 %collective-permute-start = (f32[512,256]{1,0:T(8,128)S(1)}, f32[512,256]{1,0:T(8,128)S(1)}, u32[]{:S(2)}, u32[]{:S(2)}) collective-permute-start(f32[512,256]{1,0:T(8,128)S(1)} %get-tuple-element.17), channel_id=1, source_target_pairs={{0,3},{1,0},{2,1},{3,2},{4,7},{5,4},{6,5},{7,6},{8,11},{9,8},{10,9... | collective-permute-start | bytes 1572872 | tf_op jit(solution)/shard_map/ppermute | solution.py:306
  18.2 0.0 collective-permute-start.3
  18.2 4.5 %slot_sums.5 = (f32[512,256]{1,0:T(8,128)S(1)}, f32[512,256]{1,0:T(8,128)S(1)}) custom-call(s32[2,8192]{1,0:T(2,128)S(1)} %get-tuple-element.14.codes_ref, bf16[8192,256]{1,0:T(8,128)(2,1)S(1)} %get-tuple-element.15.grads_ref), custom_call_target="tpu_custom_call" | custom-call | flops 429496736 | bytes 419430 | tf_op jit(solution)/shard_map/slot_sums/pallas_call | solution.py:151
  22.7 0.0 collective-permute-done.4
  22.7 0.1 add.7
  22.8 2.7 %collective-permute-start.5 = (f32[512,256]{1,0:T(8,128)S(1)}, f32[512,256]{1,0:T(8,128)S(1)}, u32[]{:S(2)}, u32[]{:S(2)}) collective-permute-start(f32[512,256]{1,0:T(8,128)S(1)} %add.7), channel_id=1, source_target_pairs={{0,3},{1,0},{2,1},{3,2},{4,7},{5,4},{6,5},{7,6},{8,11},{9,8},{10,9... | collective-permute-start | bytes 1572872 | tf_op jit(solution)/shard_map/ppermute | solution.py:306
  25.5 0.0 collective-permute-done.1
  25.5 0.1 add.6
  25.6 0.0 copy-start.2
  25.6 0.3 collective-permute-start.2
  25.9 4.5 %slot_sums.3 = (f32[512,256]{1,0:T(8,128)S(1)}, f32[512,256]{1,0:T(8,128)S(1)}) custom-call(s32[2,8192]{1,0:T(2,128)S(1)} %get-tuple-element.14.codes_ref, bf16[8192,256]{1,0:T(8,128)(2,1)S(1)} %get-tuple-element.15.grads_ref), custom_call_target="tpu_custom_call" | custom-call | flops 429496736 | bytes 419430 | tf_op jit(solution)/shard_map/slot_sums/pallas_call | solution.py:151
  30.4 0.0 collective-permute-done.b0
  30.4 0.0 collective-permute-done.3.n1
  30.4 1.3 %collective-permute-done.5.b1 = f32[512,256]{1,0:T(8,128)S(1)} collective-permute-done((f32[512,256]{1,0:T(8,128)S(1)}, f32[512,256]{1,0:T(8,128)S(1)}, u32[]{:S(2)}, u32[]{:S(2)}) %collective-permute-start.5) | collective-permute-done | bytes 524320 | tf_op jit(solution)/shard_map/ppermute | solution.py:306
  31.7 3.7 %collective-permute-done.2.n0 = f32[512,256]{1,0:T(8,128)S(1)} collective-permute-done((f32[512,256]{1,0:T(8,128)S(1)}, f32[512,256]{1,0:T(8,128)S(1)}, u32[]{:S(2)}, u32[]{:S(2)}) %collective-permute-start.2) | collective-permute-done | bytes 524320 | tf_op jit(solution)/shard_map/ppermute | solution.py:306
  35.4 0.0 copy-done.2
  35.4 0.2 finish_first_ring.1
  35.6 0.0 copy-start
  35.6 0.0 copy-start.1
  35.7 18.9 %all_to_all.5.spread_ref = f32[16,136,128]{2,1,0:T(8,128)S(1)} all-to-all(f32[16,136,128]{2,1,0:T(8,128)S(1)} %finish_first_ring.1), channel_id=1, replica_groups={{0,4,8,12,32,36,40,44,64,68,72,76,96,100,104,108},{1,5,9,13,33,37,41,45..., dimensions={0} | all-to-all | bytes 2228224 | tf_op jit(solution)/shard_map/all_to_all | solution.py:320
  54.5 0.1 finish_second_ring.1
  54.6 4.9 %collective-permute-start.6 = (f32[4,72,128]{2,1,0:T(8,128)S(1)}, f32[4,72,128]{2,1,0:T(8,128)S(1)}, u32[]{:S(2)}, u32[]{:S(2)}) collective-permute-start(f32[4,72,128]{2,1,0:T(8,128)S(1)} %get-tuple-element.25), channel_id=1, source_target_pairs={{0,16},{16,0},{32,48},{48,32},{64,80},{80,64},{96,112},{112,96},{1... | collective-permute-start | bytes 442376 | tf_op jit(solution)/shard_map/ppermute | solution.py:330
  59.5 1.0 %collective-permute-done.6.swapped_ref = f32[4,72,128]{2,1,0:T(8,128)S(1)} collective-permute-done((f32[4,72,128]{2,1,0:T(8,128)S(1)}, f32[4,72,128]{2,1,0:T(8,128)S(1)}, u32[]{:S(2)}, u32[]{:S(2)}) %collective-permute-start.6) | collective-permute-done | bytes 147488 | tf_op jit(solution)/shard_map/ppermute | solution.py:330
  60.5 0.0 copy-done
  60.5 0.0 copy-done.1
  60.5 2.7 %apply_update.1 = (f32[2,1024,256]{2,1,0:T(8,128)}, f32[2,1024]{1,0:T(2,128)}) custom-call(f32[4,72,128]{2,1,0:T(8,128)S(1)} %get-tuple-element.24.kept_ref, f32[4,72,128]{2,1,0:T(8,128)S(1)} %collective-permute-done.6.swapped_ref, f32[2,1024,256]{2,1,0:T(8,128)S(1)} %copy-done, f32[2,1024]{1,0:T(2,128)S(1)} %copy-done.1), custom_call_target="tpu_custom_call" | custom-call | tf_op jit(solution)/shard_map/apply_update/pallas_call | solution.py:291
Async XLA Ops:
  6.3 16.4 %collective-permute-start.4 = (f32[512,256]{1,0:T(8,128)S(1)}, f32[512,256]{1,0:T(8,128)S(1)}, u32[]{:S(2)}, u32[]{:S(2)}) collective-permute-start(f32[512,256]{1,0:T(8,128)S(1)} %get-tuple-element.23), channel_id=1, source_target_pairs={{0,3},{1,0},{2,1},{3,2},{4,7},{5,4},{6,5},{7,6},{8,11},{9,8},{10,9... | collective-permute-start | bytes 1572872 | tf_op jit(solution)/shard_map/ppermute | solution.py:306
  11.0 14.5 %collective-permute-start.1 = (f32[512,256]{1,0:T(8,128)S(1)}, f32[512,256]{1,0:T(8,128)S(1)}, u32[]{:S(2)}, u32[]{:S(2)}) collective-permute-start(f32[512,256]{1,0:T(8,128)S(1)} %get-tuple-element.19), channel_id=1, source_target_pairs={{0,1},{1,2},{2,3},{3,0},{4,5},{5,6},{6,7},{7,4},{8,9},{9,10},{10,1... | collective-permute-start | bytes 1572872 | tf_op jit(solution)/shard_map/ppermute | solution.py:306
  15.5 14.9 %collective-permute-start = (f32[512,256]{1,0:T(8,128)S(1)}, f32[512,256]{1,0:T(8,128)S(1)}, u32[]{:S(2)}, u32[]{:S(2)}) collective-permute-start(f32[512,256]{1,0:T(8,128)S(1)} %get-tuple-element.17), channel_id=1, source_target_pairs={{0,3},{1,0},{2,1},{3,2},{4,7},{5,4},{6,5},{7,6},{8,11},{9,8},{10,9... | collective-permute-start | bytes 1572872 | tf_op jit(solution)/shard_map/ppermute | solution.py:306
  18.2 12.2 %collective-permute-start.3 = (f32[512,256]{1,0:T(8,128)S(1)}, f32[512,256]{1,0:T(8,128)S(1)}, u32[]{:S(2)}, u32[]{:S(2)}) collective-permute-start(f32[512,256]{1,0:T(8,128)S(1)} %get-tuple-element.21), channel_id=1, source_target_pairs={{0,1},{1,2},{2,3},{3,0},{4,5},{5,6},{6,7},{7,4},{8,9},{9,10},{10,1... | collective-permute-start | bytes 1572872 | tf_op jit(solution)/shard_map/ppermute | solution.py:306
  22.8 8.9 %collective-permute-start.5 = (f32[512,256]{1,0:T(8,128)S(1)}, f32[512,256]{1,0:T(8,128)S(1)}, u32[]{:S(2)}, u32[]{:S(2)}) collective-permute-start(f32[512,256]{1,0:T(8,128)S(1)} %add.7), channel_id=1, source_target_pairs={{0,3},{1,0},{2,1},{3,2},{4,7},{5,4},{6,5},{7,6},{8,11},{9,8},{10,9... | collective-permute-start | bytes 1572872 | tf_op jit(solution)/shard_map/ppermute | solution.py:306
  25.6 9.8 %copy-start.2 = (s32[2,128]{1,0:T(2,128)S(1)}, s32[2,128]{1,0:T(2,128)}, u32[]{:S(2)}) copy-start(s32[2,128]{1,0:T(2,128)} %unique_ref.1) | copy-start | bytes 3076
  25.6 9.8 %collective-permute-start.2 = (f32[512,256]{1,0:T(8,128)S(1)}, f32[512,256]{1,0:T(8,128)S(1)}, u32[]{:S(2)}, u32[]{:S(2)}) collective-permute-start(f32[512,256]{1,0:T(8,128)S(1)} %add.6), channel_id=1, source_target_pairs={{0,1},{1,2},{2,3},{3,0},{4,5},{5,6},{6,7},{7,4},{8,9},{9,10},{10,1... | collective-permute-start | bytes 1572872 | tf_op jit(solution)/shard_map/ppermute | solution.py:306
  35.6 24.9 %copy-start = (f32[2,1024,256]{2,1,0:T(8,128)S(1)}, f32[2,1024,256]{2,1,0:T(8,128)}, u32[]{:S(2)}) copy-start(f32[2,1024,256]{2,1,0:T(8,128)} %tables_ref.1) | copy-start | bytes 6291460
  35.6 24.9 %copy-start.1 = (f32[2,1024]{1,0:T(2,128)S(1)}, f32[2,1024]{1,0:T(2,128)}, u32[]{:S(2)}) copy-start(f32[2,1024]{1,0:T(2,128)} %accums_ref.1) | copy-start | bytes 24580
  54.6 5.9 %collective-permute-start.6 = (f32[4,72,128]{2,1,0:T(8,128)S(1)}, f32[4,72,128]{2,1,0:T(8,128)S(1)}, u32[]{:S(2)}, u32[]{:S(2)}) collective-permute-start(f32[4,72,128]{2,1,0:T(8,128)S(1)} %get-tuple-element.25), channel_id=1, source_target_pairs={{0,16},{16,0},{32,48},{48,32},{64,80},{80,64},{96,112},{112,96},{1... | collective-permute-start | bytes 442376 | tf_op jit(solution)/shard_map/ppermute | solution.py:330

commit v6 on v5

--- a/solution.py
+++ b/solution.py
@@ -19,12 +19,12 @@
 IN_HBM = pl.BlockSpec(memory_space=pltpu.HBM)
 
 
-def ring_pairs(n_group, n_local, step):
+def ring_pairs(n_group, n_local, ring, step):
     pairs = []
     for group in range(n_group):
         for place in range(n_local):
             z, x = divmod(place, SIDE)
-            if group % CORES == 0:
+            if (group + ring) % CORES == 0:
                 x = (x + step) % SIDE
             else:
                 z = (z + step) % SIDE
@@ -38,19 +38,6 @@
     z, x = lax.shift_right_logical(place, 2), place & (SIDE - 1)
     even = group & (CORES - 1) == 0
     return group, jnp.where(even, x, z), jnp.where(even, z, x), even
-
-
-def second_groups(n_group, n_local):
-    groups = []
-    for core in range(CORES):
-        for first in range(SIDE):
-            members = []
-            for chip in range(n_group // CORES):
-                for second in range(SIDE):
-                    z, x = (second, first) if core == 0 else (first, second)
-                    members.append((chip * CORES + core) * n_local + z * SIDE + x)
-            groups.append(members)
-    return groups
 
 
 def call(body, name, out_shape, in_specs, out_specs=None, scratch=(), cost=None):
@@ -107,12 +94,13 @@
             )
         for copy in copies:
             copy.start()
-        _, own_first, _, even = position()
+        _, own_first, own_second, even = position()
         index_copy.wait()
         index = index_ref[...]
         first = lax.shift_right_logical(index, jnp.where(even, 7, 9)) & (SIDE - 1)
         second = lax.shift_right_logical(index, jnp.where(even, 9, 7)) & (SIDE - 1)
         first = (first - own_first) & (SIDE - 1)
+        second = (second - own_second) & (SIDE - 1)
         codes_ref[...] = first * rows + second * LANES + (index & (LANES - 1))
         for i, piece in enumerate(pieces):
             copies[i].wait()
@@ -138,12 +126,12 @@
     )
 
 
-def slot_sums(codes, lookup_grads, targets):
+def slot_sums(codes, lookup_grads, targets, after):
     count, width = lookup_grads.shape
     rows = SIDE * LANES
     block = BLOCK
 
-    def body(codes_ref, grads_ref, *out_refs):
+    def body(codes_ref, grads_ref, after_ref, *out_refs):
         for start in range(0, count, block):
             piece = pl.ds(start, block)
             add_block(codes_ref[:, piece], grads_ref[piece, :], targets, start, out_refs)
@@ -152,68 +140,52 @@
         body,
         "slot_sums",
         [f32(rows, width) for _ in targets],
-        [IN_VMEM] * 2,
+        [IN_VMEM] * 3,
         cost=kernel_cost(rows, count, width),
-    )(codes, lookup_grads)
-
-
-def finish_first_ring(unique_rows, own0, back0, next0, own1, next1, back1):
+    )(codes, lookup_grads, after)
+
+
+def finish_first_ring(token, own0, back0, next0, own1, next1, back1):
     rows, width = own0.shape
+    slots = rows // SIDE
+
+    def body(token_ref, o0, b0, n0, o1, n1, b1, *out_refs):
+        for offset in range(SIDE):
+            piece = pl.ds(offset * slots, slots)
+            for table, refs in enumerate([(o0, b0, n0), (o1, n1, b1)]):
+                total = refs[0][piece, :] + refs[1][piece, :] + refs[2][piece, :]
+                out_refs[offset][pl.ds(table * slots, slots), :] = total
+
+    return call(body, "finish_first_ring", [f32(2 * slots, width)] * SIDE, [IN_VMEM] * 7)(
+        token, own0, back0, next0, own1, next1, back1
+    )
+
+
+def finish_second_ring(unique_rows, pieces):
+    rows, width = pieces[0].shape
+    slots = rows // 2
     chips = SIDE
-    block = rows // SIDE // chips
-    tiles = 2 * width // LANES
-
-    def body(unique_ref, o0, b0, n0, o1, n1, b1, spread):
-        own_second = position()[2]
+    bucket = slots // (CORES * chips)
+    height = 2 * bucket + 8
+
+    def body(unique_ref, p0, p1, p2, p3, kept, given):
+        group = position()[0]
+        core = group & (CORES - 1)
         numbers = unique_ref[...].astype(jnp.float32) + 1.0
-        numbers = jnp.concatenate([numbers, jnp.zeros((6, LANES), jnp.float32)], axis=0)
-        for second in range(SIDE):
-            mine = jnp.where(own_second == second, numbers, 0.0)
-            for chip in range(chips):
-                member = chip * SIDE + second
-                piece = pl.ds((second * chips + chip) * block, block)
-                for table, refs in enumerate([(o0, b0, n0), (o1, n1, b1)]):
-                    total = refs[0][piece, :] + refs[1][piece, :] + refs[2][piece, :]
-                    for tile in range(tiles // 2):
-                        spot = pl.ds((table * (tiles // 2) + tile) * block, block)
-                        spread[member, spot, :] = total[:, tile * LANES : (tile + 1) * LANES]
-                spread[member, pl.ds(tiles * block, 8), :] = mine
+        for offset in range(chips):
+            chip = (lax.shift_right_logical(group, 1) + offset) & (chips - 1)
+            for out_ref, owner in [(kept, core), (given, 1 - core)]:
+                for table in range(2):
+                    start = table * slots + (chip * CORES + owner) * bucket
+                    piece = pl.ds(pl.multiple_of(start, bucket), bucket)
+                    total = (p0[piece, :] + p1[piece, :]) + (p2[piece, :] + p3[piece, :])
+                    out_ref[offset, pl.ds(table * bucket, bucket), :] = total
+                out_ref[offset, pl.ds(2 * bucket, 8), :] = jnp.zeros((8, width), jnp.float32)
+                out_ref[offset, pl.ds(2 * bucket, 2), pl.ds(0, LANES)] = numbers
 
     return call(
-        body,
-        "finish_first_ring",
-        [f32(SIDE * chips, tiles * block + 8, LANES)],
-        [IN_VMEM] * 7,
-    )(unique_rows, own0, back0, next0, own1, next1, back1)[0]
-
-
-def finish_second_ring(spread):
-    members, rows, lanes = spread.shape
-    chips = members // SIDE
-    half = LANES // 8
-    tiles = (rows - 8) // (CORES * half)
-
-    def body(spread_ref, kept, given):
-        even = position()[3]
-
-        def total(chip, piece):
-            pieces = [spread_ref[chip * SIDE + second, piece, :] for second in range(SIDE)]
-            return (pieces[0] + pieces[1]) + (pieces[2] + pieces[3])
-
-        for chip in range(chips):
-            for tile in range(tiles):
-                low = total(chip, pl.ds(tile * CORES * half, half))
-                high = total(chip, pl.ds(tile * CORES * half + half, half))
-                spot = pl.ds(tile * half, half)
-                kept[chip, spot, :] = jnp.where(even, low, high)
-                given[chip, spot, :] = jnp.where(even, high, low)
-            numbers = total(chip, pl.ds(rows - 8, 8))
-            kept[chip, pl.ds(tiles * half, 8), :] = numbers
-            given[chip, pl.ds(tiles * half, 8), :] = numbers
-
-    return call(
-        body, "finish_second_ring", [f32(chips, tiles * half + 8, lanes)] * 2, [IN_VMEM]
-    )(spread)
+        body, "finish_second_ring", [f32(chips, height, width)] * 2, [IN_VMEM] * (1 + SIDE)
+    )(unique_rows, *pieces)
 
 
 def eye():
@@ -227,35 +199,31 @@
     return jnp.sum(square, axis=axis, keepdims=True)
 
 
-def apply_update(kept, swapped, tables, accums):
+def apply_update(arrived, tables, accums):
     rows_dev, width = tables.shape[1:]
     rows = 256
     count = rows_dev // rows
-
-    chips, slots = kept.shape[:2]
-    bucket = LANES // (CORES * chips)
-    slots -= 8
-    tiles = width // LANES
-
-    def body(kept_ref, swapped_ref, tables_ref, accums_ref, *refs):
-        new_tables_hbm, new_accums_ref, done_ref, sems = refs
+    height = arrived[0].shape[0] // CORES
+    bucket = (height - 8) // 2
+
+    def body(*refs):
+        arrived_refs = refs[:SIDE]
+        tables_ref, accums_ref, new_tables_hbm, new_accums_ref, done_ref, sems = refs[SIDE:]
         diagonal = eye()
         copies = []
-        sources = [(ref, chip) for ref in (kept_ref, swapped_ref) for chip in range(chips)]
+        sources = [(ref, core * height) for ref in arrived_refs for core in range(CORES)]
         group = position()[0]
         lane = lax.broadcasted_iota(jnp.int32, (8, LANES), 1) // bucket
         local_rows = jnp.zeros((8, LANES), jnp.int32)
-        for spot, (ref, chip) in enumerate(sources):
-            listed = ref[chip, pl.ds(slots, 8), :].astype(jnp.int32)
+        for spot, (ref, first) in enumerate(sources):
+            listed = ref[pl.ds(first + 2 * bucket, 8), pl.ds(0, LANES)].astype(jnp.int32)
             listed = pltpu.roll(listed, ((spot - group) * bucket) & (LANES - 1), 1)
             local_rows = jnp.where(lane == spot, listed, local_rows)
         local_rows = jnp.where(local_rows == 0, -1, (local_rows - 1) & (rows_dev - 1))
         for table in range(2):
-            columns = []
-            for tile in range(table * tiles, (table + 1) * tiles):
-                spot = pl.ds(tile * bucket, bucket)
-                columns.append(jnp.concatenate([ref[chip, spot, :] for ref, chip in sources]))
-            values = jnp.concatenate(columns, axis=1)
+            values = jnp.concatenate(
+                [ref[pl.ds(first + table * bucket, bucket), :] for ref, first in sources]
+            )
             high = values.astype(jnp.bfloat16)
             rest = values - high.astype(jnp.float32)
             middle = rest.astype(jnp.bfloat16)
@@ -292,43 +260,49 @@
         body,
         "apply_update",
         [f32(*tables.shape), f32(*accums.shape)],
-        [IN_VMEM] * 4,
+        [IN_VMEM] * (SIDE + 2),
         [IN_HBM, IN_VMEM],
         [pltpu.VMEM(tables.shape, jnp.float32), pltpu.SemaphoreType.DMA((2 * count,))],
-    )(kept, swapped, tables, accums)
+    )(*arrived, tables, accums)
 
 
 def local(lookup_grads, slot_index, unique_rows, tables, accums):
     n_group = lax.axis_size("group")
     n_local = lax.axis_size("local")
 
-    def send(value, step):
-        return lax.ppermute(value, AXES, ring_pairs(n_group, n_local, step))
+    def send(value, step, ring=0):
+        return lax.ppermute(value, AXES, ring_pairs(n_group, n_local, ring, step))
+
+    def send_along(value, step):
+        return lax.ppermute(
+            value, "group", [(i, (i + CORES * step) % n_group) for i in range(n_group)]
+        )
 
     far0, far1, grads, codes = first_sums(slot_index, lookup_grads, [(0, 2), (1, 2)])
+    back0, next1 = slot_sums(codes, grads, [(0, 3), (1, 1)], far0)
+    next0, back1 = slot_sums(codes, grads, [(0, 1), (1, 3)], next1)
+    own0, own1 = slot_sums(codes, grads, [(0, 0), (1, 0)], back1)
     far0 = send(far0, 1)
     far1 = send(far1, -1)
-    back0, next1 = slot_sums(codes, grads, [(0, 3), (1, 1)])
     next1 = send(next1, 1)
     back0 = send(back0, -1)
-    next0, back1 = slot_sums(codes, grads, [(0, 1), (1, 3)])
     next0 = send(next0 + far0, 1)
     back1 = send(back1 + far1, -1)
-    own0, own1 = slot_sums(codes, grads, [(0, 0), (1, 0)])
-
-    spread = finish_first_ring(unique_rows, own0, back0, next0, own1, next1, back1)
-    spread = lax.all_to_all(
-        spread,
-        AXES,
-        split_axis=0,
-        concat_axis=0,
-        axis_index_groups=second_groups(n_group, n_local),
-        tiled=True,
-    )
-    kept, given = finish_second_ring(spread)
+
+    token = lax.ppermute(
+        sum(value[:8, :LANES] for value in (next0, back0, next1, back1, own0)),
+        "group",
+        [(i, i ^ 1) for i in range(n_group)],
+    )
+
+    pieces = finish_first_ring(token, own0, back0, next0, own1, next1, back1)
+    pieces = [pieces[0]] + [send(pieces[step], step, ring=1) for step in range(1, SIDE)]
+    kept, given = finish_second_ring(unique_rows, pieces)
 
     swapped = lax.ppermute(given, "group", [(i, i ^ 1) for i in range(n_group)])
-    new_tables, new_accums = apply_update(kept, swapped, tables, accums)
+    arrived = [jnp.concatenate([kept[step], swapped[step]]) for step in range(SIDE)]
+    arrived = [arrived[0]] + [send_along(arrived[step], step) for step in range(1, SIDE)]
+    new_tables, new_accums = apply_update(arrived, tables, accums)
     return (new_tables, new_accums)
 
 

time: 63.5 us -> 62.1 us (0.978)
  blocking collectives: 18.9 us -> 0 us
  waiting for transfers between devices: 6.04 us -> 16.6 us
  starting transfers between devices: 15.3 us -> 22.2 us
    all_to_all x1 -> x0, blocking collectives: 18.9 us -> none  [local(): lax.all_to_all(spread, AXES, split_axis=0, concat_axis=0, axis_index_grou...]
    ppermute x6 -> x13, waiting for transfers between devices: 5.04 us -> 15.6 us  [the longest x9 11.9 us: send(): return lax.ppermute(value, AXES, ring_pairs(n_group, n_local, ring, step))]
    ppermute x6 -> x13, starting transfers between devices: 10.4 us -> 19.3 us  [the longest x9 12.5 us: send(): return lax.ppermute(value, AXES, ring_pairs(n_group, n_local, ring, step))]
    ppermute x1, starting transfers between devices: 4.9 us -> 2.9 us  [local(): swapped = lax.ppermute(given, 'group', [(i, i ^ 1) for i in range(n_group)])]
  transfers between devices with their start and end apart: 7 -> 14, of which waited for: 3 -> 7; matrix products, arithmetic and copies ran while one was open for 0% -> 0% of each run, Pallas kernels for 21% -> 22%
where the time goes in v6:
time: 62.1 us; the launch traced here: 62 us
  starting transfers between devices  22.2 us (36%)
  Pallas kernels  22 us (35%)
  waiting for transfers between devices  16.6 us (27%)
  between operations  0.91 us (1%)
    pallas_call x3, Pallas kernels, slot_sums(): call(body, 'slot_sums', [f32(rows, width) for _ in targets], [IN_VMEM] *...  13.4 us
    ppermute x9, starting transfers between devices, send(): return lax.ppermute(value, AXES, ring_pairs(n_group, n_local, ring, step))  12.5 us
    ppermute x9, waiting for transfers between devices, send(): return lax.ppermute(value, AXES, ring_pairs(n_group, n_local, ring, step))  11.9 us
    pallas_call x1, Pallas kernels, first_sums(): call(body, 'first_sums', [*[f32(rows, width) for _ in targets], jax.Shape...  5.7 us
    ppermute x3, starting transfers between devices, send_along(): lax.ppermute(value, 'group', [(i, (i + CORES * step) % n_group) for i in...  5.08 us
    ppermute x1, starting transfers between devices, local(): swapped = lax.ppermute(given, 'group', [(i, i ^ 1) for i in range(n_group)])  2.9 us
    ppermute x3, waiting for transfers between devices, send_along(): lax.ppermute(value, 'group', [(i, (i + CORES * step) % n_group) for i in...  2.86 us
    pallas_call x1, Pallas kernels, apply_update(): call(body, 'apply_update', [f32(*tables.shape), f32(*accums.shape)], [IN_...  2.65 us
  transfers between devices with their start and end apart: 14, of which 7 were waited for; matrix products, arithmetic and copies ran while one was open for 0% of the time, Pallas kernels for 22%

profile of v6, /device:TPU:1, one launch (start us, length us, event | category | flops | bytes accessed | tf_op | source)
XLA Modules:
  0.0 62.0 jit_solution(14387791661342237113)
XLA Ops:
  0.6 5.7 %first_sums.1 = (f32[512,256]{1,0:T(8,128)S(1)}, f32[512,256]{1,0:T(8,128)S(1)}, bf16[8192,256]{1,0:T(8,128)(2,1)S(1)}, s32[2,8192]{1,0:T(2,128)S(1)}) custom-call(s32[2,8192]{1,0:T(2,128)} %index_hbm.1, bf16[8192,256]{1,0:T(8,128)(2,1)} %grads_hbm.1), custom_call_target="tpu_custom_call" | custom-call | flops 429496736 | bytes 419430 | tf_op jit(solution)/shard_map/first_sums/pallas_call | solution.py:109
  6.3 4.7 %collective-permute-start.4 = (f32[512,256]{1,0:T(8,128)S(1)}, f32[512,256]{1,0:T(8,128)S(1)}, u32[]{:S(2)}, u32[]{:S(2)}) collective-permute-start(f32[512,256]{1,0:T(8,128)S(1)} %get-tuple-element.25), channel_id=1, source_target_pairs={{0,3},{1,0},{2,1},{3,2},{4,7},{5,4},{6,5},{7,6},{8,11},{9,8},{10,9... | collective-permute-start | bytes 1572872 | tf_op jit(solution)/shard_map/ppermute | solution.py:274
  11.0 4.5 %slot_sums.3 = (f32[512,256]{1,0:T(8,128)S(1)}, f32[512,256]{1,0:T(8,128)S(1)}) custom-call(s32[2,8192]{1,0:T(2,128)S(1)} %get-tuple-element.18.codes_ref, bf16[8192,256]{1,0:T(8,128)(2,1)S(1)} %get-tuple-element.19.grads_ref, f32[512,256]{1,0:T(8,128)S(1)} %get-tuple-element.20.after_ref), custom_call_target="tpu_custom_call" | custom-call | flops 429496736 | bytes 419430 | tf_op jit(solution)/shard_map/slot_sums/pallas_call | solution.py:139
  15.5 0.1 collective-permute-start.3
  15.6 2.7 %collective-permute-start.2 = (f32[512,256]{1,0:T(8,128)S(1)}, f32[512,256]{1,0:T(8,128)S(1)}, u32[]{:S(2)}, u32[]{:S(2)}) collective-permute-start(f32[512,256]{1,0:T(8,128)S(1)} %get-tuple-element.23), channel_id=1, source_target_pairs={{0,3},{1,0},{2,1},{3,2},{4,7},{5,4},{6,5},{7,6},{8,11},{9,8},{10,9... | collective-permute-start | bytes 1572872 | tf_op jit(solution)/shard_map/ppermute | solution.py:274
  18.3 4.5 %slot_sums.4 = (f32[512,256]{1,0:T(8,128)S(1)}, f32[512,256]{1,0:T(8,128)S(1)}) custom-call(s32[2,8192]{1,0:T(2,128)S(1)} %get-tuple-element.18.codes_ref, bf16[8192,256]{1,0:T(8,128)(2,1)S(1)} %get-tuple-element.19.grads_ref, f32[512,256]{1,0:T(8,128)S(1)} %get-tuple-element.21.after_ref), custom_call_target="tpu_custom_call" | custom-call | flops 429496736 | bytes 419430 | tf_op jit(solution)/shard_map/slot_sums/pallas_call | solution.py:139
  22.8 0.1 add.21
  22.9 1.4 %collective-permute-start.5 = (f32[512,256]{1,0:T(8,128)S(1)}, f32[512,256]{1,0:T(8,128)S(1)}, u32[]{:S(2)}, u32[]{:S(2)}) collective-permute-start(f32[512,256]{1,0:T(8,128)S(1)} %add.21), channel_id=1, source_target_pairs={{0,3},{1,0},{2,1},{3,2},{4,7},{5,4},{6,5},{7,6},{8,11},{9,8},{10,9... | collective-permute-start | bytes 1572872 | tf_op jit(solution)/shard_map/ppermute | solution.py:274
  24.3 0.1 add.18
  24.4 0.0 copy-start.2
  24.4 0.0 copy-start
  24.4 0.3 collective-permute-start.1
  24.8 4.5 %slot_sums.5 = (f32[512,256]{1,0:T(8,128)S(1)}, f32[512,256]{1,0:T(8,128)S(1)}) custom-call(s32[2,8192]{1,0:T(2,128)S(1)} %get-tuple-element.18.codes_ref, bf16[8192,256]{1,0:T(8,128)(2,1)S(1)} %get-tuple-element.19.grads_ref, f32[512,256]{1,0:T(8,128)S(1)} %get-tuple-element.24.after_ref), custom_call_target="tpu_custom_call" | custom-call | flops 429496736 | bytes 419430 | tf_op jit(solution)/shard_map/slot_sums/pallas_call | solution.py:139
  29.3 2.0 %collective-permute-done.5.b1 = f32[512,256]{1,0:T(8,128)S(1)} collective-permute-done((f32[512,256]{1,0:T(8,128)S(1)}, f32[512,256]{1,0:T(8,128)S(1)}, u32[]{:S(2)}, u32[]{:S(2)}) %collective-permute-start.5) | collective-permute-done | bytes 524320 | tf_op jit(solution)/shard_map/ppermute | solution.py:274
  31.3 2.9 %collective-permute-done.1.n0 = f32[512,256]{1,0:T(8,128)S(1)} collective-permute-done((f32[512,256]{1,0:T(8,128)S(1)}, f32[512,256]{1,0:T(8,128)S(1)}, u32[]{:S(2)}, u32[]{:S(2)}) %collective-permute-start.1) | collective-permute-done | bytes 524320 | tf_op jit(solution)/shard_map/ppermute | solution.py:274
  34.2 1.7 %collective-permute-start.6 = (f32[8,128]{1,0:T(8,128)S(1)}, f32[8,128]{1,0:T(8,128)S(1)}, u32[]{:S(2)}, u32[]{:S(2)}) collective-permute-start(f32[8,128]{1,0:T(8,128)S(1)} %fusion), channel_id=1, source_target_pairs={{0,16},{16,0},{32,48},{48,32},{64,80},{80,64},{96,112},{112,96},{1... | collective-permute-start | bytes 12296 | tf_op jit(solution)/shard_map/ppermute | solution.py:292
  35.9 0.8 %collective-permute-done.6.token_ref = f32[8,128]{1,0:T(8,128)S(1)} collective-permute-done((f32[8,128]{1,0:T(8,128)S(1)}, f32[8,128]{1,0:T(8,128)S(1)}, u32[]{:S(2)}, u32[]{:S(2)}) %collective-permute-start.6) | collective-permute-done | bytes 4128 | tf_op jit(solution)/shard_map/ppermute | solution.py:292
  36.7 0.2 finish_first_ring.1
  36.9 0.1 collective-permute-start.7
  37.0 2.0 %collective-permute-start.8 = (f32[256,256]{1,0:T(8,128)S(1)}, f32[256,256]{1,0:T(8,128)S(1)}, u32[]{:S(2)}, u32[]{:S(2)}) collective-permute-start(f32[256,256]{1,0:T(8,128)S(1)} %get-tuple-element.30), channel_id=1, source_target_pairs={{0,8},{1,9},{2,10},{3,11},{4,12},{5,13},{6,14},{7,15},{8,0},{9,1},... | collective-permute-start | bytes 786440 | tf_op jit(solution)/shard_map/ppermute | solution.py:274
  39.0 1.1 %collective-permute-start.9 = (f32[256,256]{1,0:T(8,128)S(1)}, f32[256,256]{1,0:T(8,128)S(1)}, u32[]{:S(2)}, u32[]{:S(2)}) collective-permute-start(f32[256,256]{1,0:T(8,128)S(1)} %get-tuple-element.31), channel_id=1, source_target_pairs={{0,12},{1,13},{2,14},{3,15},{4,0},{5,1},{6,2},{7,3},{8,4},{9,5},{1... | collective-permute-start | bytes 786440 | tf_op jit(solution)/shard_map/ppermute | solution.py:274
  40.1 6.1 %collective-permute-done.7.p1 = f32[256,256]{1,0:T(8,128)S(1)} collective-permute-done((f32[256,256]{1,0:T(8,128)S(1)}, f32[256,256]{1,0:T(8,128)S(1)}, u32[]{:S(2)}, u32[]{:S(2)}) %collective-permute-start.7) | collective-permute-done | bytes 262176 | tf_op jit(solution)/shard_map/ppermute | solution.py:274
  46.2 0.9 %collective-permute-done.9.p3 = f32[256,256]{1,0:T(8,128)S(1)} collective-permute-done((f32[256,256]{1,0:T(8,128)S(1)}, f32[256,256]{1,0:T(8,128)S(1)}, u32[]{:S(2)}, u32[]{:S(2)}) %collective-permute-start.9) | collective-permute-done | bytes 262176 | tf_op jit(solution)/shard_map/ppermute | solution.py:274
  47.1 0.1 finish_second_ring.1
  47.2 2.9 %collective-permute-start.10 = (f32[4,40,256]{2,1,0:T(8,128)S(1)}, f32[4,40,256]{2,1,0:T(8,128)S(1)}, u32[]{:S(2)}, u32[]{:S(2)}) collective-permute-start(f32[4,40,256]{2,1,0:T(8,128)S(1)} %get-tuple-element.33), channel_id=1, source_target_pairs={{0,16},{16,0},{32,48},{48,32},{64,80},{80,64},{96,112},{112,96},{1... | collective-permute-start | bytes 491528 | tf_op jit(solution)/shard_map/ppermute | solution.py:302
  50.1 1.0 %collective-permute-done.10 = f32[4,40,256]{2,1,0:T(8,128)S(1)} collective-permute-done((f32[4,40,256]{2,1,0:T(8,128)S(1)}, f32[4,40,256]{2,1,0:T(8,128)S(1)}, u32[]{:S(2)}, u32[]{:S(2)}) %collective-permute-start.10) | collective-permute-done | bytes 163872 | tf_op jit(solution)/shard_map/ppermute | solution.py:302
  51.2 1.4 %collective-permute-start.11 = (f32[80,256]{1,0:T(8,128)S(1)}, f32[80,256]{1,0:T(8,128)S(1)}, u32[]{:S(2)}, u32[]{:S(2)}) collective-permute-start(f32[80,256]{1,0:T(8,128)S(1)} %pad_maximum_fusion.1), channel_id=1, source_target_pairs={{0,32},{16,48},{32,64},{48,80},{64,96},{80,112},{96,0},{112,16},{1... | collective-permute-start | bytes 245768 | tf_op jit(solution)/shard_map/ppermute | solution.py:277
  52.5 2.6 %collective-permute-start.12 = (f32[80,256]{1,0:T(8,128)S(1)}, f32[80,256]{1,0:T(8,128)S(1)}, u32[]{:S(2)}, u32[]{:S(2)}) collective-permute-start(f32[80,256]{1,0:T(8,128)S(1)} %pad_maximum_fusion.2), channel_id=1, source_target_pairs={{0,64},{16,80},{32,96},{48,112},{64,0},{80,16},{96,32},{112,48},{1... | collective-permute-start | bytes 245768 | tf_op jit(solution)/shard_map/ppermute | solution.py:277
  55.2 1.1 %collective-permute-start.13 = (f32[80,256]{1,0:T(8,128)S(1)}, f32[80,256]{1,0:T(8,128)S(1)}, u32[]{:S(2)}, u32[]{:S(2)}) collective-permute-start(f32[80,256]{1,0:T(8,128)S(1)} %pad_maximum_fusion.3), channel_id=1, source_target_pairs={{0,96},{16,112},{32,0},{48,16},{64,32},{80,48},{96,64},{112,80},{1... | collective-permute-start | bytes 245768 | tf_op jit(solution)/shard_map/ppermute | solution.py:277
  56.3 0.0 collective-permute-done.11.refs_1_
  56.3 2.8 %collective-permute-done.12.refs_2_ = f32[80,256]{1,0:T(8,128)S(1)} collective-permute-done((f32[80,256]{1,0:T(8,128)S(1)}, f32[80,256]{1,0:T(8,128)S(1)}, u32[]{:S(2)}, u32[]{:S(2)}) %collective-permute-start.12) | collective-permute-done | bytes 81952 | tf_op jit(solution)/shard_map/ppermute | solution.py:277
  59.1 2.7 %apply_update.1 = (f32[2,1024,256]{2,1,0:T(8,128)}, f32[2,1024]{1,0:T(2,128)}) custom-call(f32[80,256]{1,0:T(8,128)S(1)} %pad_maximum_fusion.refs_0_, f32[80,256]{1,0:T(8,128)S(1)} %collective-permute-done.11.refs_1_, f32[80,256]{1,0:T(8,128)S(1)} %collective-permute-done.12.refs_2_, f32[80,256]{1,0:T(8,128)S(1)} %collective-permute-done.13.refs_3_, ...), custom_call_target="tpu_custom_call" | custom-call | tf_op jit(solution)/shard_map/apply_update/pallas_call | solution.py:259
  (18 shorter events, 0.1 us)
Async XLA Ops:
  6.3 16.5 %collective-permute-start.4 = (f32[512,256]{1,0:T(8,128)S(1)}, f32[512,256]{1,0:T(8,128)S(1)}, u32[]{:S(2)}, u32[]{:S(2)}) collective-permute-start(f32[512,256]{1,0:T(8,128)S(1)} %get-tuple-element.25), channel_id=1, source_target_pairs={{0,3},{1,0},{2,1},{3,2},{4,7},{5,4},{6,5},{7,6},{8,11},{9,8},{10,9... | collective-permute-start | bytes 1572872 | tf_op jit(solution)/shard_map/ppermute | solution.py:274
  11.0 13.3 %collective-permute-start = (f32[512,256]{1,0:T(8,128)S(1)}, f32[512,256]{1,0:T(8,128)S(1)}, u32[]{:S(2)}, u32[]{:S(2)}) collective-permute-start(f32[512,256]{1,0:T(8,128)S(1)} %get-tuple-element.20.after_ref), channel_id=1, source_target_pairs={{0,1},{1,2},{2,3},{3,0},{4,5},{5,6},{6,7},{7,4},{8,9},{9,10},{10,1... | collective-permute-start | bytes 1572872 | tf_op jit(solution)/shard_map/ppermute | solution.py:274
  15.5 13.8 %collective-permute-start.3 = (f32[512,256]{1,0:T(8,128)S(1)}, f32[512,256]{1,0:T(8,128)S(1)}, u32[]{:S(2)}, u32[]{:S(2)}) collective-permute-start(f32[512,256]{1,0:T(8,128)S(1)} %get-tuple-element.21.after_ref), channel_id=1, source_target_pairs={{0,1},{1,2},{2,3},{3,0},{4,5},{5,6},{6,7},{7,4},{8,9},{9,10},{10,1... | collective-permute-start | bytes 1572872 | tf_op jit(solution)/shard_map/ppermute | solution.py:274
  15.6 13.7 %collective-permute-start.2 = (f32[512,256]{1,0:T(8,128)S(1)}, f32[512,256]{1,0:T(8,128)S(1)}, u32[]{:S(2)}, u32[]{:S(2)}) collective-permute-start(f32[512,256]{1,0:T(8,128)S(1)} %get-tuple-element.23), channel_id=1, source_target_pairs={{0,3},{1,0},{2,1},{3,2},{4,7},{5,4},{6,5},{7,6},{8,11},{9,8},{10,9... | collective-permute-start | bytes 1572872 | tf_op jit(solution)/shard_map/ppermute | solution.py:274
  22.9 8.4 %collective-permute-start.5 = (f32[512,256]{1,0:T(8,128)S(1)}, f32[512,256]{1,0:T(8,128)S(1)}, u32[]{:S(2)}, u32[]{:S(2)}) collective-permute-start(f32[512,256]{1,0:T(8,128)S(1)} %add.21), channel_id=1, source_target_pairs={{0,3},{1,0},{2,1},{3,2},{4,7},{5,4},{6,5},{7,6},{8,11},{9,8},{10,9... | collective-permute-start | bytes 1572872 | tf_op jit(solution)/shard_map/ppermute | solution.py:274
  24.4 22.7 %copy-start.2 = (s32[2,128]{1,0:T(2,128)S(1)}, s32[2,128]{1,0:T(2,128)}, u32[]{:S(2)}) copy-start(s32[2,128]{1,0:T(2,128)} %unique_ref.1) | copy-start | bytes 3076
  24.4 34.7 %copy-start = (f32[2,1024,256]{2,1,0:T(8,128)S(1)}, f32[2,1024,256]{2,1,0:T(8,128)}, u32[]{:S(2)}) copy-start(f32[2,1024,256]{2,1,0:T(8,128)} %refs_4_.1) | copy-start | bytes 6291460
  24.4 34.7 %copy-start.1 = (f32[2,1024]{1,0:T(2,128)S(1)}, f32[2,1024]{1,0:T(2,128)}, u32[]{:S(2)}) copy-start(f32[2,1024]{1,0:T(2,128)} %refs_5_.1) | copy-start | bytes 24580
  24.4 9.8 %collective-permute-start.1 = (f32[512,256]{1,0:T(8,128)S(1)}, f32[512,256]{1,0:T(8,128)S(1)}, u32[]{:S(2)}, u32[]{:S(2)}) collective-permute-start(f32[512,256]{1,0:T(8,128)S(1)} %add.18), channel_id=1, source_target_pairs={{0,1},{1,2},{2,3},{3,0},{4,5},{5,6},{6,7},{7,4},{8,9},{9,10},{10,1... | collective-permute-start | bytes 1572872 | tf_op jit(solution)/shard_map/ppermute | solution.py:274
  34.2 2.5 %collective-permute-start.6 = (f32[8,128]{1,0:T(8,128)S(1)}, f32[8,128]{1,0:T(8,128)S(1)}, u32[]{:S(2)}, u32[]{:S(2)}) collective-permute-start(f32[8,128]{1,0:T(8,128)S(1)} %fusion), channel_id=1, source_target_pairs={{0,16},{16,0},{32,48},{48,32},{64,80},{80,64},{96,112},{112,96},{1... | collective-permute-start | bytes 12296 | tf_op jit(solution)/shard_map/ppermute | solution.py:292
  36.9 9.3 %collective-permute-start.7 = (f32[256,256]{1,0:T(8,128)S(1)}, f32[256,256]{1,0:T(8,128)S(1)}, u32[]{:S(2)}, u32[]{:S(2)}) collective-permute-start(f32[256,256]{1,0:T(8,128)S(1)} %get-tuple-element.29), channel_id=1, source_target_pairs={{0,4},{1,5},{2,6},{3,7},{4,8},{5,9},{6,10},{7,11},{8,12},{9,13},{1... | collective-permute-start | bytes 786440 | tf_op jit(solution)/shard_map/ppermute | solution.py:274
  37.0 9.2 %collective-permute-start.8 = (f32[256,256]{1,0:T(8,128)S(1)}, f32[256,256]{1,0:T(8,128)S(1)}, u32[]{:S(2)}, u32[]{:S(2)}) collective-permute-start(f32[256,256]{1,0:T(8,128)S(1)} %get-tuple-element.30), channel_id=1, source_target_pairs={{0,8},{1,9},{2,10},{3,11},{4,12},{5,13},{6,14},{7,15},{8,0},{9,1},... | collective-permute-start | bytes 786440 | tf_op jit(solution)/shard_map/ppermute | solution.py:274
  39.0 8.1 %collective-permute-start.9 = (f32[256,256]{1,0:T(8,128)S(1)}, f32[256,256]{1,0:T(8,128)S(1)}, u32[]{:S(2)}, u32[]{:S(2)}) collective-permute-start(f32[256,256]{1,0:T(8,128)S(1)} %get-tuple-element.31), channel_id=1, source_target_pairs={{0,12},{1,13},{2,14},{3,15},{4,0},{5,1},{6,2},{7,3},{8,4},{9,5},{1... | collective-permute-start | bytes 786440 | tf_op jit(solution)/shard_map/ppermute | solution.py:274
  47.2 3.9 %collective-permute-start.10 = (f32[4,40,256]{2,1,0:T(8,128)S(1)}, f32[4,40,256]{2,1,0:T(8,128)S(1)}, u32[]{:S(2)}, u32[]{:S(2)}) collective-permute-start(f32[4,40,256]{2,1,0:T(8,128)S(1)} %get-tuple-element.33), channel_id=1, source_target_pairs={{0,16},{16,0},{32,48},{48,32},{64,80},{80,64},{96,112},{112,96},{1... | collective-permute-start | bytes 491528 | tf_op jit(solution)/shard_map/ppermute | solution.py:302
  51.2 5.1 %collective-permute-start.11 = (f32[80,256]{1,0:T(8,128)S(1)}, f32[80,256]{1,0:T(8,128)S(1)}, u32[]{:S(2)}, u32[]{:S(2)}) collective-permute-start(f32[80,256]{1,0:T(8,128)S(1)} %pad_maximum_fusion.1), channel_id=1, source_target_pairs={{0,32},{16,48},{32,64},{48,80},{64,96},{80,112},{96,0},{112,16},{1... | collective-permute-start | bytes 245768 | tf_op jit(solution)/shard_map/ppermute | solution.py:277
  52.5 6.6 %collective-permute-start.12 = (f32[80,256]{1,0:T(8,128)S(1)}, f32[80,256]{1,0:T(8,128)S(1)}, u32[]{:S(2)}, u32[]{:S(2)}) collective-permute-start(f32[80,256]{1,0:T(8,128)S(1)} %pad_maximum_fusion.2), channel_id=1, source_target_pairs={{0,64},{16,80},{32,96},{48,112},{64,0},{80,16},{96,32},{112,48},{1... | collective-permute-start | bytes 245768 | tf_op jit(solution)/shard_map/ppermute | solution.py:277
  55.2 3.9 %collective-permute-start.13 = (f32[80,256]{1,0:T(8,128)S(1)}, f32[80,256]{1,0:T(8,128)S(1)}, u32[]{:S(2)}, u32[]{:S(2)}) collective-permute-start(f32[80,256]{1,0:T(8,128)S(1)} %pad_maximum_fusion.3), channel_id=1, source_target_pairs={{0,96},{16,112},{32,0},{48,16},{64,32},{80,48},{96,64},{112,80},{1... | collective-permute-start | bytes 245768 | tf_op jit(solution)/shard_map/ppermute | solution.py:277

commit v7 on v6

--- a/solution.py
+++ b/solution.py
@@ -296,12 +296,12 @@
     )
 
     pieces = finish_first_ring(token, own0, back0, next0, own1, next1, back1)
-    pieces = [pieces[0]] + [send(pieces[step], step, ring=1) for step in range(1, SIDE)]
+    pieces = [pieces[0]] + [send(pieces[step], step, ring=1) for step in (2, 1, 3)]
     kept, given = finish_second_ring(unique_rows, pieces)
 
     swapped = lax.ppermute(given, "group", [(i, i ^ 1) for i in range(n_group)])
     arrived = [jnp.concatenate([kept[step], swapped[step]]) for step in range(SIDE)]
-    arrived = [arrived[0]] + [send_along(arrived[step], step) for step in range(1, SIDE)]
+    arrived = [arrived[0]] + [send_along(arrived[step], step) for step in (2, 1, 3)]
     new_tables, new_accums = apply_update(arrived, tables, accums)
     return (new_tables, new_accums)
 

time: 62.1 us -> 61.5 us (level)
  waiting for transfers between devices: 16.6 us -> 14.7 us
  starting transfers between devices: 22.2 us -> 23.1 us
    ppermute x3, waiting for transfers between devices: 2.86 us -> 1.81 us  [send_along(): lax.ppermute(value, 'group', [(i, (i + CORES * step) % n_group) for i in...]
    ppermute x9, waiting for transfers between devices: 11.9 us -> 11 us  [send(): return lax.ppermute(value, AXES, ring_pairs(n_group, n_local, ring, step))]
    ppermute x9, starting transfers between devices: 12.5 us -> 13.1 us  [send(): return lax.ppermute(value, AXES, ring_pairs(n_group, n_local, ring, step))]
where the time goes in v7:
time: 61.5 us; the launch traced here: 60.9 us
  starting transfers between devices  23.1 us (38%)
  Pallas kernels  22 us (36%)
  waiting for transfers between devices  14.7 us (24%)
  between operations  0.9 us (1%)
    pallas_call x3, Pallas kernels, slot_sums(): call(body, 'slot_sums', [f32(rows, width) for _ in targets], [IN_VMEM] *...  13.4 us
    ppermute x9, starting transfers between devices, send(): return lax.ppermute(value, AXES, ring_pairs(n_group, n_local, ring, step))  13.1 us
    ppermute x9, waiting for transfers between devices, send(): return lax.ppermute(value, AXES, ring_pairs(n_group, n_local, ring, step))  11 us
    pallas_call x1, Pallas kernels, first_sums(): call(body, 'first_sums', [*[f32(rows, width) for _ in targets], jax.Shape...  5.7 us
    ppermute x3, starting transfers between devices, send_along(): lax.ppermute(value, 'group', [(i, (i + CORES * step) % n_group) for i in...  5.69 us
    pallas_call x1, Pallas kernels, apply_update(): call(body, 'apply_update', [f32(*tables.shape), f32(*accums.shape)], [IN_...  2.65 us
    ppermute x1, starting transfers between devices, local(): swapped = lax.ppermute(given, 'group', [(i, i ^ 1) for i in range(n_group)])  2.61 us
    ppermute x3, waiting for transfers between devices, send_along(): lax.ppermute(value, 'group', [(i, (i + CORES * step) % n_group) for i in...  1.81 us
  transfers between devices with their start and end apart: 14, of which 7 were waited for; matrix products, arithmetic and copies ran while one was open for 0% of the time, Pallas kernels for 22%

profile of v7, /device:TPU:1, one launch (start us, length us, event | category | flops | bytes accessed | tf_op | source)
XLA Modules:
  0.0 60.9 jit_solution(16953005013430049592)
XLA Ops:
  0.6 5.7 %first_sums.1 = (f32[512,256]{1,0:T(8,128)S(1)}, f32[512,256]{1,0:T(8,128)S(1)}, bf16[8192,256]{1,0:T(8,128)(2,1)S(1)}, s32[2,8192]{1,0:T(2,128)S(1)}) custom-call(s32[2,8192]{1,0:T(2,128)} %index_hbm.1, bf16[8192,256]{1,0:T(8,128)(2,1)} %grads_hbm.1), custom_call_target="tpu_custom_call" | custom-call | flops 429496736 | bytes 419430 | tf_op jit(solution)/shard_map/first_sums/pallas_call | solution.py:109
  6.3 4.7 %collective-permute-start.4 = (f32[512,256]{1,0:T(8,128)S(1)}, f32[512,256]{1,0:T(8,128)S(1)}, u32[]{:S(2)}, u32[]{:S(2)}) collective-permute-start(f32[512,256]{1,0:T(8,128)S(1)} %get-tuple-element.25), channel_id=1, source_target_pairs={{0,3},{1,0},{2,1},{3,2},{4,7},{5,4},{6,5},{7,6},{8,11},{9,8},{10,9... | collective-permute-start | bytes 1572872 | tf_op jit(solution)/shard_map/ppermute | solution.py:274
  11.0 4.5 %slot_sums.3 = (f32[512,256]{1,0:T(8,128)S(1)}, f32[512,256]{1,0:T(8,128)S(1)}) custom-call(s32[2,8192]{1,0:T(2,128)S(1)} %get-tuple-element.18.codes_ref, bf16[8192,256]{1,0:T(8,128)(2,1)S(1)} %get-tuple-element.19.grads_ref, f32[512,256]{1,0:T(8,128)S(1)} %get-tuple-element.20.after_ref), custom_call_target="tpu_custom_call" | custom-call | flops 429496736 | bytes 419430 | tf_op jit(solution)/shard_map/slot_sums/pallas_call | solution.py:139
  15.5 0.1 collective-permute-start.3
  15.6 2.7 %collective-permute-start.2 = (f32[512,256]{1,0:T(8,128)S(1)}, f32[512,256]{1,0:T(8,128)S(1)}, u32[]{:S(2)}, u32[]{:S(2)}) collective-permute-start(f32[512,256]{1,0:T(8,128)S(1)} %get-tuple-element.23), channel_id=1, source_target_pairs={{0,3},{1,0},{2,1},{3,2},{4,7},{5,4},{6,5},{7,6},{8,11},{9,8},{10,9... | collective-permute-start | bytes 1572872 | tf_op jit(solution)/shard_map/ppermute | solution.py:274
  18.3 4.5 %slot_sums.4 = (f32[512,256]{1,0:T(8,128)S(1)}, f32[512,256]{1,0:T(8,128)S(1)}) custom-call(s32[2,8192]{1,0:T(2,128)S(1)} %get-tuple-element.18.codes_ref, bf16[8192,256]{1,0:T(8,128)(2,1)S(1)} %get-tuple-element.19.grads_ref, f32[512,256]{1,0:T(8,128)S(1)} %get-tuple-element.21.after_ref), custom_call_target="tpu_custom_call" | custom-call | flops 429496736 | bytes 419430 | tf_op jit(solution)/shard_map/slot_sums/pallas_call | solution.py:139
  22.8 0.1 add.21
  22.9 1.4 %collective-permute-start.5 = (f32[512,256]{1,0:T(8,128)S(1)}, f32[512,256]{1,0:T(8,128)S(1)}, u32[]{:S(2)}, u32[]{:S(2)}) collective-permute-start(f32[512,256]{1,0:T(8,128)S(1)} %add.21), channel_id=1, source_target_pairs={{0,3},{1,0},{2,1},{3,2},{4,7},{5,4},{6,5},{7,6},{8,11},{9,8},{10,9... | collective-permute-start | bytes 1572872 | tf_op jit(solution)/shard_map/ppermute | solution.py:274
  24.3 0.1 add.18
  24.4 0.0 copy-start.2
  24.4 0.0 copy-start
  24.4 0.0 copy-start.1
  24.4 0.3 collective-permute-start.1
  24.8 4.5 %slot_sums.5 = (f32[512,256]{1,0:T(8,128)S(1)}, f32[512,256]{1,0:T(8,128)S(1)}) custom-call(s32[2,8192]{1,0:T(2,128)S(1)} %get-tuple-element.18.codes_ref, bf16[8192,256]{1,0:T(8,128)(2,1)S(1)} %get-tuple-element.19.grads_ref, f32[512,256]{1,0:T(8,128)S(1)} %get-tuple-element.24.after_ref), custom_call_target="tpu_custom_call" | custom-call | flops 429496736 | bytes 419430 | tf_op jit(solution)/shard_map/slot_sums/pallas_call | solution.py:139
  29.3 2.0 %collective-permute-done.5.b1 = f32[512,256]{1,0:T(8,128)S(1)} collective-permute-done((f32[512,256]{1,0:T(8,128)S(1)}, f32[512,256]{1,0:T(8,128)S(1)}, u32[]{:S(2)}, u32[]{:S(2)}) %collective-permute-start.5) | collective-permute-done | bytes 524320 | tf_op jit(solution)/shard_map/ppermute | solution.py:274
  31.3 2.9 %collective-permute-done.1.n0 = f32[512,256]{1,0:T(8,128)S(1)} collective-permute-done((f32[512,256]{1,0:T(8,128)S(1)}, f32[512,256]{1,0:T(8,128)S(1)}, u32[]{:S(2)}, u32[]{:S(2)}) %collective-permute-start.1) | collective-permute-done | bytes 524320 | tf_op jit(solution)/shard_map/ppermute | solution.py:274
  34.2 1.7 %collective-permute-start.6 = (f32[8,128]{1,0:T(8,128)S(1)}, f32[8,128]{1,0:T(8,128)S(1)}, u32[]{:S(2)}, u32[]{:S(2)}) collective-permute-start(f32[8,128]{1,0:T(8,128)S(1)} %fusion), channel_id=1, source_target_pairs={{0,16},{16,0},{32,48},{48,32},{64,80},{80,64},{96,112},{112,96},{1... | collective-permute-start | bytes 12296 | tf_op jit(solution)/shard_map/ppermute | solution.py:292
  35.9 0.8 %collective-permute-done.6.token_ref = f32[8,128]{1,0:T(8,128)S(1)} collective-permute-done((f32[8,128]{1,0:T(8,128)S(1)}, f32[8,128]{1,0:T(8,128)S(1)}, u32[]{:S(2)}, u32[]{:S(2)}) %collective-permute-start.6) | collective-permute-done | bytes 4128 | tf_op jit(solution)/shard_map/ppermute | solution.py:292
  36.7 0.2 finish_first_ring.1
  36.9 1.2 %collective-permute-start.7 = (f32[256,256]{1,0:T(8,128)S(1)}, f32[256,256]{1,0:T(8,128)S(1)}, u32[]{:S(2)}, u32[]{:S(2)}) collective-permute-start(f32[256,256]{1,0:T(8,128)S(1)} %get-tuple-element.29), channel_id=1, source_target_pairs={{0,8},{1,9},{2,10},{3,11},{4,12},{5,13},{6,14},{7,15},{8,0},{9,1},... | collective-permute-start | bytes 786440 | tf_op jit(solution)/shard_map/ppermute | solution.py:274
  38.1 0.3 collective-permute-start.8
  38.4 2.4 %collective-permute-start.9 = (f32[256,256]{1,0:T(8,128)S(1)}, f32[256,256]{1,0:T(8,128)S(1)}, u32[]{:S(2)}, u32[]{:S(2)}) collective-permute-start(f32[256,256]{1,0:T(8,128)S(1)} %get-tuple-element.31), channel_id=1, source_target_pairs={{0,12},{1,13},{2,14},{3,15},{4,0},{5,1},{6,2},{7,3},{8,4},{9,5},{1... | collective-permute-start | bytes 786440 | tf_op jit(solution)/shard_map/ppermute | solution.py:274
  40.8 3.3 %collective-permute-done.7.p1 = f32[256,256]{1,0:T(8,128)S(1)} collective-permute-done((f32[256,256]{1,0:T(8,128)S(1)}, f32[256,256]{1,0:T(8,128)S(1)}, u32[]{:S(2)}, u32[]{:S(2)}) %collective-permute-start.7) | collective-permute-done | bytes 262176 | tf_op jit(solution)/shard_map/ppermute | solution.py:274
  44.0 2.8 %collective-permute-done.8.p2 = f32[256,256]{1,0:T(8,128)S(1)} collective-permute-done((f32[256,256]{1,0:T(8,128)S(1)}, f32[256,256]{1,0:T(8,128)S(1)}, u32[]{:S(2)}, u32[]{:S(2)}) %collective-permute-start.8) | collective-permute-done | bytes 262176 | tf_op jit(solution)/shard_map/ppermute | solution.py:274
  46.8 0.1 finish_second_ring.1
  46.9 2.6 %collective-permute-start.10 = (f32[4,40,256]{2,1,0:T(8,128)S(1)}, f32[4,40,256]{2,1,0:T(8,128)S(1)}, u32[]{:S(2)}, u32[]{:S(2)}) collective-permute-start(f32[4,40,256]{2,1,0:T(8,128)S(1)} %get-tuple-element.33), channel_id=1, source_target_pairs={{0,16},{16,0},{32,48},{48,32},{64,80},{80,64},{96,112},{112,96},{1... | collective-permute-start | bytes 491528 | tf_op jit(solution)/shard_map/ppermute | solution.py:302
  49.5 1.0 %collective-permute-done.10 = f32[4,40,256]{2,1,0:T(8,128)S(1)} collective-permute-done((f32[4,40,256]{2,1,0:T(8,128)S(1)}, f32[4,40,256]{2,1,0:T(8,128)S(1)}, u32[]{:S(2)}, u32[]{:S(2)}) %collective-permute-start.10) | collective-permute-done | bytes 163872 | tf_op jit(solution)/shard_map/ppermute | solution.py:302
  50.6 3.0 %collective-permute-start.11 = (f32[80,256]{1,0:T(8,128)S(1)}, f32[80,256]{1,0:T(8,128)S(1)}, u32[]{:S(2)}, u32[]{:S(2)}) collective-permute-start(f32[80,256]{1,0:T(8,128)S(1)} %pad_maximum_fusion.1), channel_id=1, source_target_pairs={{0,64},{16,80},{32,96},{48,112},{64,0},{80,16},{96,32},{112,48},{1... | collective-permute-start | bytes 245768 | tf_op jit(solution)/shard_map/ppermute | solution.py:277
  53.6 0.4 collective-permute-start.12
  54.0 2.3 %collective-permute-start.13 = (f32[80,256]{1,0:T(8,128)S(1)}, f32[80,256]{1,0:T(8,128)S(1)}, u32[]{:S(2)}, u32[]{:S(2)}) collective-permute-start(f32[80,256]{1,0:T(8,128)S(1)} %pad_maximum_fusion.3), channel_id=1, source_target_pairs={{0,96},{16,112},{32,0},{48,16},{64,32},{80,48},{96,64},{112,80},{1... | collective-permute-start | bytes 245768 | tf_op jit(solution)/shard_map/ppermute | solution.py:277
  56.3 1.8 %collective-permute-done.12.refs_2_ = f32[80,256]{1,0:T(8,128)S(1)} collective-permute-done((f32[80,256]{1,0:T(8,128)S(1)}, f32[80,256]{1,0:T(8,128)S(1)}, u32[]{:S(2)}, u32[]{:S(2)}) %collective-permute-start.12) | collective-permute-done | bytes 81952 | tf_op jit(solution)/shard_map/ppermute | solution.py:277
  58.1 2.7 %apply_update.1 = (f32[2,1024,256]{2,1,0:T(8,128)}, f32[2,1024]{1,0:T(2,128)}) custom-call(f32[80,256]{1,0:T(8,128)S(1)} %pad_maximum_fusion.refs_0_, f32[80,256]{1,0:T(8,128)S(1)} %collective-permute-done.11.refs_1_, f32[80,256]{1,0:T(8,128)S(1)} %collective-permute-done.12.refs_2_, f32[80,256]{1,0:T(8,128)S(1)} %collective-permute-done.13.refs_3_, ...), custom_call_target="tpu_custom_call" | custom-call | tf_op jit(solution)/shard_map/apply_update/pallas_call | solution.py:259
  (18 shorter events, 0.1 us)
Async XLA Ops:
  6.3 16.5 %collective-permute-start.4 = (f32[512,256]{1,0:T(8,128)S(1)}, f32[512,256]{1,0:T(8,128)S(1)}, u32[]{:S(2)}, u32[]{:S(2)}) collective-permute-start(f32[512,256]{1,0:T(8,128)S(1)} %get-tuple-element.25), channel_id=1, source_target_pairs={{0,3},{1,0},{2,1},{3,2},{4,7},{5,4},{6,5},{7,6},{8,11},{9,8},{10,9... | collective-permute-start | bytes 1572872 | tf_op jit(solution)/shard_map/ppermute | solution.py:274
  11.0 13.3 %collective-permute-start = (f32[512,256]{1,0:T(8,128)S(1)}, f32[512,256]{1,0:T(8,128)S(1)}, u32[]{:S(2)}, u32[]{:S(2)}) collective-permute-start(f32[512,256]{1,0:T(8,128)S(1)} %get-tuple-element.20.after_ref), channel_id=1, source_target_pairs={{0,1},{1,2},{2,3},{3,0},{4,5},{5,6},{6,7},{7,4},{8,9},{9,10},{10,1... | collective-permute-start | bytes 1572872 | tf_op jit(solution)/shard_map/ppermute | solution.py:274
  15.5 13.8 %collective-permute-start.3 = (f32[512,256]{1,0:T(8,128)S(1)}, f32[512,256]{1,0:T(8,128)S(1)}, u32[]{:S(2)}, u32[]{:S(2)}) collective-permute-start(f32[512,256]{1,0:T(8,128)S(1)} %get-tuple-element.21.after_ref), channel_id=1, source_target_pairs={{0,1},{1,2},{2,3},{3,0},{4,5},{5,6},{6,7},{7,4},{8,9},{9,10},{10,1... | collective-permute-start | bytes 1572872 | tf_op jit(solution)/shard_map/ppermute | solution.py:274
  15.6 13.7 %collective-permute-start.2 = (f32[512,256]{1,0:T(8,128)S(1)}, f32[512,256]{1,0:T(8,128)S(1)}, u32[]{:S(2)}, u32[]{:S(2)}) collective-permute-start(f32[512,256]{1,0:T(8,128)S(1)} %get-tuple-element.23), channel_id=1, source_target_pairs={{0,3},{1,0},{2,1},{3,2},{4,7},{5,4},{6,5},{7,6},{8,11},{9,8},{10,9... | collective-permute-start | bytes 1572872 | tf_op jit(solution)/shard_map/ppermute | solution.py:274
  22.9 8.4 %collective-permute-start.5 = (f32[512,256]{1,0:T(8,128)S(1)}, f32[512,256]{1,0:T(8,128)S(1)}, u32[]{:S(2)}, u32[]{:S(2)}) collective-permute-start(f32[512,256]{1,0:T(8,128)S(1)} %add.21), channel_id=1, source_target_pairs={{0,3},{1,0},{2,1},{3,2},{4,7},{5,4},{6,5},{7,6},{8,11},{9,8},{10,9... | collective-permute-start | bytes 1572872 | tf_op jit(solution)/shard_map/ppermute | solution.py:274
  24.4 22.4 %copy-start.2 = (s32[2,128]{1,0:T(2,128)S(1)}, s32[2,128]{1,0:T(2,128)}, u32[]{:S(2)}) copy-start(s32[2,128]{1,0:T(2,128)} %unique_ref.1) | copy-start | bytes 3076
  24.4 33.7 %copy-start = (f32[2,1024,256]{2,1,0:T(8,128)S(1)}, f32[2,1024,256]{2,1,0:T(8,128)}, u32[]{:S(2)}) copy-start(f32[2,1024,256]{2,1,0:T(8,128)} %refs_4_.1) | copy-start | bytes 6291460
  24.4 33.7 %copy-start.1 = (f32[2,1024]{1,0:T(2,128)S(1)}, f32[2,1024]{1,0:T(2,128)}, u32[]{:S(2)}) copy-start(f32[2,1024]{1,0:T(2,128)} %refs_5_.1) | copy-start | bytes 24580
  24.4 9.8 %collective-permute-start.1 = (f32[512,256]{1,0:T(8,128)S(1)}, f32[512,256]{1,0:T(8,128)S(1)}, u32[]{:S(2)}, u32[]{:S(2)}) collective-permute-start(f32[512,256]{1,0:T(8,128)S(1)} %add.18), channel_id=1, source_target_pairs={{0,1},{1,2},{2,3},{3,0},{4,5},{5,6},{6,7},{7,4},{8,9},{9,10},{10,1... | collective-permute-start | bytes 1572872 | tf_op jit(solution)/shard_map/ppermute | solution.py:274
  34.2 2.5 %collective-permute-start.6 = (f32[8,128]{1,0:T(8,128)S(1)}, f32[8,128]{1,0:T(8,128)S(1)}, u32[]{:S(2)}, u32[]{:S(2)}) collective-permute-start(f32[8,128]{1,0:T(8,128)S(1)} %fusion), channel_id=1, source_target_pairs={{0,16},{16,0},{32,48},{48,32},{64,80},{80,64},{96,112},{112,96},{1... | collective-permute-start | bytes 12296 | tf_op jit(solution)/shard_map/ppermute | solution.py:292
  36.9 7.1 %collective-permute-start.7 = (f32[256,256]{1,0:T(8,128)S(1)}, f32[256,256]{1,0:T(8,128)S(1)}, u32[]{:S(2)}, u32[]{:S(2)}) collective-permute-start(f32[256,256]{1,0:T(8,128)S(1)} %get-tuple-element.29), channel_id=1, source_target_pairs={{0,8},{1,9},{2,10},{3,11},{4,12},{5,13},{6,14},{7,15},{8,0},{9,1},... | collective-permute-start | bytes 786440 | tf_op jit(solution)/shard_map/ppermute | solution.py:274
  38.1 8.7 %collective-permute-start.8 = (f32[256,256]{1,0:T(8,128)S(1)}, f32[256,256]{1,0:T(8,128)S(1)}, u32[]{:S(2)}, u32[]{:S(2)}) collective-permute-start(f32[256,256]{1,0:T(8,128)S(1)} %get-tuple-element.30), channel_id=1, source_target_pairs={{0,4},{1,5},{2,6},{3,7},{4,8},{5,9},{6,10},{7,11},{8,12},{9,13},{1... | collective-permute-start | bytes 786440 | tf_op jit(solution)/shard_map/ppermute | solution.py:274
  38.4 8.4 %collective-permute-start.9 = (f32[256,256]{1,0:T(8,128)S(1)}, f32[256,256]{1,0:T(8,128)S(1)}, u32[]{:S(2)}, u32[]{:S(2)}) collective-permute-start(f32[256,256]{1,0:T(8,128)S(1)} %get-tuple-element.31), channel_id=1, source_target_pairs={{0,12},{1,13},{2,14},{3,15},{4,0},{5,1},{6,2},{7,3},{8,4},{9,5},{1... | collective-permute-start | bytes 786440 | tf_op jit(solution)/shard_map/ppermute | solution.py:274
  46.9 3.6 %collective-permute-start.10 = (f32[4,40,256]{2,1,0:T(8,128)S(1)}, f32[4,40,256]{2,1,0:T(8,128)S(1)}, u32[]{:S(2)}, u32[]{:S(2)}) collective-permute-start(f32[4,40,256]{2,1,0:T(8,128)S(1)} %get-tuple-element.33), channel_id=1, source_target_pairs={{0,16},{16,0},{32,48},{48,32},{64,80},{80,64},{96,112},{112,96},{1... | collective-permute-start | bytes 491528 | tf_op jit(solution)/shard_map/ppermute | solution.py:302
  50.6 5.7 %collective-permute-start.11 = (f32[80,256]{1,0:T(8,128)S(1)}, f32[80,256]{1,0:T(8,128)S(1)}, u32[]{:S(2)}, u32[]{:S(2)}) collective-permute-start(f32[80,256]{1,0:T(8,128)S(1)} %pad_maximum_fusion.1), channel_id=1, source_target_pairs={{0,64},{16,80},{32,96},{48,112},{64,0},{80,16},{96,32},{112,48},{1... | collective-permute-start | bytes 245768 | tf_op jit(solution)/shard_map/ppermute | solution.py:277
  53.6 4.5 %collective-permute-start.12 = (f32[80,256]{1,0:T(8,128)S(1)}, f32[80,256]{1,0:T(8,128)S(1)}, u32[]{:S(2)}, u32[]{:S(2)}) collective-permute-start(f32[80,256]{1,0:T(8,128)S(1)} %pad_maximum_fusion.2), channel_id=1, source_target_pairs={{0,32},{16,48},{32,64},{48,80},{64,96},{80,112},{96,0},{112,16},{1... | collective-permute-start | bytes 245768 | tf_op jit(solution)/shard_map/ppermute | solution.py:277
  54.0 4.1 %collective-permute-start.13 = (f32[80,256]{1,0:T(8,128)S(1)}, f32[80,256]{1,0:T(8,128)S(1)}, u32[]{:S(2)}, u32[]{:S(2)}) collective-permute-start(f32[80,256]{1,0:T(8,128)S(1)} %pad_maximum_fusion.3), channel_id=1, source_target_pairs={{0,96},{16,112},{32,0},{48,16},{64,32},{80,48},{96,64},{112,80},{1... | collective-permute-start | bytes 245768 | tf_op jit(solution)/shard_map/ppermute | solution.py:277

commit v8 on v7

--- a/solution.py
+++ b/solution.py
@@ -13,7 +13,7 @@
 CORES = 2
 LANES = 128
 VMEM_BYTES = 16 << 20
-FIRST_BLOCKS = (1024, 3072, 4096)
+FIRST_BLOCKS = (512, 1536, 2048, 4096)
 BLOCK = 1024
 IN_VMEM = pl.BlockSpec(memory_space=pltpu.VMEM)
 IN_HBM = pl.BlockSpec(memory_space=pltpu.HBM)
@@ -96,15 +96,16 @@
             copy.start()
         _, own_first, own_second, even = position()
         index_copy.wait()
-        index = index_ref[...]
-        first = lax.shift_right_logical(index, jnp.where(even, 7, 9)) & (SIDE - 1)
-        second = lax.shift_right_logical(index, jnp.where(even, 9, 7)) & (SIDE - 1)
-        first = (first - own_first) & (SIDE - 1)
-        second = (second - own_second) & (SIDE - 1)
-        codes_ref[...] = first * rows + second * LANES + (index & (LANES - 1))
         for i, piece in enumerate(pieces):
+            index = index_ref[:, piece]
+            first = lax.shift_right_logical(index, jnp.where(even, 7, 9)) & (SIDE - 1)
+            second = lax.shift_right_logical(index, jnp.where(even, 9, 7)) & (SIDE - 1)
+            first = (first - own_first) & (SIDE - 1)
+            second = (second - own_second) & (SIDE - 1)
+            codes = first * rows + second * LANES + (index & (LANES - 1))
+            codes_ref[:, piece] = codes
             copies[i].wait()
-            add_block(codes_ref[:, piece], grads_ref[piece, :], targets, i, out_refs)
+            add_block(codes, grads_ref[piece, :], targets, i, out_refs)
 
     return call(
         body,

time: 61.5 us -> 61.5 us (level)
  no operation moved by 1% of the time
where the time goes in v8:
time: 61.5 us; the launch traced here: 60.9 us
  starting transfers between devices  23.1 us (38%)
  Pallas kernels  22 us (36%)
  waiting for transfers between devices  14.6 us (24%)
  between operations  0.9 us (1%)
    pallas_call x3, Pallas kernels, slot_sums(): call(body, 'slot_sums', [f32(rows, width) for _ in targets], [IN_VMEM] *...  13.4 us
    ppermute x9, starting transfers between devices, send(): return lax.ppermute(value, AXES, ring_pairs(n_group, n_local, ring, step))  13.1 us
    ppermute x9, waiting for transfers between devices, send(): return lax.ppermute(value, AXES, ring_pairs(n_group, n_local, ring, step))  11 us
    pallas_call x1, Pallas kernels, first_sums(): call(body, 'first_sums', [*[f32(rows, width) for _ in targets], jax.Shape...  5.69 us
    ppermute x3, starting transfers between devices, send_along(): lax.ppermute(value, 'group', [(i, (i + CORES * step) % n_group) for i in...  5.65 us
    pallas_call x1, Pallas kernels, apply_update(): call(body, 'apply_update', [f32(*tables.shape), f32(*accums.shape)], [IN_...  2.65 us
    ppermute x1, starting transfers between devices, local(): swapped = lax.ppermute(given, 'group', [(i, i ^ 1) for i in range(n_group)])  2.64 us
    ppermute x3, waiting for transfers between devices, send_along(): lax.ppermute(value, 'group', [(i, (i + CORES * step) % n_group) for i in...  1.81 us
  transfers between devices with their start and end apart: 14, of which 7 were waited for; matrix products, arithmetic and copies ran while one was open for 0% of the time, Pallas kernels for 22%

profile of v8, /device:TPU:1, one launch (start us, length us, event | category | flops | bytes accessed | tf_op | source)
XLA Modules:
  0.0 60.9 jit_solution(13164893778641116666)
XLA Ops:
  0.6 5.7 %first_sums.1 = (f32[512,256]{1,0:T(8,128)S(1)}, f32[512,256]{1,0:T(8,128)S(1)}, bf16[8192,256]{1,0:T(8,128)(2,1)S(1)}, s32[2,8192]{1,0:T(2,128)S(1)}) custom-call(s32[2,8192]{1,0:T(2,128)} %index_hbm.1, bf16[8192,256]{1,0:T(8,128)(2,1)} %grads_hbm.1), custom_call_target="tpu_custom_call" | custom-call | flops 429496736 | bytes 419430 | tf_op jit(solution)/shard_map/first_sums/pallas_call | solution.py:110
  6.3 4.7 %collective-permute-start.4 = (f32[512,256]{1,0:T(8,128)S(1)}, f32[512,256]{1,0:T(8,128)S(1)}, u32[]{:S(2)}, u32[]{:S(2)}) collective-permute-start(f32[512,256]{1,0:T(8,128)S(1)} %get-tuple-element.25), channel_id=1, source_target_pairs={{0,3},{1,0},{2,1},{3,2},{4,7},{5,4},{6,5},{7,6},{8,11},{9,8},{10,9... | collective-permute-start | bytes 1572872 | tf_op jit(solution)/shard_map/ppermute | solution.py:275
  11.0 4.5 %slot_sums.3 = (f32[512,256]{1,0:T(8,128)S(1)}, f32[512,256]{1,0:T(8,128)S(1)}) custom-call(s32[2,8192]{1,0:T(2,128)S(1)} %get-tuple-element.18.codes_ref, bf16[8192,256]{1,0:T(8,128)(2,1)S(1)} %get-tuple-element.19.grads_ref, f32[512,256]{1,0:T(8,128)S(1)} %get-tuple-element.20.after_ref), custom_call_target="tpu_custom_call" | custom-call | flops 429496736 | bytes 419430 | tf_op jit(solution)/shard_map/slot_sums/pallas_call | solution.py:140
  15.5 0.1 collective-permute-start.3
  15.5 2.7 %collective-permute-start.2 = (f32[512,256]{1,0:T(8,128)S(1)}, f32[512,256]{1,0:T(8,128)S(1)}, u32[]{:S(2)}, u32[]{:S(2)}) collective-permute-start(f32[512,256]{1,0:T(8,128)S(1)} %get-tuple-element.23), channel_id=1, source_target_pairs={{0,3},{1,0},{2,1},{3,2},{4,7},{5,4},{6,5},{7,6},{8,11},{9,8},{10,9... | collective-permute-start | bytes 1572872 | tf_op jit(solution)/shard_map/ppermute | solution.py:275
  18.3 4.5 %slot_sums.4 = (f32[512,256]{1,0:T(8,128)S(1)}, f32[512,256]{1,0:T(8,128)S(1)}) custom-call(s32[2,8192]{1,0:T(2,128)S(1)} %get-tuple-element.18.codes_ref, bf16[8192,256]{1,0:T(8,128)(2,1)S(1)} %get-tuple-element.19.grads_ref, f32[512,256]{1,0:T(8,128)S(1)} %get-tuple-element.21.after_ref), custom_call_target="tpu_custom_call" | custom-call | flops 429496736 | bytes 419430 | tf_op jit(solution)/shard_map/slot_sums/pallas_call | solution.py:140
  22.8 0.1 add.21
  22.9 1.5 %collective-permute-start.5 = (f32[512,256]{1,0:T(8,128)S(1)}, f32[512,256]{1,0:T(8,128)S(1)}, u32[]{:S(2)}, u32[]{:S(2)}) collective-permute-start(f32[512,256]{1,0:T(8,128)S(1)} %add.21), channel_id=1, source_target_pairs={{0,3},{1,0},{2,1},{3,2},{4,7},{5,4},{6,5},{7,6},{8,11},{9,8},{10,9... | collective-permute-start | bytes 1572872 | tf_op jit(solution)/shard_map/ppermute | solution.py:275
  24.3 0.1 add.18
  24.4 0.0 copy-start.2
  24.4 0.0 copy-start
  24.4 0.0 copy-start.1
  24.4 0.3 collective-permute-start.1
  24.7 4.5 %slot_sums.5 = (f32[512,256]{1,0:T(8,128)S(1)}, f32[512,256]{1,0:T(8,128)S(1)}) custom-call(s32[2,8192]{1,0:T(2,128)S(1)} %get-tuple-element.18.codes_ref, bf16[8192,256]{1,0:T(8,128)(2,1)S(1)} %get-tuple-element.19.grads_ref, f32[512,256]{1,0:T(8,128)S(1)} %get-tuple-element.24.after_ref), custom_call_target="tpu_custom_call" | custom-call | flops 429496736 | bytes 419430 | tf_op jit(solution)/shard_map/slot_sums/pallas_call | solution.py:140
  29.2 2.0 %collective-permute-done.5.b1 = f32[512,256]{1,0:T(8,128)S(1)} collective-permute-done((f32[512,256]{1,0:T(8,128)S(1)}, f32[512,256]{1,0:T(8,128)S(1)}, u32[]{:S(2)}, u32[]{:S(2)}) %collective-permute-start.5) | collective-permute-done | bytes 524320 | tf_op jit(solution)/shard_map/ppermute | solution.py:275
  31.2 3.0 %collective-permute-done.1.n0 = f32[512,256]{1,0:T(8,128)S(1)} collective-permute-done((f32[512,256]{1,0:T(8,128)S(1)}, f32[512,256]{1,0:T(8,128)S(1)}, u32[]{:S(2)}, u32[]{:S(2)}) %collective-permute-start.1) | collective-permute-done | bytes 524320 | tf_op jit(solution)/shard_map/ppermute | solution.py:275
  34.2 1.7 %collective-permute-start.6 = (f32[8,128]{1,0:T(8,128)S(1)}, f32[8,128]{1,0:T(8,128)S(1)}, u32[]{:S(2)}, u32[]{:S(2)}) collective-permute-start(f32[8,128]{1,0:T(8,128)S(1)} %fusion), channel_id=1, source_target_pairs={{0,16},{16,0},{32,48},{48,32},{64,80},{80,64},{96,112},{112,96},{1... | collective-permute-start | bytes 12296 | tf_op jit(solution)/shard_map/ppermute | solution.py:293
  35.9 0.8 %collective-permute-done.6.token_ref = f32[8,128]{1,0:T(8,128)S(1)} collective-permute-done((f32[8,128]{1,0:T(8,128)S(1)}, f32[8,128]{1,0:T(8,128)S(1)}, u32[]{:S(2)}, u32[]{:S(2)}) %collective-permute-start.6) | collective-permute-done | bytes 4128 | tf_op jit(solution)/shard_map/ppermute | solution.py:293
  36.7 0.2 finish_first_ring.1
  36.9 1.2 %collective-permute-start.7 = (f32[256,256]{1,0:T(8,128)S(1)}, f32[256,256]{1,0:T(8,128)S(1)}, u32[]{:S(2)}, u32[]{:S(2)}) collective-permute-start(f32[256,256]{1,0:T(8,128)S(1)} %get-tuple-element.29), channel_id=1, source_target_pairs={{0,8},{1,9},{2,10},{3,11},{4,12},{5,13},{6,14},{7,15},{8,0},{9,1},... | collective-permute-start | bytes 786440 | tf_op jit(solution)/shard_map/ppermute | solution.py:275
  38.1 0.3 collective-permute-start.8
  38.4 2.4 %collective-permute-start.9 = (f32[256,256]{1,0:T(8,128)S(1)}, f32[256,256]{1,0:T(8,128)S(1)}, u32[]{:S(2)}, u32[]{:S(2)}) collective-permute-start(f32[256,256]{1,0:T(8,128)S(1)} %get-tuple-element.31), channel_id=1, source_target_pairs={{0,12},{1,13},{2,14},{3,15},{4,0},{5,1},{6,2},{7,3},{8,4},{9,5},{1... | collective-permute-start | bytes 786440 | tf_op jit(solution)/shard_map/ppermute | solution.py:275
  40.8 3.3 %collective-permute-done.7.p1 = f32[256,256]{1,0:T(8,128)S(1)} collective-permute-done((f32[256,256]{1,0:T(8,128)S(1)}, f32[256,256]{1,0:T(8,128)S(1)}, u32[]{:S(2)}, u32[]{:S(2)}) %collective-permute-start.7) | collective-permute-done | bytes 262176 | tf_op jit(solution)/shard_map/ppermute | solution.py:275
  44.0 2.8 %collective-permute-done.8.p2 = f32[256,256]{1,0:T(8,128)S(1)} collective-permute-done((f32[256,256]{1,0:T(8,128)S(1)}, f32[256,256]{1,0:T(8,128)S(1)}, u32[]{:S(2)}, u32[]{:S(2)}) %collective-permute-start.8) | collective-permute-done | bytes 262176 | tf_op jit(solution)/shard_map/ppermute | solution.py:275
  46.8 0.1 finish_second_ring.1
  46.9 2.6 %collective-permute-start.10 = (f32[4,40,256]{2,1,0:T(8,128)S(1)}, f32[4,40,256]{2,1,0:T(8,128)S(1)}, u32[]{:S(2)}, u32[]{:S(2)}) collective-permute-start(f32[4,40,256]{2,1,0:T(8,128)S(1)} %get-tuple-element.33), channel_id=1, source_target_pairs={{0,16},{16,0},{32,48},{48,32},{64,80},{80,64},{96,112},{112,96},{1... | collective-permute-start | bytes 491528 | tf_op jit(solution)/shard_map/ppermute | solution.py:303
  49.5 1.0 %collective-permute-done.10 = f32[4,40,256]{2,1,0:T(8,128)S(1)} collective-permute-done((f32[4,40,256]{2,1,0:T(8,128)S(1)}, f32[4,40,256]{2,1,0:T(8,128)S(1)}, u32[]{:S(2)}, u32[]{:S(2)}) %collective-permute-start.10) | collective-permute-done | bytes 163872 | tf_op jit(solution)/shard_map/ppermute | solution.py:303
  50.6 3.0 %collective-permute-start.11 = (f32[80,256]{1,0:T(8,128)S(1)}, f32[80,256]{1,0:T(8,128)S(1)}, u32[]{:S(2)}, u32[]{:S(2)}) collective-permute-start(f32[80,256]{1,0:T(8,128)S(1)} %pad_maximum_fusion.1), channel_id=1, source_target_pairs={{0,64},{16,80},{32,96},{48,112},{64,0},{80,16},{96,32},{112,48},{1... | collective-permute-start | bytes 245768 | tf_op jit(solution)/shard_map/ppermute | solution.py:278
  53.5 0.4 collective-permute-start.12
  53.9 2.3 %collective-permute-start.13 = (f32[80,256]{1,0:T(8,128)S(1)}, f32[80,256]{1,0:T(8,128)S(1)}, u32[]{:S(2)}, u32[]{:S(2)}) collective-permute-start(f32[80,256]{1,0:T(8,128)S(1)} %pad_maximum_fusion.3), channel_id=1, source_target_pairs={{0,96},{16,112},{32,0},{48,16},{64,32},{80,48},{96,64},{112,80},{1... | collective-permute-start | bytes 245768 | tf_op jit(solution)/shard_map/ppermute | solution.py:278
  56.2 1.8 %collective-permute-done.12.refs_2_ = f32[80,256]{1,0:T(8,128)S(1)} collective-permute-done((f32[80,256]{1,0:T(8,128)S(1)}, f32[80,256]{1,0:T(8,128)S(1)}, u32[]{:S(2)}, u32[]{:S(2)}) %collective-permute-start.12) | collective-permute-done | bytes 81952 | tf_op jit(solution)/shard_map/ppermute | solution.py:278
  58.1 2.7 %apply_update.1 = (f32[2,1024,256]{2,1,0:T(8,128)}, f32[2,1024]{1,0:T(2,128)}) custom-call(f32[80,256]{1,0:T(8,128)S(1)} %pad_maximum_fusion.refs_0_, f32[80,256]{1,0:T(8,128)S(1)} %collective-permute-done.11.refs_1_, f32[80,256]{1,0:T(8,128)S(1)} %collective-permute-done.12.refs_2_, f32[80,256]{1,0:T(8,128)S(1)} %collective-permute-done.13.refs_3_, ...), custom_call_target="tpu_custom_call" | custom-call | tf_op jit(solution)/shard_map/apply_update/pallas_call | solution.py:260
  (18 shorter events, 0.1 us)
Async XLA Ops:
  6.3 16.4 %collective-permute-start.4 = (f32[512,256]{1,0:T(8,128)S(1)}, f32[512,256]{1,0:T(8,128)S(1)}, u32[]{:S(2)}, u32[]{:S(2)}) collective-permute-start(f32[512,256]{1,0:T(8,128)S(1)} %get-tuple-element.25), channel_id=1, source_target_pairs={{0,3},{1,0},{2,1},{3,2},{4,7},{5,4},{6,5},{7,6},{8,11},{9,8},{10,9... | collective-permute-start | bytes 1572872 | tf_op jit(solution)/shard_map/ppermute | solution.py:275
  11.0 13.3 %collective-permute-start = (f32[512,256]{1,0:T(8,128)S(1)}, f32[512,256]{1,0:T(8,128)S(1)}, u32[]{:S(2)}, u32[]{:S(2)}) collective-permute-start(f32[512,256]{1,0:T(8,128)S(1)} %get-tuple-element.20.after_ref), channel_id=1, source_target_pairs={{0,1},{1,2},{2,3},{3,0},{4,5},{5,6},{6,7},{7,4},{8,9},{9,10},{10,1... | collective-permute-start | bytes 1572872 | tf_op jit(solution)/shard_map/ppermute | solution.py:275
  15.5 13.8 %collective-permute-start.3 = (f32[512,256]{1,0:T(8,128)S(1)}, f32[512,256]{1,0:T(8,128)S(1)}, u32[]{:S(2)}, u32[]{:S(2)}) collective-permute-start(f32[512,256]{1,0:T(8,128)S(1)} %get-tuple-element.21.after_ref), channel_id=1, source_target_pairs={{0,1},{1,2},{2,3},{3,0},{4,5},{5,6},{6,7},{7,4},{8,9},{9,10},{10,1... | collective-permute-start | bytes 1572872 | tf_op jit(solution)/shard_map/ppermute | solution.py:275
  15.5 13.7 %collective-permute-start.2 = (f32[512,256]{1,0:T(8,128)S(1)}, f32[512,256]{1,0:T(8,128)S(1)}, u32[]{:S(2)}, u32[]{:S(2)}) collective-permute-start(f32[512,256]{1,0:T(8,128)S(1)} %get-tuple-element.23), channel_id=1, source_target_pairs={{0,3},{1,0},{2,1},{3,2},{4,7},{5,4},{6,5},{7,6},{8,11},{9,8},{10,9... | collective-permute-start | bytes 1572872 | tf_op jit(solution)/shard_map/ppermute | solution.py:275
  22.9 8.4 %collective-permute-start.5 = (f32[512,256]{1,0:T(8,128)S(1)}, f32[512,256]{1,0:T(8,128)S(1)}, u32[]{:S(2)}, u32[]{:S(2)}) collective-permute-start(f32[512,256]{1,0:T(8,128)S(1)} %add.21), channel_id=1, source_target_pairs={{0,3},{1,0},{2,1},{3,2},{4,7},{5,4},{6,5},{7,6},{8,11},{9,8},{10,9... | collective-permute-start | bytes 1572872 | tf_op jit(solution)/shard_map/ppermute | solution.py:275
  24.4 22.4 %copy-start.2 = (s32[2,128]{1,0:T(2,128)S(1)}, s32[2,128]{1,0:T(2,128)}, u32[]{:S(2)}) copy-start(s32[2,128]{1,0:T(2,128)} %unique_ref.1) | copy-start | bytes 3076
  24.4 33.7 %copy-start = (f32[2,1024,256]{2,1,0:T(8,128)S(1)}, f32[2,1024,256]{2,1,0:T(8,128)}, u32[]{:S(2)}) copy-start(f32[2,1024,256]{2,1,0:T(8,128)} %refs_4_.1) | copy-start | bytes 6291460
  24.4 33.6 %copy-start.1 = (f32[2,1024]{1,0:T(2,128)S(1)}, f32[2,1024]{1,0:T(2,128)}, u32[]{:S(2)}) copy-start(f32[2,1024]{1,0:T(2,128)} %refs_5_.1) | copy-start | bytes 24580
  24.4 9.8 %collective-permute-start.1 = (f32[512,256]{1,0:T(8,128)S(1)}, f32[512,256]{1,0:T(8,128)S(1)}, u32[]{:S(2)}, u32[]{:S(2)}) collective-permute-start(f32[512,256]{1,0:T(8,128)S(1)} %add.18), channel_id=1, source_target_pairs={{0,1},{1,2},{2,3},{3,0},{4,5},{5,6},{6,7},{7,4},{8,9},{9,10},{10,1... | collective-permute-start | bytes 1572872 | tf_op jit(solution)/shard_map/ppermute | solution.py:275
  34.2 2.5 %collective-permute-start.6 = (f32[8,128]{1,0:T(8,128)S(1)}, f32[8,128]{1,0:T(8,128)S(1)}, u32[]{:S(2)}, u32[]{:S(2)}) collective-permute-start(f32[8,128]{1,0:T(8,128)S(1)} %fusion), channel_id=1, source_target_pairs={{0,16},{16,0},{32,48},{48,32},{64,80},{80,64},{96,112},{112,96},{1... | collective-permute-start | bytes 12296 | tf_op jit(solution)/shard_map/ppermute | solution.py:293
  36.9 7.1 %collective-permute-start.7 = (f32[256,256]{1,0:T(8,128)S(1)}, f32[256,256]{1,0:T(8,128)S(1)}, u32[]{:S(2)}, u32[]{:S(2)}) collective-permute-start(f32[256,256]{1,0:T(8,128)S(1)} %get-tuple-element.29), channel_id=1, source_target_pairs={{0,8},{1,9},{2,10},{3,11},{4,12},{5,13},{6,14},{7,15},{8,0},{9,1},... | collective-permute-start | bytes 786440 | tf_op jit(solution)/shard_map/ppermute | solution.py:275
  38.1 8.7 %collective-permute-start.8 = (f32[256,256]{1,0:T(8,128)S(1)}, f32[256,256]{1,0:T(8,128)S(1)}, u32[]{:S(2)}, u32[]{:S(2)}) collective-permute-start(f32[256,256]{1,0:T(8,128)S(1)} %get-tuple-element.30), channel_id=1, source_target_pairs={{0,4},{1,5},{2,6},{3,7},{4,8},{5,9},{6,10},{7,11},{8,12},{9,13},{1... | collective-permute-start | bytes 786440 | tf_op jit(solution)/shard_map/ppermute | solution.py:275
  38.4 8.4 %collective-permute-start.9 = (f32[256,256]{1,0:T(8,128)S(1)}, f32[256,256]{1,0:T(8,128)S(1)}, u32[]{:S(2)}, u32[]{:S(2)}) collective-permute-start(f32[256,256]{1,0:T(8,128)S(1)} %get-tuple-element.31), channel_id=1, source_target_pairs={{0,12},{1,13},{2,14},{3,15},{4,0},{5,1},{6,2},{7,3},{8,4},{9,5},{1... | collective-permute-start | bytes 786440 | tf_op jit(solution)/shard_map/ppermute | solution.py:275
  46.9 3.7 %collective-permute-start.10 = (f32[4,40,256]{2,1,0:T(8,128)S(1)}, f32[4,40,256]{2,1,0:T(8,128)S(1)}, u32[]{:S(2)}, u32[]{:S(2)}) collective-permute-start(f32[4,40,256]{2,1,0:T(8,128)S(1)} %get-tuple-element.33), channel_id=1, source_target_pairs={{0,16},{16,0},{32,48},{48,32},{64,80},{80,64},{96,112},{112,96},{1... | collective-permute-start | bytes 491528 | tf_op jit(solution)/shard_map/ppermute | solution.py:303
  50.6 5.7 %collective-permute-start.11 = (f32[80,256]{1,0:T(8,128)S(1)}, f32[80,256]{1,0:T(8,128)S(1)}, u32[]{:S(2)}, u32[]{:S(2)}) collective-permute-start(f32[80,256]{1,0:T(8,128)S(1)} %pad_maximum_fusion.1), channel_id=1, source_target_pairs={{0,64},{16,80},{32,96},{48,112},{64,0},{80,16},{96,32},{112,48},{1... | collective-permute-start | bytes 245768 | tf_op jit(solution)/shard_map/ppermute | solution.py:278
  53.5 4.5 %collective-permute-start.12 = (f32[80,256]{1,0:T(8,128)S(1)}, f32[80,256]{1,0:T(8,128)S(1)}, u32[]{:S(2)}, u32[]{:S(2)}) collective-permute-start(f32[80,256]{1,0:T(8,128)S(1)} %pad_maximum_fusion.2), channel_id=1, source_target_pairs={{0,32},{16,48},{32,64},{48,80},{64,96},{80,112},{96,0},{112,16},{1... | collective-permute-start | bytes 245768 | tf_op jit(solution)/shard_map/ppermute | solution.py:278
  53.9 4.1 %collective-permute-start.13 = (f32[80,256]{1,0:T(8,128)S(1)}, f32[80,256]{1,0:T(8,128)S(1)}, u32[]{:S(2)}, u32[]{:S(2)}) collective-permute-start(f32[80,256]{1,0:T(8,128)S(1)} %pad_maximum_fusion.3), channel_id=1, source_target_pairs={{0,96},{16,112},{32,0},{48,16},{64,32},{80,48},{96,64},{112,80},{1... | collective-permute-start | bytes 245768 | tf_op jit(solution)/shard_map/ppermute | solution.py:278
